TPU v7x, 32 devices: a whole 2x2x4 slice. The times are simulated.
32 devices in a mesh: groups: 2 (over y), blk: 4 (over x, core), narrow: 4 (over z).
Axes of the slice: x: 2, y: 2, z: 4, core: 2. Of those that a mesh axis runs over, the one named last changes fastest.
Arguments:
- tokens: bfloat16 [8192, 1024], P(('groups', 'blk', 'narrow')), parts along dimension 0, may hold values from -64 to 64
- latents: bfloat16 [2048, 1024], P('blk'), may hold values from -48 to 48
- cotangent: bfloat16 [4096, 1024], P(('groups', 'blk')), parts along dimension 0, may hold values from -6 to 6
- query_weight: bfloat16 [1024, 1024], replicated, may hold values from -0.1875 to 0.1875
- keyvalue_weight: bfloat16 [1024, 2048], replicated, may hold values from -0.1875 to 0.1875
- counts: int32 [8, 4], P(('groups', 'blk')), parts along dimension 0, may hold values from 1 to 256, 614 in all within a row
Outputs:
- latent_out: bfloat16 [4096, 1024], P(('groups', 'blk')), parts along dimension 0
- grad_latents: bfloat16 [4096, 1024], P(('groups', 'blk')), parts along dimension 0
- grad_query_weight: bfloat16 [2048, 1024], P('groups', 'narrow'), parts along dimension 0
- grad_tokens: bfloat16 [8192, 1024], P(('groups', 'blk', 'narrow')), parts along dimension 0
There are 2 independent parts, one for each index of `groups`. A program takes and returns all parts, laid end to end along the dimension named above; an argument that names none is the same for every part. Nothing has to cross between parts.
Inputs may be any that keep to these rules, and one draw needn't show every extreme that they name: Each row of counts sums to 614 and has an entry equal to 256.
All inputs are finite; a program needn't handle non-finite values.
Results may differ from a plain program's by a relative error of at most 0.0102.
The roundings to bfloat16 on the way count: a program that leaves them out, or rounds other values in their place, can miss the bound.
Values may be sent and summed in bfloat16 or wider, within the bound.
No kernel may reach another device: no remote copies, remote signals or barrier semaphores. Data moves between devices by JAX's collectives and lax.ppermute only.
A program may use at most 128 MiB of HBM per device.

v0:
```python
import jax
import jax.numpy as jnp
from jax import lax
from jax.sharding import PartitionSpec as P

HEADS = 16
HEAD = 64


NEG = -1e30


def shifted(shard, axis, by):
    length = lax.axis_size(axis)
    return lax.ppermute(shard, axis, [(i, (i + by) % length) for i in range(length)])


def merged_2(shard, axis, combine):
    everything = jax.tree.map(lambda part: lax.all_gather(part, axis), shard)
    initial = jax.tree.map(lambda part: part[0], everything)

    def turn(k, so_far):
        return combine(so_far, jax.tree.map(lambda part: part[k], everything))

    return lax.fori_loop(1, lax.axis_size(axis), turn, initial)


def attend_forward(queries, row_max, row_sum, weighted, key_heads, value_heads, valid_mask):
    latent_rows, col_count = queries.shape
    heads_here = key_heads.shape[1]
    head_size = key_heads.shape[2]
    query_heads = queries.reshape(latent_rows, heads_here, head_size)
    scores = jnp.einsum(
        "qhd,khd->hqk", query_heads, key_heads, preferred_element_type=jnp.float32
    ) * head_size ** (-0.5)
    scores = jnp.where(valid_mask[None, None, :], scores, NEG)
    new_max = jnp.maximum(row_max, jnp.max(scores, axis=2))
    powers = jnp.exp(scores - new_max[:, :, None])
    rescale = jnp.exp(row_max - new_max)
    row_sum = row_sum * rescale + jnp.sum(powers, axis=2)
    update = jnp.einsum(
        "hqk,khd->qhd", powers.astype(jnp.bfloat16), value_heads, preferred_element_type=jnp.float32
    )
    weighted = weighted.reshape(latent_rows, heads_here, head_size) * rescale.T[:, :, None] + update
    return (new_max, row_sum, weighted.reshape(latent_rows, col_count))


def join_partials(earlier, latter):
    max_one, sum_one, acc_one = earlier
    max_two, sum_two, acc_two = latter
    new_max = jnp.maximum(max_one, max_two)
    scale_one = jnp.exp(max_one - new_max)
    scale_two = jnp.exp(max_two - new_max)
    latent_rows = acc_one.shape[0]
    heads_here = max_one.shape[0]
    merged = (
        acc_one.reshape(latent_rows, heads_here, -1) * scale_one.T[:, :, None]
        + acc_two.reshape(latent_rows, heads_here, -1) * scale_two.T[:, :, None]
    )
    return (new_max, sum_one * scale_one + sum_two * scale_two, merged.reshape(latent_rows, -1))


def attend_backward(queries, grads, log_total, delta, key_heads, value_heads, valid_mask):
    latent_rows, col_count = queries.shape
    heads_here = key_heads.shape[1]
    head_size = key_heads.shape[2]
    factor = head_size ** (-0.5)
    query_heads = queries.reshape(latent_rows, heads_here, head_size)
    grad_heads = grads.reshape(latent_rows, heads_here, head_size)
    scores = (
        jnp.einsum("qhd,khd->hqk", query_heads, key_heads, preferred_element_type=jnp.float32)
        * factor
    )
    scores = jnp.where(valid_mask[None, None, :], scores, NEG)
    probs = jnp.exp(scores - log_total[:, :, None])
    dprob = jnp.einsum("qhd,khd->hqk", grad_heads, value_heads, preferred_element_type=jnp.float32)
    dscore = (probs * (dprob - delta[:, :, None]) * factor).astype(jnp.bfloat16)
    query_term = jnp.einsum("hqk,khd->qhd", dscore, key_heads, preferred_element_type=jnp.float32)
    key_term = jnp.einsum("hqk,qhd->khd", dscore, query_heads, preferred_element_type=jnp.float32)
    value_term = jnp.einsum(
        "hqk,qhd->khd", probs.astype(jnp.bfloat16), grad_heads, preferred_element_type=jnp.float32
    )
    return (
        query_term.reshape(latent_rows, col_count),
        key_term.reshape(-1, col_count),
        value_term.reshape(-1, col_count),
    )


def forward_cycle(queries, key_heads, value_heads, valid_mask):
    latent_rows, col_count = queries.shape
    heads_here = key_heads.shape[1]
    initial = (
        queries,
        jnp.full((heads_here, latent_rows), NEG, jnp.float32),
        jnp.zeros((heads_here, latent_rows), jnp.float32),
        jnp.zeros((latent_rows, col_count), jnp.float32),
    )

    def forward_cycle_step(carried, unused):
        current, row_max, row_sum, weighted = carried
        row_max, row_sum, weighted = attend_forward(
            current, row_max, row_sum, weighted, key_heads, value_heads, valid_mask
        )
        moved = shifted(current, "blk", 1)
        row_max, row_sum, weighted = shifted((row_max, row_sum, weighted), "blk", 1)
        return ((moved, row_max, row_sum, weighted), current)

    final, visited = lax.scan(forward_cycle_step, initial, None, length=lax.axis_size("blk"))
    return (final[1], final[2], final[3], visited)


def backward_cycle(visited, grad_share, log_total, delta, key_heads, value_heads, valid_mask):
    latent_rows, col_count = grad_share.shape
    token_count = key_heads.shape[0]
    initial = (
        grad_share,
        log_total,
        delta,
        jnp.zeros((latent_rows, col_count), jnp.float32),
        jnp.zeros((token_count, col_count), jnp.float32),
        jnp.zeros((token_count, col_count), jnp.float32),
    )

    def backward_cycle_step(carried, queries):
        grads, log_here, delta_here, query_grad, key_grad, value_grad = carried
        query_term, key_term, value_term = attend_backward(
            queries, grads, log_here, delta_here, key_heads, value_heads, valid_mask
        )
        moved = shifted(grads, "blk", 1)
        log_here, delta_here, query_grad = shifted(
            (log_here, delta_here, query_grad + query_term), "blk", 1
        )
        return (
            (moved, log_here, delta_here, query_grad, key_grad + key_term, value_grad + value_term),
            None,
        )

    final, unused = lax.scan(backward_cycle_step, initial, visited)
    return (final[3], final[4], final[5])


def on_device(tokens, latents, cotangent, query_weight, keyvalue_weight, counts):
    narrow_size = lax.axis_size("narrow")
    narrow_index = lax.axis_index("narrow")
    tok_rows = tokens.shape[0]
    model_width = tokens.shape[1]
    share = model_width // narrow_size
    queries = jnp.dot(latents, query_weight, preferred_element_type=jnp.float32).astype(
        jnp.bfloat16
    )
    pairs = jnp.dot(tokens, keyvalue_weight, preferred_element_type=jnp.float32).astype(
        jnp.bfloat16
    )
    key_heads = pairs[:, :model_width].reshape(tok_rows, HEADS, HEAD)
    value_heads = pairs[:, model_width:].reshape(tok_rows, HEADS, HEAD)
    valid_mask = jnp.arange(tok_rows) < counts[0, narrow_index]
    row_max, row_sum, weighted, visited = forward_cycle(queries, key_heads, value_heads, valid_mask)
    row_max, row_sum, weighted = merged_2((row_max, row_sum, weighted), "narrow", join_partials)
    heads_here = row_max.shape[0]
    latent_rows = weighted.shape[0]
    attended = weighted.reshape(latent_rows, heads_here, HEAD) / row_sum.T[:, :, None]
    attended_low = attended.reshape(latent_rows, -1).astype(jnp.bfloat16)
    delta = jnp.sum(
        cotangent.astype(jnp.float32).reshape(latent_rows, heads_here, HEAD) * attended, axis=2
    ).T
    log_total = row_max + jnp.log(row_sum)
    query_grad, key_grad, value_grad = backward_cycle(
        visited, cotangent, log_total, delta, key_heads, value_heads, valid_mask
    )
    pair_grad = jnp.concatenate([key_grad, value_grad], axis=1).astype(jnp.bfloat16)
    query_part = lax.psum_scatter(query_grad, "narrow", scatter_dimension=1, tiled=True)
    query_low = query_part.astype(jnp.bfloat16)
    weight_cols = lax.dynamic_slice_in_dim(query_weight, narrow_index * share, share, 1)
    weight_term = lax.dot_general(
        latents, query_low, (((0,), (0,)), ((), ())), preferred_element_type=jnp.float32
    )
    grad_query_weight = lax.psum(weight_term, "blk").astype(jnp.bfloat16)
    latent_term = lax.dot_general(
        query_low, weight_cols, (((1,), (1,)), ((), ())), preferred_element_type=jnp.float32
    )
    grad_latents = lax.psum(latent_term, "narrow").astype(jnp.bfloat16)
    grad_tokens = lax.dot_general(
        pair_grad, keyvalue_weight, (((1,), (1,)), ((), ())), preferred_element_type=jnp.float32
    ).astype(jnp.bfloat16)
    return (attended_low, grad_latents, grad_query_weight, grad_tokens)


def solution(mesh):
    placed = (
        P(("groups", "blk", "narrow"), None),
        P("blk", None),
        P(("groups", "blk"), None),
        P(),
        P(),
        P(("groups", "blk"), None),
    )
    return jax.shard_map(
        on_device,
        mesh=mesh,
        in_specs=placed,
        out_specs=(
            P(("groups", "blk"), None),
            P(("groups", "blk"), None),
            P("groups", "narrow"),
            P(("groups", "blk", "narrow"), None),
        ),
        check_vma=False,
    )
```

profile of v0, /device:TPU:0, one launch (start us, length us, event | category | flops | bytes accessed | tf_op | source)
XLA Modules:
  0.0 774.0 jit_solution(7601242237769275390)
XLA Ops:
  19.1 190.9 %while.60 = (s32[]{:T(128)}, bf16[512,1024]{0,1:T(8,128)(2,1)}, f32[16,512]{1,0:T(8,128)S(1)}, f32[16,512]{1,0:T(8,128)S(1)}, f32[512,1024]{0,1:T(8,128)}, /*ind...) while((s32[]{:T(128)}, bf16[512,1024]{0,1:T(8,128)(2,1)}, ...), condition=%wide.region_3.4_spmd.clone, body=%wide.region_0.3_spmd.clone.sunk | while | flops 561012992 | bytes 51119908 | solution.py:109
  35.3 20.5 %collective-permute-done.1 = f32[16,512]{1,0:T(8,128)S(1)} collective-permute-done((f32[16,512]{1,0:T(8,128)S(1)}, f32[16,512]{1,0:T(8,128)S(1)}, u32[]{:S(2)}, u32[]{:S(2)}) %collective-permute-start.1) | collective-permute-done | bytes 32800 | tf_op jit(solution)/shard_map/while/body/eval_jaxpr/ppermute | solution.py:15
  55.8 11.6 %collective-permute-done.2 = f32[16,512]{1,0:T(8,128)S(1)} collective-permute-done((f32[16,512]{1,0:T(8,128)S(1)}, f32[16,512]{1,0:T(8,128)S(1)}, u32[]{:S(2)}, u32[]{:S(2)}) %collective-permute-start.2) | collective-permute-done | bytes 32800 | tf_op jit(solution)/shard_map/while/body/eval_jaxpr/ppermute | solution.py:15
  72.3 5.0 bitcast_add_fusion.7
  82.8 20.5 %collective-permute-done.1 = f32[16,512]{1,0:T(8,128)S(1)} collective-permute-done((f32[16,512]{1,0:T(8,128)S(1)}, f32[16,512]{1,0:T(8,128)S(1)}, u32[]{:S(2)}, u32[]{:S(2)}) %collective-permute-start.1) | collective-permute-done | bytes 32800 | tf_op jit(solution)/shard_map/while/body/eval_jaxpr/ppermute | solution.py:15
  103.3 11.6 %collective-permute-done.2 = f32[16,512]{1,0:T(8,128)S(1)} collective-permute-done((f32[16,512]{1,0:T(8,128)S(1)}, f32[16,512]{1,0:T(8,128)S(1)}, u32[]{:S(2)}, u32[]{:S(2)}) %collective-permute-start.2) | collective-permute-done | bytes 32800 | tf_op jit(solution)/shard_map/while/body/eval_jaxpr/ppermute | solution.py:15
  130.4 20.5 %collective-permute-done.1 = f32[16,512]{1,0:T(8,128)S(1)} collective-permute-done((f32[16,512]{1,0:T(8,128)S(1)}, f32[16,512]{1,0:T(8,128)S(1)}, u32[]{:S(2)}, u32[]{:S(2)}) %collective-permute-start.1) | collective-permute-done | bytes 32800 | tf_op jit(solution)/shard_map/while/body/eval_jaxpr/ppermute | solution.py:15
  150.9 11.6 %collective-permute-done.2 = f32[16,512]{1,0:T(8,128)S(1)} collective-permute-done((f32[16,512]{1,0:T(8,128)S(1)}, f32[16,512]{1,0:T(8,128)S(1)}, u32[]{:S(2)}, u32[]{:S(2)}) %collective-permute-start.2) | collective-permute-done | bytes 32800 | tf_op jit(solution)/shard_map/while/body/eval_jaxpr/ppermute | solution.py:15
  167.5 5.0 bitcast_add_fusion.7
  177.9 20.5 %collective-permute-done.1 = f32[16,512]{1,0:T(8,128)S(1)} collective-permute-done((f32[16,512]{1,0:T(8,128)S(1)}, f32[16,512]{1,0:T(8,128)S(1)}, u32[]{:S(2)}, u32[]{:S(2)}) %collective-permute-start.1) | collective-permute-done | bytes 32800 | tf_op jit(solution)/shard_map/while/body/eval_jaxpr/ppermute | solution.py:15
  198.5 11.6 %collective-permute-done.2 = f32[16,512]{1,0:T(8,128)S(1)} collective-permute-done((f32[16,512]{1,0:T(8,128)S(1)}, f32[16,512]{1,0:T(8,128)S(1)}, u32[]{:S(2)}, u32[]{:S(2)}) %collective-permute-start.2) | collective-permute-done | bytes 32800 | tf_op jit(solution)/shard_map/while/body/eval_jaxpr/ppermute | solution.py:15
  210.1 14.4 %all-gather = f32[64,512]{1,0:T(8,128)S(1)} all-gather(f32[16,512]{1,0:T(8,128)S(1)} %get-tuple-element.291), channel_id=2, replica_groups=mesh['groups'=2,'blk'=4,'narrow'=4] {'narrow'}, dimensions={0}, use_global_device_ids=true | all-gather | bytes 163840 | tf_op jit(solution)/shard_map/all_gather | solution.py:19
  224.6 17.4 %all-gather.1 = f32[64,512]{1,0:T(8,128)S(1)} all-gather(f32[16,512]{1,0:T(8,128)S(1)} %get-tuple-element.292), channel_id=3, replica_groups=mesh['groups'=2,'blk'=4,'narrow'=4] {'narrow'}, dimensions={0}, use_global_device_ids=true | all-gather | bytes 163840 | tf_op jit(solution)/shard_map/all_gather | solution.py:19
  244.3 119.5 %all-gather.5.cloned.1.call-done = f32[2048,1024]{0,1:T(8,128)} async-done(((f32[512,1024]{0,1:T(8,128)}), f32[2048,1024]{0,1:T(8,128)}) %all-gather.5.cloned.1.call-update) | async-done | bytes 8388624 | tf_op jit(solution)/shard_map/all_gather | solution.py:19
  363.8 10.8 %reshape.92 = f32[4,512,1024]{1,0,2:T(4,128)} reshape(f32[2048,1024]{0,1:T(8,128)} %all-gather.5.cloned.1.call-done) | data formatting | bytes 16777216 | tf_op jit(solution)/shard_map/all_gather | solution.py:19
  377.7 23.0 %while.59 = (s32[]{:T(128)}, f32[16,512]{1,0:T(8,128)S(1)}, f32[16,512]{1,0:T(8,128)S(1)}, f32[512,1024]{0,1:T(8,128)}, f32[4,16,512]{2,1,0:T(8,128)S(1)}, /*ind...) while((s32[]{:T(128)}, f32[16,512]{1,0:T(8,128)S(1)}, ...), condition=%wide.region_5.6_spmd, body=%wide.region_4.5_spmd.sunk | while | flops 1630213 | bytes 27754708 | solution.py:25
  377.8 5.3 constant_dynamic-slice_fusion.5
  385.5 5.3 constant_dynamic-slice_fusion.5
  393.2 5.3 constant_dynamic-slice_fusion.5
  404.8 211.6 %while.61 = (s32[]{:T(128)}, bf16[512,1024]{0,1:T(8,128)(2,1)}, f32[16,512]{1,0:T(8,128)S(1)}, f32[16,512]{1,0:T(8,128)S(1)}, f32[512,1024]{0,1:T(8,128)}, /*ind...) while((s32[]{:T(128)}, bf16[512,1024]{0,1:T(8,128)(2,1)}, ...), condition=%wide.region_8.9_spmd.clone, body=%wide.region_7.8_spmd.clone.sunk | while | flops 1366819072 | bytes 115311720 | solution.py:139
  410.5 5.0 multiply_convert_fusion.2
  430.8 15.4 %collective-permute-done.5 = f32[16,512]{1,0:T(8,128)S(1)} collective-permute-done((f32[16,512]{1,0:T(8,128)S(1)}, f32[16,512]{1,0:T(8,128)S(1)}, u32[]{:S(2)}, u32[]{:S(2)}) %collective-permute-start.5) | collective-permute-done | bytes 32800 | tf_op jit(solution)/shard_map/while/body/eval_jaxpr/ppermute | solution.py:15
  446.1 11.6 %collective-permute-done.6 = f32[16,512]{1,0:T(8,128)S(1)} collective-permute-done((f32[16,512]{1,0:T(8,128)S(1)}, f32[16,512]{1,0:T(8,128)S(1)}, u32[]{:S(2)}, u32[]{:S(2)}) %collective-permute-start.6) | collective-permute-done | bytes 32800 | tf_op jit(solution)/shard_map/while/body/eval_jaxpr/ppermute | solution.py:15
  485.1 13.9 %collective-permute-done.5 = f32[16,512]{1,0:T(8,128)S(1)} collective-permute-done((f32[16,512]{1,0:T(8,128)S(1)}, f32[16,512]{1,0:T(8,128)S(1)}, u32[]{:S(2)}, u32[]{:S(2)}) %collective-permute-start.5) | collective-permute-done | bytes 32800 | tf_op jit(solution)/shard_map/while/body/eval_jaxpr/ppermute | solution.py:15
  499.0 11.6 %collective-permute-done.6 = f32[16,512]{1,0:T(8,128)S(1)} collective-permute-done((f32[16,512]{1,0:T(8,128)S(1)}, f32[16,512]{1,0:T(8,128)S(1)}, u32[]{:S(2)}, u32[]{:S(2)}) %collective-permute-start.6) | collective-permute-done | bytes 32800 | tf_op jit(solution)/shard_map/while/body/eval_jaxpr/ppermute | solution.py:15
  538.0 13.9 %collective-permute-done.5 = f32[16,512]{1,0:T(8,128)S(1)} collective-permute-done((f32[16,512]{1,0:T(8,128)S(1)}, f32[16,512]{1,0:T(8,128)S(1)}, u32[]{:S(2)}, u32[]{:S(2)}) %collective-permute-start.5) | collective-permute-done | bytes 32800 | tf_op jit(solution)/shard_map/while/body/eval_jaxpr/ppermute | solution.py:15
  551.9 11.6 %collective-permute-done.6 = f32[16,512]{1,0:T(8,128)S(1)} collective-permute-done((f32[16,512]{1,0:T(8,128)S(1)}, f32[16,512]{1,0:T(8,128)S(1)}, u32[]{:S(2)}, u32[]{:S(2)}) %collective-permute-start.6) | collective-permute-done | bytes 32800 | tf_op jit(solution)/shard_map/while/body/eval_jaxpr/ppermute | solution.py:15
  590.9 13.9 %collective-permute-done.5 = f32[16,512]{1,0:T(8,128)S(1)} collective-permute-done((f32[16,512]{1,0:T(8,128)S(1)}, f32[16,512]{1,0:T(8,128)S(1)}, u32[]{:S(2)}, u32[]{:S(2)}) %collective-permute-start.5) | collective-permute-done | bytes 32800 | tf_op jit(solution)/shard_map/while/body/eval_jaxpr/ppermute | solution.py:15
  604.8 11.6 %collective-permute-done.6 = f32[16,512]{1,0:T(8,128)S(1)} collective-permute-done((f32[16,512]{1,0:T(8,128)S(1)}, f32[16,512]{1,0:T(8,128)S(1)}, u32[]{:S(2)}, u32[]{:S(2)}) %collective-permute-start.6) | collective-permute-done | bytes 32800 | tf_op jit(solution)/shard_map/while/body/eval_jaxpr/ppermute | solution.py:15
  628.5 30.0 %reduce-scatter.2.cloned.1.call-done = f32[512,256]{0,1:T(8,128)} async-done(((f32[512,1024]{0,1:T(8,128)}), f32[512,256]{0,1:T(8,128)}) %reduce-scatter.2.cloned.1.call-update) | async-done | bytes 524304 | tf_op jit(solution)/shard_map/reduce_scatter | solution.py:172
  661.4 76.5 %all-reduce.2 = bf16[512,1024]{1,0:T(8,128)(2,1)} all-reduce(f32[512,1024]{1,0:T(8,128)} %fusion.35), channel_id=1, replica_groups=mesh['groups'=2,'blk'=4,'narrow'=4] {'narrow'}, use_global_device_ids=true, to_apply=%region_10.11 | all-reduce | flops 524288 | bytes 3145728 | tf_op jit(solution)/shard_map/psum | solution.py:182
  739.8 25.4 %all-reduce.3 = bf16[1024,256]{0,1:T(8,128)(2,1)} all-reduce(f32[1024,256]{0,1:T(8,128)S(1)} %convolution_bitcast_fusion), channel_id=1, replica_groups=mesh['groups'=2,'blk'=4,'narrow'=4] {'blk'}, use_global_device_ids=true, to_apply=%region_11.12 | all-reduce | flops 262144 | bytes 1572864 | tf_op jit(solution)/shard_map/psum | solution.py:178
  (217 shorter events, 202.5 us)
Async XLA Ops:
  7.2 356.6 %all-gather.5.cloned.1.call-start = ((), (), s32[]{:S(2)}) async-start(), calls=%async_computation.2 | async-start | bytes 10485760 | tf_op jit(solution)/shard_map/all_gather | solution.py:19
  29.1 38.3 %collective-permute-start.3 = (f32[512,1024]{0,1:T(8,128)}, f32[512,1024]{0,1:T(8,128)}, u32[]{:S(2)}, u32[]{:S(2)}) collective-permute-start(f32[512,1024]{0,1:T(8,128)} %bitcast.133), channel_id=1, source_target_pairs={{0,4},{4,8},{8,12},{12,0},{1,5},{5,9},{9,13},{13,1},{2,6},{6,10},{... | collective-permute-start | bytes 6291464 | tf_op jit(solution)/shard_map/while/body/eval_jaxpr/ppermute | solution.py:15
  29.6 26.2 %collective-permute-start.1 = (f32[16,512]{1,0:T(8,128)S(1)}, f32[16,512]{1,0:T(8,128)S(1)}, u32[]{:S(2)}, u32[]{:S(2)}) collective-permute-start(f32[16,512]{1,0:T(8,128)S(1)} %get-tuple-element.658), channel_id=1, source_target_pairs={{0,4},{4,8},{8,12},{12,0},{1,5},{5,9},{9,13},{13,1},{2,6},{6,10},{... | collective-permute-start | bytes 98312 | tf_op jit(solution)/shard_map/while/body/eval_jaxpr/ppermute | solution.py:15
  32.2 35.2 %collective-permute-start = (bf16[512,1024]{0,1:T(8,128)(2,1)S(1)}, bf16[512,1024]{0,1:T(8,128)(2,1)}, u32[]{:S(2)}, u32[]{:S(2)}) collective-permute-start(bf16[512,1024]{0,1:T(8,128)(2,1)S(1)} %copy.49), channel_id=1, source_target_pairs={{0,4},{4,8},{8,12},{12,0},{1,5},{5,9},{9,13},{13,1},{2,6},{6,10},{... | collective-permute-start | bytes 3145736 | tf_op jit(solution)/shard_map/while/body/eval_jaxpr/ppermute | solution.py:15
  34.1 33.2 %collective-permute-start.2 = (f32[16,512]{1,0:T(8,128)S(1)}, f32[16,512]{1,0:T(8,128)S(1)}, u32[]{:S(2)}, u32[]{:S(2)}) collective-permute-start(f32[16,512]{1,0:T(8,128)S(1)} %multiply_add_fusion.2), channel_id=1, source_target_pairs={{0,4},{4,8},{8,12},{12,0},{1,5},{5,9},{9,13},{13,1},{2,6},{6,10},{... | collective-permute-start | bytes 98312 | tf_op jit(solution)/shard_map/while/body/eval_jaxpr/ppermute | solution.py:15
  77.3 37.6 %collective-permute-start.3 = (f32[512,1024]{0,1:T(8,128)}, f32[512,1024]{0,1:T(8,128)}, u32[]{:S(2)}, u32[]{:S(2)}) collective-permute-start(f32[512,1024]{0,1:T(8,128)} %bitcast.133), channel_id=1, source_target_pairs={{0,4},{4,8},{8,12},{12,0},{1,5},{5,9},{9,13},{13,1},{2,6},{6,10},{... | collective-permute-start | bytes 6291464 | tf_op jit(solution)/shard_map/while/body/eval_jaxpr/ppermute | solution.py:15
  77.3 26.0 %collective-permute-start.1 = (f32[16,512]{1,0:T(8,128)S(1)}, f32[16,512]{1,0:T(8,128)S(1)}, u32[]{:S(2)}, u32[]{:S(2)}) collective-permute-start(f32[16,512]{1,0:T(8,128)S(1)} %get-tuple-element.658), channel_id=1, source_target_pairs={{0,4},{4,8},{8,12},{12,0},{1,5},{5,9},{9,13},{13,1},{2,6},{6,10},{... | collective-permute-start | bytes 98312 | tf_op jit(solution)/shard_map/while/body/eval_jaxpr/ppermute | solution.py:15
  79.7 35.2 %collective-permute-start = (bf16[512,1024]{0,1:T(8,128)(2,1)S(1)}, bf16[512,1024]{0,1:T(8,128)(2,1)}, u32[]{:S(2)}, u32[]{:S(2)}) collective-permute-start(bf16[512,1024]{0,1:T(8,128)(2,1)S(1)} %copy.49), channel_id=1, source_target_pairs={{0,4},{4,8},{8,12},{12,0},{1,5},{5,9},{9,13},{13,1},{2,6},{6,10},{... | collective-permute-start | bytes 3145736 | tf_op jit(solution)/shard_map/while/body/eval_jaxpr/ppermute | solution.py:15
  81.7 33.2 %collective-permute-start.2 = (f32[16,512]{1,0:T(8,128)S(1)}, f32[16,512]{1,0:T(8,128)S(1)}, u32[]{:S(2)}, u32[]{:S(2)}) collective-permute-start(f32[16,512]{1,0:T(8,128)S(1)} %multiply_add_fusion.2), channel_id=1, source_target_pairs={{0,4},{4,8},{8,12},{12,0},{1,5},{5,9},{9,13},{13,1},{2,6},{6,10},{... | collective-permute-start | bytes 98312 | tf_op jit(solution)/shard_map/while/body/eval_jaxpr/ppermute | solution.py:15
  124.9 37.6 %collective-permute-start.3 = (f32[512,1024]{0,1:T(8,128)}, f32[512,1024]{0,1:T(8,128)}, u32[]{:S(2)}, u32[]{:S(2)}) collective-permute-start(f32[512,1024]{0,1:T(8,128)} %bitcast.133), channel_id=1, source_target_pairs={{0,4},{4,8},{8,12},{12,0},{1,5},{5,9},{9,13},{13,1},{2,6},{6,10},{... | collective-permute-start | bytes 6291464 | tf_op jit(solution)/shard_map/while/body/eval_jaxpr/ppermute | solution.py:15
  124.9 26.0 %collective-permute-start.1 = (f32[16,512]{1,0:T(8,128)S(1)}, f32[16,512]{1,0:T(8,128)S(1)}, u32[]{:S(2)}, u32[]{:S(2)}) collective-permute-start(f32[16,512]{1,0:T(8,128)S(1)} %get-tuple-element.658), channel_id=1, source_target_pairs={{0,4},{4,8},{8,12},{12,0},{1,5},{5,9},{9,13},{13,1},{2,6},{6,10},{... | collective-permute-start | bytes 98312 | tf_op jit(solution)/shard_map/while/body/eval_jaxpr/ppermute | solution.py:15
  127.3 35.2 %collective-permute-start = (bf16[512,1024]{0,1:T(8,128)(2,1)S(1)}, bf16[512,1024]{0,1:T(8,128)(2,1)}, u32[]{:S(2)}, u32[]{:S(2)}) collective-permute-start(bf16[512,1024]{0,1:T(8,128)(2,1)S(1)} %copy.49), channel_id=1, source_target_pairs={{0,4},{4,8},{8,12},{12,0},{1,5},{5,9},{9,13},{13,1},{2,6},{6,10},{... | collective-permute-start | bytes 3145736 | tf_op jit(solution)/shard_map/while/body/eval_jaxpr/ppermute | solution.py:15
  129.3 33.2 %collective-permute-start.2 = (f32[16,512]{1,0:T(8,128)S(1)}, f32[16,512]{1,0:T(8,128)S(1)}, u32[]{:S(2)}, u32[]{:S(2)}) collective-permute-start(f32[16,512]{1,0:T(8,128)S(1)} %multiply_add_fusion.2), channel_id=1, source_target_pairs={{0,4},{4,8},{8,12},{12,0},{1,5},{5,9},{9,13},{13,1},{2,6},{6,10},{... | collective-permute-start | bytes 98312 | tf_op jit(solution)/shard_map/while/body/eval_jaxpr/ppermute | solution.py:15
  172.4 37.6 %collective-permute-start.3 = (f32[512,1024]{0,1:T(8,128)}, f32[512,1024]{0,1:T(8,128)}, u32[]{:S(2)}, u32[]{:S(2)}) collective-permute-start(f32[512,1024]{0,1:T(8,128)} %bitcast.133), channel_id=1, source_target_pairs={{0,4},{4,8},{8,12},{12,0},{1,5},{5,9},{9,13},{13,1},{2,6},{6,10},{... | collective-permute-start | bytes 6291464 | tf_op jit(solution)/shard_map/while/body/eval_jaxpr/ppermute | solution.py:15
  172.4 26.0 %collective-permute-start.1 = (f32[16,512]{1,0:T(8,128)S(1)}, f32[16,512]{1,0:T(8,128)S(1)}, u32[]{:S(2)}, u32[]{:S(2)}) collective-permute-start(f32[16,512]{1,0:T(8,128)S(1)} %get-tuple-element.658), channel_id=1, source_target_pairs={{0,4},{4,8},{8,12},{12,0},{1,5},{5,9},{9,13},{13,1},{2,6},{6,10},{... | collective-permute-start | bytes 98312 | tf_op jit(solution)/shard_map/while/body/eval_jaxpr/ppermute | solution.py:15
  174.8 35.2 %collective-permute-start = (bf16[512,1024]{0,1:T(8,128)(2,1)S(1)}, bf16[512,1024]{0,1:T(8,128)(2,1)}, u32[]{:S(2)}, u32[]{:S(2)}) collective-permute-start(bf16[512,1024]{0,1:T(8,128)(2,1)S(1)} %copy.49), channel_id=1, source_target_pairs={{0,4},{4,8},{8,12},{12,0},{1,5},{5,9},{9,13},{13,1},{2,6},{6,10},{... | collective-permute-start | bytes 3145736 | tf_op jit(solution)/shard_map/while/body/eval_jaxpr/ppermute | solution.py:15
  176.8 33.2 %collective-permute-start.2 = (f32[16,512]{1,0:T(8,128)S(1)}, f32[16,512]{1,0:T(8,128)S(1)}, u32[]{:S(2)}, u32[]{:S(2)}) collective-permute-start(f32[16,512]{1,0:T(8,128)S(1)} %multiply_add_fusion.2), channel_id=1, source_target_pairs={{0,4},{4,8},{8,12},{12,0},{1,5},{5,9},{9,13},{13,1},{2,6},{6,10},{... | collective-permute-start | bytes 98312 | tf_op jit(solution)/shard_map/while/body/eval_jaxpr/ppermute | solution.py:15
  210.1 448.5 %reduce-scatter.2.cloned.1.call-start = ((), (), s32[]{:S(2)}) async-start(), calls=%async_computation.1 | async-start | bytes 2621440 | tf_op jit(solution)/shard_map/reduce_scatter | solution.py:172
  420.1 37.6 %collective-permute-start.7 = (f32[512,1024]{0,1:T(8,128)}, f32[512,1024]{0,1:T(8,128)}, u32[]{:S(2)}, u32[]{:S(2)}) collective-permute-start(f32[512,1024]{0,1:T(8,128)} %bitcast_add_fusion.8), channel_id=1, source_target_pairs={{0,4},{4,8},{8,12},{12,0},{1,5},{5,9},{9,13},{13,1},{2,6},{6,10},{... | collective-permute-start | bytes 6291464 | tf_op jit(solution)/shard_map/while/body/eval_jaxpr/ppermute | solution.py:15
  421.5 36.2 %collective-permute-start.4 = (bf16[512,1024]{0,1:T(8,128)(2,1)}, bf16[512,1024]{0,1:T(8,128)(2,1)}, u32[]{:S(2)}, u32[]{:S(2)}) collective-permute-start(bf16[512,1024]{0,1:T(8,128)(2,1)} %copy.80), channel_id=1, source_target_pairs={{0,4},{4,8},{8,12},{12,0},{1,5},{5,9},{9,13},{13,1},{2,6},{6,10},{... | collective-permute-start | bytes 3145736 | tf_op jit(solution)/shard_map/while/body/eval_jaxpr/ppermute | solution.py:15
  421.5 36.2 %collective-permute-start.6 = (f32[16,512]{1,0:T(8,128)S(1)}, f32[16,512]{1,0:T(8,128)S(1)}, u32[]{:S(2)}, u32[]{:S(2)}) collective-permute-start(f32[16,512]{1,0:T(8,128)S(1)} %copy.82), channel_id=1, source_target_pairs={{0,4},{4,8},{8,12},{12,0},{1,5},{5,9},{9,13},{13,1},{2,6},{6,10},{... | collective-permute-start | bytes 98312 | tf_op jit(solution)/shard_map/while/body/eval_jaxpr/ppermute | solution.py:15
  473.0 37.6 %collective-permute-start.7 = (f32[512,1024]{0,1:T(8,128)}, f32[512,1024]{0,1:T(8,128)}, u32[]{:S(2)}, u32[]{:S(2)}) collective-permute-start(f32[512,1024]{0,1:T(8,128)} %bitcast_add_fusion.8), channel_id=1, source_target_pairs={{0,4},{4,8},{8,12},{12,0},{1,5},{5,9},{9,13},{13,1},{2,6},{6,10},{... | collective-permute-start | bytes 6291464 | tf_op jit(solution)/shard_map/while/body/eval_jaxpr/ppermute | solution.py:15
  473.0 26.0 %collective-permute-start.5 = (f32[16,512]{1,0:T(8,128)S(1)}, f32[16,512]{1,0:T(8,128)S(1)}, u32[]{:S(2)}, u32[]{:S(2)}) collective-permute-start(f32[16,512]{1,0:T(8,128)S(1)} %copy.81), channel_id=1, source_target_pairs={{0,4},{4,8},{8,12},{12,0},{1,5},{5,9},{9,13},{13,1},{2,6},{6,10},{... | collective-permute-start | bytes 98312 | tf_op jit(solution)/shard_map/while/body/eval_jaxpr/ppermute | solution.py:15
  474.4 36.2 %collective-permute-start.4 = (bf16[512,1024]{0,1:T(8,128)(2,1)}, bf16[512,1024]{0,1:T(8,128)(2,1)}, u32[]{:S(2)}, u32[]{:S(2)}) collective-permute-start(bf16[512,1024]{0,1:T(8,128)(2,1)} %copy.80), channel_id=1, source_target_pairs={{0,4},{4,8},{8,12},{12,0},{1,5},{5,9},{9,13},{13,1},{2,6},{6,10},{... | collective-permute-start | bytes 3145736 | tf_op jit(solution)/shard_map/while/body/eval_jaxpr/ppermute | solution.py:15
  474.4 36.2 %collective-permute-start.6 = (f32[16,512]{1,0:T(8,128)S(1)}, f32[16,512]{1,0:T(8,128)S(1)}, u32[]{:S(2)}, u32[]{:S(2)}) collective-permute-start(f32[16,512]{1,0:T(8,128)S(1)} %copy.82), channel_id=1, source_target_pairs={{0,4},{4,8},{8,12},{12,0},{1,5},{5,9},{9,13},{13,1},{2,6},{6,10},{... | collective-permute-start | bytes 98312 | tf_op jit(solution)/shard_map/while/body/eval_jaxpr/ppermute | solution.py:15
  525.9 37.6 %collective-permute-start.7 = (f32[512,1024]{0,1:T(8,128)}, f32[512,1024]{0,1:T(8,128)}, u32[]{:S(2)}, u32[]{:S(2)}) collective-permute-start(f32[512,1024]{0,1:T(8,128)} %bitcast_add_fusion.8), channel_id=1, source_target_pairs={{0,4},{4,8},{8,12},{12,0},{1,5},{5,9},{9,13},{13,1},{2,6},{6,10},{... | collective-permute-start | bytes 6291464 | tf_op jit(solution)/shard_map/while/body/eval_jaxpr/ppermute | solution.py:15
  527.3 36.2 %collective-permute-start.4 = (bf16[512,1024]{0,1:T(8,128)(2,1)}, bf16[512,1024]{0,1:T(8,128)(2,1)}, u32[]{:S(2)}, u32[]{:S(2)}) collective-permute-start(bf16[512,1024]{0,1:T(8,128)(2,1)} %copy.80), channel_id=1, source_target_pairs={{0,4},{4,8},{8,12},{12,0},{1,5},{5,9},{9,13},{13,1},{2,6},{6,10},{... | collective-permute-start | bytes 3145736 | tf_op jit(solution)/shard_map/while/body/eval_jaxpr/ppermute | solution.py:15
  527.3 36.2 %collective-permute-start.6 = (f32[16,512]{1,0:T(8,128)S(1)}, f32[16,512]{1,0:T(8,128)S(1)}, u32[]{:S(2)}, u32[]{:S(2)}) collective-permute-start(f32[16,512]{1,0:T(8,128)S(1)} %copy.82), channel_id=1, source_target_pairs={{0,4},{4,8},{8,12},{12,0},{1,5},{5,9},{9,13},{13,1},{2,6},{6,10},{... | collective-permute-start | bytes 98312 | tf_op jit(solution)/shard_map/while/body/eval_jaxpr/ppermute | solution.py:15
  578.8 37.6 %collective-permute-start.7 = (f32[512,1024]{0,1:T(8,128)}, f32[512,1024]{0,1:T(8,128)}, u32[]{:S(2)}, u32[]{:S(2)}) collective-permute-start(f32[512,1024]{0,1:T(8,128)} %bitcast_add_fusion.8), channel_id=1, source_target_pairs={{0,4},{4,8},{8,12},{12,0},{1,5},{5,9},{9,13},{13,1},{2,6},{6,10},{... | collective-permute-start | bytes 6291464 | tf_op jit(solution)/shard_map/while/body/eval_jaxpr/ppermute | solution.py:15
  578.8 26.0 %collective-permute-start.5 = (f32[16,512]{1,0:T(8,128)S(1)}, f32[16,512]{1,0:T(8,128)S(1)}, u32[]{:S(2)}, u32[]{:S(2)}) collective-permute-start(f32[16,512]{1,0:T(8,128)S(1)} %copy.81), channel_id=1, source_target_pairs={{0,4},{4,8},{8,12},{12,0},{1,5},{5,9},{9,13},{13,1},{2,6},{6,10},{... | collective-permute-start | bytes 98312 | tf_op jit(solution)/shard_map/while/body/eval_jaxpr/ppermute | solution.py:15
  580.2 36.2 %collective-permute-start.4 = (bf16[512,1024]{0,1:T(8,128)(2,1)}, bf16[512,1024]{0,1:T(8,128)(2,1)}, u32[]{:S(2)}, u32[]{:S(2)}) collective-permute-start(bf16[512,1024]{0,1:T(8,128)(2,1)} %copy.80), channel_id=1, source_target_pairs={{0,4},{4,8},{8,12},{12,0},{1,5},{5,9},{9,13},{13,1},{2,6},{6,10},{... | collective-permute-start | bytes 3145736 | tf_op jit(solution)/shard_map/while/body/eval_jaxpr/ppermute | solution.py:15
  580.2 36.2 %collective-permute-start.6 = (f32[16,512]{1,0:T(8,128)S(1)}, f32[16,512]{1,0:T(8,128)S(1)}, u32[]{:S(2)}, u32[]{:S(2)}) collective-permute-start(f32[16,512]{1,0:T(8,128)S(1)} %copy.82), channel_id=1, source_target_pairs={{0,4},{4,8},{8,12},{12,0},{1,5},{5,9},{9,13},{13,1},{2,6},{6,10},{... | collective-permute-start | bytes 98312 | tf_op jit(solution)/shard_map/while/body/eval_jaxpr/ppermute | solution.py:15
  (24 other events, 141.4 us)
Sparse Core Ops, SparseCore 0:
  210.2 153.5 all-gather.4
  616.6 41.9 reduce-scatter.1
where the time goes:
time: 776 us; the launch traced here: 774 us
  waiting for transfers between devices  381 us (49%)
  blocking collectives  134 us (17%)
  matrix products  105 us (14%)
  local copies, waits for them, and re-layouts  70.6 us (9%)
  other arithmetic  49.2 us (6%)
  starting transfers between devices  19.8 us (3%)
  between operations  14.1 us (2%)
    ppermute x32, waiting for transfers between devices, shifted(): lax.ppermute(shard, axis, [(i, (i + by) % length) for i in range(length)])  232 us
    all_gather x1, waiting for transfers between devices, merged_2(): everything = jax.tree.map(lambda part: lax.all_gather(part, axis), shard)  120 us
    psum x1, blocking collectives, on_device(): grad_latents = lax.psum(latent_term, 'narrow').astype(jnp.bfloat16)  76.5 us
    all_gather x2, blocking collectives, merged_2(): everything = jax.tree.map(lambda part: lax.all_gather(part, axis), shard)  31.9 us
    reduce_scatter x1, waiting for transfers between devices, on_device(): lax.psum_scatter(query_grad, 'narrow', scatter_dimension=1, tiled=True)  30 us
    psum x1, blocking collectives, on_device(): grad_query_weight = lax.psum(weight_term, 'blk').astype(jnp.bfloat16)  25.4 us
    dot_general x4, matrix products, attend_forward(): jnp.einsum('hqk,khd->qhd', powers.astype(jnp.bfloat16), value_heads, pref...  19.9 us
    dot_general x4, matrix products, attend_backward(): jnp.einsum('qhd,khd->hqk', grad_heads, value_heads, preferred_element_typ...  19.9 us
  transfers between devices with their start and end apart: 34, of which 18 were waited for; matrix products, arithmetic and copies ran while one was open for 8% of the time, Pallas kernels for 0%

commit v1 on v0

--- a/solution.py
+++ b/solution.py
@@ -1,6 +1,10 @@
+import functools
+
 import jax
 import jax.numpy as jnp
 from jax import lax
+from jax.experimental import pallas as pl
+from jax.experimental.pallas import tpu as pltpu
 from jax.sharding import PartitionSpec as P
 
 HEADS = 16
@@ -140,6 +144,326 @@
     return (final[3], final[4], final[5])
 
 
+NT = (((1,), (1,)), ((), ()))
+NN = (((1,), (0,)), ((), ()))
+LOG2E = 1.4426950408889634
+
+
+def mm(one, two, dims=NN):
+    return lax.dot_general(one, two, dims, preferred_element_type=jnp.float32)
+
+
+def whole(shape):
+    return pl.BlockSpec(shape, lambda *unused: (0,) * len(shape))
+
+
+def pairs_kernel(tok_ref, key_w_ref, value_w_ref, out_ref, *, heads):
+    tok = tok_ref[...]
+    keys = mm(tok, key_w_ref[...]).astype(jnp.bfloat16)
+    values = mm(tok, value_w_ref[...]).astype(jnp.bfloat16)
+    for h in range(heads):
+        cols = slice(h * HEAD, (h + 1) * HEAD)
+        out_ref[h, 0] = jnp.concatenate([keys[:, cols], values[:, cols]], axis=1)
+
+
+def project_pairs(tokens, weight, groups):
+    rows, width = tokens.shape
+    cols = width // groups
+    heads = cols // HEAD
+    return pl.pallas_call(
+        functools.partial(pairs_kernel, heads=heads),
+        grid=(groups,),
+        in_specs=[
+            whole((rows, width)),
+            pl.BlockSpec((width, cols), lambda n: (0, n)),
+            pl.BlockSpec((width, cols), lambda n: (0, n + groups)),
+        ],
+        out_specs=pl.BlockSpec((heads, 1, rows, 2 * HEAD), lambda n: (0, n, 0, 0)),
+        out_shape=jax.ShapeDtypeStruct((heads, groups, rows, 2 * HEAD), jnp.bfloat16),
+        name="project_pairs",
+    )(tokens, weight, weight)
+
+
+def queries_kernel(index_ref, lat_ref, w_ref, grad_ref, out_ref, *, heads):
+    queries = mm(lat_ref[...], w_ref[...]).astype(jnp.bfloat16)
+    grads = grad_ref[...]
+    for h in range(heads):
+        cols = slice(h * HEAD, (h + 1) * HEAD)
+        out_ref[h] = jnp.concatenate([queries[:, cols], grads[:, cols]], axis=1)
+
+
+def project_queries(latents, weight, cotangent, index, groups):
+    rows, width = latents.shape
+    cols = width // groups
+    heads = cols // HEAD
+    return pl.pallas_call(
+        functools.partial(queries_kernel, heads=heads),
+        grid_spec=pltpu.PrefetchScalarGridSpec(
+            num_scalar_prefetch=1,
+            grid=(1,),
+            in_specs=[
+                pl.BlockSpec((rows, width), lambda i, at: (0, 0)),
+                pl.BlockSpec((width, cols), lambda i, at: (0, at[0])),
+                pl.BlockSpec((rows, cols), lambda i, at: (0, at[0])),
+            ],
+            out_specs=pl.BlockSpec((heads, rows, 2 * HEAD), lambda i, at: (0, 0, 0)),
+        ),
+        out_shape=jax.ShapeDtypeStruct((heads, rows, 2 * HEAD), jnp.bfloat16),
+        name="project_queries",
+    )(index, latents, weight, cotangent)
+
+
+def attention_kernel(
+    counts_ref, kv_ref, qg_ref, og_ref, dkv_ref, wide, kv, kvt, scores, acc, *, valid, tile
+):
+    step = pl.program_id(0)
+    sources, slot, width = kv_ref.shape
+    block = qg_ref.shape[0]
+    padded = kv.shape[0]
+    factor = HEAD ** (-0.5)
+    row8 = lax.broadcasted_iota(jnp.int32, (8, width), 0)
+
+    @pl.when(step == 0)
+    def _():
+        at = jnp.int32(0)
+        for s in range(sources):
+            offset = at % 8
+            base = pl.multiple_of(at - offset, 8)
+            rows = kv_ref[s].astype(jnp.float32)
+            rows = jnp.concatenate([rows, jnp.zeros((8, width), jnp.float32)], axis=0)
+            rows = pltpu.roll(rows, offset, 0)
+            earlier = wide[pl.ds(base, 8), :]
+            wide[pl.ds(base, 8), :] = jnp.where(row8 < offset, earlier, rows[:8])
+            wide[pl.ds(base + 8, slot), :] = rows[8:]
+            at = at + counts_ref[s]
+        for t in range(0, padded, tile):
+            size = min(tile, padded - t)
+            part = wide[t:t + size, :]
+            if t + size > valid:
+                part = jnp.where(
+                    lax.broadcasted_iota(jnp.int32, (size, width), 0) < valid - t, part, 0.0
+                )
+            kv[t:t + size, :] = part.astype(jnp.bfloat16)
+            kvt[:, t:t + size] = part.T.astype(jnp.bfloat16)
+        acc[...] = jnp.zeros(acc.shape, jnp.float32)
+
+    qg = qg_ref[...]
+    lane = lax.broadcasted_iota(jnp.int32, (block, width), 1)
+    zero = jnp.zeros_like(qg)
+    query = jnp.where(lane < HEAD, qg, zero)
+    grad = jnp.where(lane < HEAD, zero, qg)
+    grad_t = qg.astype(jnp.float32).T[HEAD:, :]
+    tiles = [(t, min(tile, padded - t)) for t in range(0, padded, tile)]
+    highest = jnp.full((8, block), NEG, jnp.float32)
+    for t, size in tiles:
+        part = mm(kv[t:t + size, :], query, NT)
+        if t + size > valid:
+            part = jnp.where(
+                lax.broadcasted_iota(jnp.int32, (size, block), 0) < valid - t, part, NEG
+            )
+        scores[t:t + size, :] = part
+        highest = jnp.maximum(highest, jnp.max(part.reshape(size // 8, 8, block), axis=0))
+    top = jnp.max(highest, axis=0, keepdims=True)
+    total = jnp.zeros((8, block), jnp.float32)
+    out_t = jnp.zeros((HEAD, block), jnp.float32)
+    for t, size in tiles:
+        power = jnp.exp2((scores[t:t + size, :] - top) * (factor * LOG2E))
+        scores[t:t + size, :] = power
+        total = total + jnp.sum(power.reshape(size // 8, 8, block), axis=0)
+        out_t = out_t + mm(kvt[HEAD:, t:t + size], power.astype(jnp.bfloat16))
+    inverse = 1.0 / jnp.sum(total, axis=0, keepdims=True)
+    out_t = out_t * inverse
+    delta = jnp.sum(grad_t * out_t, axis=0, keepdims=True)
+    query_t = jnp.zeros((HEAD, block), jnp.float32)
+    for t, size in tiles:
+        dprob = mm(kv[t:t + size, :], grad, NT)
+        prob = scores[t:t + size, :] * inverse
+        dscore = (prob * (dprob - delta)).astype(jnp.bfloat16)
+        acc[t:t + size, :] += mm(dscore, query) + mm(prob.astype(jnp.bfloat16), grad)
+        query_t = query_t + mm(kvt[:HEAD, t:t + size], dscore)
+    both = jnp.concatenate([out_t, query_t * factor], axis=0)
+    og_ref[...] = both.T.astype(jnp.bfloat16)
+
+    @pl.when(step == pl.num_programs(0) - 1)
+    def _():
+        scale = jnp.where(
+            lax.broadcasted_iota(jnp.int32, (slot, width), 1) < HEAD, factor, 1.0
+        )
+        row = lax.broadcasted_iota(jnp.int32, (slot, width), 0)
+        at = jnp.int32(0)
+        for s in range(sources):
+            count = counts_ref[s]
+            offset = at % 8
+            base = pl.multiple_of(at - offset, 8)
+            rows = pltpu.roll(acc[pl.ds(base, slot + 8), :], (slot + 8 - offset) % (slot + 8), 0)
+            dkv_ref[s] = jnp.where(row < count, rows[:slot] * scale, 0.0).astype(jnp.bfloat16)
+            at = at + count
+
+
+def attention(counts, kv, qg, valid, block=256, tile=256):
+    sources, slot, width = kv.shape
+    latent_rows = qg.shape[0]
+    padded = -(-valid // 128) * 128
+    room = padded + slot + 16
+    return pl.pallas_call(
+        functools.partial(attention_kernel, valid=valid, tile=tile),
+        grid_spec=pltpu.PrefetchScalarGridSpec(
+            num_scalar_prefetch=1,
+            grid=(latent_rows // block,),
+            in_specs=[
+                pl.BlockSpec((sources, slot, width), lambda i, c: (0, 0, 0)),
+                pl.BlockSpec((block, width), lambda i, c: (i, 0)),
+            ],
+            out_specs=[
+                pl.BlockSpec((block, width), lambda i, c: (i, 0)),
+                pl.BlockSpec((sources, slot, width), lambda i, c: (0, 0, 0)),
+            ],
+            scratch_shapes=[
+                pltpu.VMEM((room, width), jnp.float32),
+                pltpu.VMEM((padded, width), jnp.bfloat16),
+                pltpu.VMEM((width, padded), jnp.bfloat16),
+                pltpu.VMEM((padded, block), jnp.float32),
+                pltpu.VMEM((room, width), jnp.float32),
+            ],
+        ),
+        out_shape=[
+            jax.ShapeDtypeStruct((latent_rows, width), jnp.bfloat16),
+            jax.ShapeDtypeStruct((sources, slot, width), jnp.bfloat16),
+        ],
+        name="attention",
+    )(counts, kv, qg)
+
+
+def side_by_side(ref_part, heads, first):
+    lanes = slice(0, HEAD) if first else slice(HEAD, 2 * HEAD)
+    return jnp.concatenate([ref_part[h][:, lanes] for h in range(heads)], axis=1)
+
+
+def token_grad_kernel(dkv_ref, key_w_ref, value_w_ref, out_ref, acc, *, heads):
+    step = pl.program_id(0)
+
+    @pl.when(step == 0)
+    def _():
+        acc[...] = jnp.zeros(acc.shape, jnp.float32)
+
+    part = dkv_ref[0]
+    keys = side_by_side(part, heads, True)
+    values = side_by_side(part, heads, False)
+    acc[...] += mm(keys, key_w_ref[...], NT) + mm(values, value_w_ref[...], NT)
+
+    @pl.when(step == pl.num_programs(0) - 1)
+    def _():
+        out_ref[...] = acc[...].astype(jnp.bfloat16)
+
+
+def token_grad(dkv, weight):
+    groups, heads, rows, pair = dkv.shape
+    width = weight.shape[0]
+    cols = heads * HEAD
+    return pl.pallas_call(
+        functools.partial(token_grad_kernel, heads=heads),
+        grid=(groups,),
+        in_specs=[
+            pl.BlockSpec((1, heads, rows, pair), lambda n: (n, 0, 0, 0)),
+            pl.BlockSpec((width, cols), lambda n: (0, n)),
+            pl.BlockSpec((width, cols), lambda n: (0, n + groups)),
+        ],
+        out_specs=whole((rows, width)),
+        out_shape=jax.ShapeDtypeStruct((rows, width), jnp.bfloat16),
+        scratch_shapes=[pltpu.VMEM((rows, width), jnp.float32)],
+        name="token_grad",
+    )(dkv, weight, weight)
+
+
+def latent_grad_kernel(og_ref, w_ref, out_ref, grad_ref, acc, *, heads):
+    step = pl.program_id(0)
+
+    @pl.when(step == 0)
+    def _():
+        acc[...] = jnp.zeros(acc.shape, jnp.float32)
+
+    part = og_ref[0]
+    out_ref[...] = side_by_side(part, heads, True)
+    acc[...] += mm(side_by_side(part, heads, False), w_ref[...], NT)
+
+    @pl.when(step == pl.num_programs(0) - 1)
+    def _():
+        grad_ref[...] = acc[...].astype(jnp.bfloat16)
+
+
+def latent_grad(og, weight):
+    groups, heads, rows, pair = og.shape
+    width = weight.shape[0]
+    cols = heads * HEAD
+    return pl.pallas_call(
+        functools.partial(latent_grad_kernel, heads=heads),
+        grid=(groups,),
+        in_specs=[
+            pl.BlockSpec((1, heads, rows, pair), lambda n: (n, 0, 0, 0)),
+            pl.BlockSpec((width, cols), lambda n: (0, n)),
+        ],
+        out_specs=[pl.BlockSpec((rows, cols), lambda n: (0, n)), whole((rows, width))],
+        out_shape=[
+            jax.ShapeDtypeStruct((rows, width), jnp.bfloat16),
+            jax.ShapeDtypeStruct((rows, width), jnp.bfloat16),
+        ],
+        scratch_shapes=[pltpu.VMEM((rows, width), jnp.float32)],
+        name="latent_grad",
+    )(og, weight)
+
+
+def weight_grad_kernel(lat_ref, og_ref, out_ref, *, heads):
+    low = side_by_side(og_ref[...], heads, False)
+    out_ref[...] = lax.dot_general(
+        lat_ref[...], low, (((0,), (0,)), ((), ())), preferred_element_type=jnp.float32
+    )
+
+
+def weight_grad(latents, og):
+    rows, width = latents.shape
+    heads, _, pair = og.shape
+    cols = heads * HEAD
+    return pl.pallas_call(
+        functools.partial(weight_grad_kernel, heads=heads),
+        out_shape=jax.ShapeDtypeStruct((width, cols), jnp.float32),
+        name="weight_grad",
+    )(latents, og)
+
+
+def by_head(tokens, latents, cotangent, query_weight, keyvalue_weight, counts):
+    blocks = lax.axis_size("blk")
+    groups = lax.axis_size("narrow")
+    everyone = ("blk", "narrow")
+    tok_rows, width = tokens.shape
+    latent_rows = latents.shape[0]
+    valid = tok_rows * groups * 614 // 1024 * blocks
+    index = lax.axis_index("narrow").astype(jnp.int32).reshape(1)
+    all_counts = lax.all_to_all(
+        jnp.broadcast_to(counts, (blocks, groups)), "blk", 0, 0, tiled=True
+    ).reshape(blocks * groups)
+    pairs = project_pairs(tokens, keyvalue_weight, groups)
+    pairs = pairs.reshape(blocks * groups, tok_rows, 2 * HEAD)
+    pairs = lax.all_to_all(pairs, everyone, 0, 0, tiled=True)
+    qg = project_queries(latents, query_weight, cotangent, index, groups)
+    qg = lax.all_to_all(qg, "blk", 0, 0, tiled=True)
+    og, dkv = attention(all_counts, pairs, qg.reshape(blocks * latent_rows, 2 * HEAD), valid)
+    dkv = lax.all_to_all(dkv, everyone, 0, 0, tiled=True)
+    dkv = dkv.reshape(blocks, groups, tok_rows, 2 * HEAD).transpose(1, 0, 2, 3)
+    grad_tokens = token_grad(dkv, keyvalue_weight)
+    og = lax.all_to_all(og.reshape(blocks, latent_rows, 2 * HEAD), "blk", 0, 0, tiled=True)
+    weight_part = weight_grad(latents, og)
+    weight_part = lax.all_to_all(weight_part.reshape(blocks, width // blocks, -1), "blk", 0, 0)
+    weight_part = jnp.sum(weight_part, axis=0).astype(jnp.bfloat16)
+    grad_query_weight = lax.all_to_all(
+        jnp.broadcast_to(weight_part, (blocks,) + weight_part.shape), "blk", 0, 0
+    ).reshape(width, -1)
+    every_og = lax.all_to_all(
+        jnp.broadcast_to(og, (groups,) + og.shape), "narrow", 0, 0, tiled=False
+    )
+    latent_out, grad_latents = latent_grad(every_og, query_weight)
+    return (latent_out, grad_latents, grad_query_weight, grad_tokens)
+
+
 def on_device(tokens, latents, cotangent, query_weight, keyvalue_weight, counts):
     narrow_size = lax.axis_size("narrow")
     narrow_index = lax.axis_index("narrow")
@@ -195,8 +519,9 @@
         P(),
         P(("groups", "blk"), None),
     )
+    one_head_each = mesh.shape["blk"] * mesh.shape["narrow"] == HEADS
     return jax.shard_map(
-        on_device,
+        by_head if one_head_each else on_device,
         mesh=mesh,
         in_specs=placed,
         out_specs=(

time: 776 us -> 224 us (0.29)
  waiting for transfers between devices: 381 us -> 71.7 us
  matrix products: 105 us -> 0 us
  local copies, waits for them, and re-layouts: 70.6 us -> 8.3 us
  blocking collectives: 134 us -> 72.6 us
  Pallas kernels: 0 us -> 52.1 us
  other arithmetic: 49.2 us -> 0.73 us
  between operations: 14.1 us -> 0.69 us
    ppermute x32 -> x0, waiting for transfers between devices: 232 us -> none  [shifted(): lax.ppermute(shard, axis, [(i, (i + by) % length) for i in range(length)])]
    all_gather x1 -> x0, waiting for transfers between devices: 120 us -> none  [merged_2(): everything = jax.tree.map(lambda part: lax.all_gather(part, axis), shard)]
    dot_general x33 -> x0, matrix products: 105 us -> none  [the longest x4 19.9 us: attend_forward(): jnp.einsum('hqk,khd->qhd', powers.astype(jnp.bfloat16), value_heads, pref...]
    psum x2 -> x0, blocking collectives: 102 us -> none  [the longest x1 76.5 us: on_device(): grad_latents = lax.psum(latent_term, 'narrow').astype(jnp.bfloat16)]
    all_to_all x0 -> x4, blocking collectives: none -> 72.6 us  [the longest x1 29.5 us: by_head(): dkv = lax.all_to_all(dkv, everyone, 0, 0, tiled=True)]
    all_to_all x0 -> x4, waiting for transfers between devices: none -> 71.7 us  [the longest x1 42.2 us: by_head(): lax.all_to_all(jnp.broadcast_to(og, (groups,) + og.shape), 'narrow', 0, 0...]
    pallas_call x0 -> x6, Pallas kernels: none -> 52.1 us  [the longest x1 30.7 us: attention(): pl.pallas_call(functools.partial(attention_kernel, valid=valid, tile=tile...]
    all_gather x2 -> x0, blocking collectives: 31.9 us -> none  [merged_2(): everything = jax.tree.map(lambda part: lax.all_gather(part, axis), shard)]
  transfers between devices with their start and end apart: 34 -> 4, of which waited for: 18 -> 4; matrix products, arithmetic and copies ran while one was open for 8% -> 1% of each run, Pallas kernels for 0% -> 6%
where the time goes in v1:
time: 224 us; the launch traced here: 223 us
  blocking collectives  72.6 us (32%)
  waiting for transfers between devices  71.7 us (32%)
  Pallas kernels  52.1 us (23%)
  starting transfers between devices  16.7 us (7%)
  local copies, waits for them, and re-layouts  8.3 us (4%)
    all_to_all x1, waiting for transfers between devices, by_head(): lax.all_to_all(jnp.broadcast_to(og, (groups,) + og.shape), 'narrow', 0, 0...  42.2 us
    pallas_call x1, Pallas kernels, attention(): pl.pallas_call(functools.partial(attention_kernel, valid=valid, tile=tile...  30.7 us
    all_to_all x1, blocking collectives, by_head(): dkv = lax.all_to_all(dkv, everyone, 0, 0, tiled=True)  29.5 us
    all_to_all x1, waiting for transfers between devices, by_head(): pairs = lax.all_to_all(pairs, everyone, 0, 0, tiled=True)  25 us
    all_to_all x1, blocking collectives, by_head(): lax.all_to_all(weight_part.reshape(blocks, width // blocks, -1), 'blk', 0...  18 us
    all_to_all x1, blocking collectives, by_head(): lax.all_to_all(og.reshape(blocks, latent_rows, 2 * HEAD), 'blk', 0, 0, ti...  13 us
    all_to_all x1, blocking collectives, by_head(): lax.all_to_all(jnp.broadcast_to(weight_part, (blocks,) + weight_part.shap...  12 us
    pallas_call x1, Pallas kernels, latent_grad(): pl.pallas_call(functools.partial(latent_grad_kernel, heads=heads), grid=(...  5.44 us
  transfers between devices with their start and end apart: 4, of which 4 were waited for; matrix products, arithmetic and copies ran while one was open for 1% of the time, Pallas kernels for 6%

profile of v1, /device:TPU:0, one launch (start us, length us, event | category | flops | bytes accessed | tf_op | source)
XLA Modules:
  0.0 222.8 jit_solution(2115218888666394870)
XLA Ops:
  0.6 1.2 broadcast_in_dim.11
  1.9 4.2 %all-to-all-start = ((s32[4,1,4]{2,1,0:T(1,128)}), s32[4,1,4]{2,1,0:T(1,128)S(1)}, u32[]{:S(2)}, u32[]{:S(2)}) async-start(s32[4,1,4]{2,1,0:T(1,128)} %broadcast_in_dim.11), calls=%async_computation | async-start | bytes 4096 | tf_op jit(solution)/shard_map/all_to_all | solution.py:441
  6.1 2.7 %project_queries.1 = bf16[4,512,128]{2,1,0:T(8,128)(2,1)} custom-call(s32[1]{0:T(128)} %bitcast.2.index_ref, bf16[512,1024]{1,0:T(8,128)(2,1)} %lat_ref.3, bf16[1024,1024]{1,0:T(8,128)(2,1)} %w_ref.3, bf16[512,1024]{1,0:T(8,128)(2,1)} %grad_ref.1), custom_call_target="tpu_custom_call" | custom-call | tf_op jit(solution)/shard_map/project_queries/pallas_call | solution.py:199
  8.8 1.0 all-to-all-done
  9.8 3.5 %all-to-all-start.2 = ((bf16[4,512,128]{2,1,0:T(8,128)(2,1)}), bf16[4,512,128]{2,1,0:T(8,128)(2,1)S(1)}, u32[]{:S(2)}, u32[]{:S(2)}) async-start(bf16[4,512,128]{2,1,0:T(8,128)(2,1)} %project_queries.1), calls=%async_computation.2 | async-start | bytes 1048576 | tf_op jit(solution)/shard_map/all_to_all | solution.py:448
  13.3 5.3 %project_pairs.1 = bf16[4,4,256,128]{3,2,1,0:T(8,128)(2,1)} custom-call(bf16[256,1024]{1,0:T(8,128)(2,1)} %tok_ref.1, bf16[1024,2048]{1,0:T(8,128)(2,1)} %value_w_ref.3, bf16[1024,2048]{1,0:T(8,128)(2,1)} %value_w_ref.3), custom_call_target="tpu_custom_call" | custom-call | tf_op jit(solution)/shard_map/project_pairs/pallas_call | solution.py:173
  18.6 3.5 %all-to-all-done.2 = bf16[4,512,128]{2,1,0:T(8,128)(2,1)S(1)} async-done(((bf16[4,512,128]{2,1,0:T(8,128)(2,1)}), bf16[4,512,128]{2,1,0:T(8,128)(2,1)S(1)}, u32[]{:S(2)}, u32[]{:S(2)}) %all-to-all-start.2) | async-done | bytes 524320 | tf_op jit(solution)/shard_map/all_to_all | solution.py:448
  22.1 5.4 %all-to-all-start.1 = ((bf16[16,256,128]{2,1,0:T(8,128)(2,1)}), bf16[16,256,128]{2,1,0:T(8,128)(2,1)S(1)}, u32[]{:S(2)}, u32[]{:S(2)}) async-start(bf16[16,256,128]{2,1,0:T(8,128)(2,1)} %bitcast.11), calls=%async_computation.1 | async-start | bytes 2097152 | tf_op jit(solution)/shard_map/all_to_all | solution.py:446
  27.5 0.5 broadcast.8
  28.0 0.7 reduce.3
  28.7 0.6 reshape.39.counts_ref
  29.3 25.0 %all-to-all-done.1.kv_ref = bf16[16,256,128]{2,1,0:T(8,128)(2,1)S(1)} async-done(((bf16[16,256,128]{2,1,0:T(8,128)(2,1)}), bf16[16,256,128]{2,1,0:T(8,128)(2,1)S(1)}, u32[]{:S(2)}, u32[]{:S(2)}) %all-to-all-start.1) | async-done | bytes 1048608 | tf_op jit(solution)/shard_map/all_to_all | solution.py:446
  54.3 0.0 copy-done.3
  54.3 1.0 copy-done.2
  55.3 30.7 %attention.1 = (bf16[2048,128]{1,0:T(8,128)(2,1)}, bf16[16,256,128]{2,1,0:T(8,128)(2,1)}) custom-call(s32[16]{0:T(128)} %reshape.39.counts_ref, bf16[16,256,128]{2,1,0:T(8,128)(2,1)} %copy-done.2, bf16[2048,128]{1,0:T(8,128)(2,1)} %bitcast.15), custom_call_target="tpu_custom_call" | custom-call | tf_op jit(solution)/shard_map/attention/pallas_call | solution.py:308
  86.0 13.0 %all_to_all.41.og_ref = bf16[4,512,128]{2,1,0:T(8,128)(2,1)} all-to-all(bf16[4,512,128]{2,1,0:T(8,128)(2,1)} %bitcast.17), channel_id=1, replica_groups=mesh['groups'=2,'blk'=4,'narrow'=4] {'blk'}, dimensions={0} | all-to-all | bytes 1048576 | tf_op jit(solution)/shard_map/all_to_all | solution.py:453
  99.0 2.9 %weight_grad.1 = f32[1024,256]{1,0:T(8,128)} custom-call(bf16[512,1024]{1,0:T(8,128)(2,1)} %lat_ref.3, bf16[4,512,128]{2,1,0:T(8,128)(2,1)} %all_to_all.41.og_ref), custom_call_target="tpu_custom_call" | custom-call | tf_op jit(solution)/shard_map/weight_grad/pallas_call | solution.py:426
  101.9 18.0 %all_to_all.42 = f32[4,256,256]{2,1,0:T(8,128)S(1)} all-to-all(f32[4,256,256]{2,1,0:T(8,128)} %bitcast.14), channel_id=1, replica_groups=mesh['groups'=2,'blk'=4,'narrow'=4] {'blk'}, dimensions={0} | all-to-all | bytes 2097152 | tf_op jit(solution)/shard_map/all_to_all | solution.py:455
  119.9 0.1 reduce_sum.9
  120.0 0.0 copy-start.1
  120.1 12.0 %all_to_all.43 = bf16[4,256,256]{2,1,0:T(8,128)(2,1)} all-to-all(bf16[4,256,256]{2,1,0:T(8,128)(2,1)S(1)} %broadcast_in_dim.13), channel_id=1, replica_groups=mesh['groups'=2,'blk'=4,'narrow'=4] {'blk'}, dimensions={0} | all-to-all | bytes 1048576 | tf_op jit(solution)/shard_map/all_to_all | solution.py:457
  132.1 0.0 copy-done.5
  132.1 29.5 %all_to_all.44 = bf16[16,256,128]{2,1,0:T(8,128)(2,1)S(1)} all-to-all(bf16[16,256,128]{2,1,0:T(8,128)(2,1)S(1)} %copy-done.5), channel_id=1, replica_groups=mesh['groups'=2,'blk'=4,'narrow'=4] {'blk','narrow'}, dimensions={0} | all-to-all | bytes 2097152 | tf_op jit(solution)/shard_map/all_to_all | solution.py:450
  161.6 0.0 copy-done.1
  161.6 1.7 broadcast_in_dim.12
  163.3 3.6 %all-to-all-start.4 = ((bf16[4,4,512,128]{3,2,1,0:T(8,128)(2,1)}), bf16[4,4,512,128]{3,2,1,0:T(8,128)(2,1)S(1)}, u32[]{:S(2)}, u32[]{:S(2)}) async-start(bf16[4,4,512,128]{3,2,1,0:T(8,128)(2,1)} %broadcast_in_dim.12), calls=%async_computation.4 | async-start | bytes 4194304 | tf_op jit(solution)/shard_map/all_to_all | solution.py:460
  166.9 1.0 copy.13
  168.0 5.0 %token_grad.1 = bf16[256,1024]{1,0:T(8,128)(2,1)} custom-call(bf16[4,4,256,128]{3,2,1,0:T(8,128)(2,1)} %bitcast.12, bf16[1024,2048]{1,0:T(8,128)(2,1)} %value_w_ref.3, bf16[1024,2048]{1,0:T(8,128)(2,1)} %value_w_ref.3), custom_call_target="tpu_custom_call" | custom-call | tf_op jit(solution)/shard_map/token_grad/pallas_call | solution.py:363
  173.0 42.2 %all-to-all-done.4.og_ref = bf16[4,4,512,128]{3,2,1,0:T(8,128)(2,1)S(1)} async-done(((bf16[4,4,512,128]{3,2,1,0:T(8,128)(2,1)}), bf16[4,4,512,128]{3,2,1,0:T(8,128)(2,1)S(1)}, u32[]{:S(2)}, u32[]{:S(2)}) %all-to-all-start.4) | async-done | bytes 2097184 | tf_op jit(solution)/shard_map/all_to_all | solution.py:460
  215.3 1.3 copy-done
  216.6 5.4 %latent_grad.1 = (bf16[512,1024]{1,0:T(8,128)(2,1)}, bf16[512,1024]{1,0:T(8,128)(2,1)}) custom-call(bf16[4,4,512,128]{3,2,1,0:T(8,128)(2,1)} %copy-done, bf16[1024,1024]{1,0:T(8,128)(2,1)} %w_ref.3), custom_call_target="tpu_custom_call" | custom-call | tf_op jit(solution)/shard_map/latent_grad/pallas_call | solution.py:398
  222.0 0.8 copy.15
  (7 shorter events, 0.0 us)
Async XLA Ops:
  1.9 7.9 %all-to-all-start = ((s32[4,1,4]{2,1,0:T(1,128)}), s32[4,1,4]{2,1,0:T(1,128)S(1)}, u32[]{:S(2)}, u32[]{:S(2)}) async-start(s32[4,1,4]{2,1,0:T(1,128)} %broadcast_in_dim.11), calls=%async_computation | async-start | bytes 4096 | tf_op jit(solution)/shard_map/all_to_all | solution.py:441
  9.8 12.3 %all-to-all-start.2 = ((bf16[4,512,128]{2,1,0:T(8,128)(2,1)}), bf16[4,512,128]{2,1,0:T(8,128)(2,1)S(1)}, u32[]{:S(2)}, u32[]{:S(2)}) async-start(bf16[4,512,128]{2,1,0:T(8,128)(2,1)} %project_queries.1), calls=%async_computation.2 | async-start | bytes 1048576 | tf_op jit(solution)/shard_map/all_to_all | solution.py:448
  22.1 32.3 %copy-start.3 = (bf16[4,512,128]{2,1,0:T(8,128)(2,1)}, bf16[4,512,128]{2,1,0:T(8,128)(2,1)S(1)}, u32[]{:S(2)}) copy-start(bf16[4,512,128]{2,1,0:T(8,128)(2,1)S(1)} %all-to-all-done.2) | copy-start | bytes 1572868
  22.1 32.3 %all-to-all-start.1 = ((bf16[16,256,128]{2,1,0:T(8,128)(2,1)}), bf16[16,256,128]{2,1,0:T(8,128)(2,1)S(1)}, u32[]{:S(2)}, u32[]{:S(2)}) async-start(bf16[16,256,128]{2,1,0:T(8,128)(2,1)} %bitcast.11), calls=%async_computation.1 | async-start | bytes 2097152 | tf_op jit(solution)/shard_map/all_to_all | solution.py:446
  54.3 1.0 copy-start.2
  101.9 30.2 %copy-start.5 = (bf16[16,256,128]{2,1,0:T(8,128)(2,1)S(1)}, bf16[16,256,128]{2,1,0:T(8,128)(2,1)}, u32[]{:S(2)}) copy-start(bf16[16,256,128]{2,1,0:T(8,128)(2,1)} %get-tuple-element.11) | copy-start | bytes 3145732
  120.0 41.6 %copy-start.1 = (bf16[4,512,128]{2,1,0:T(8,128)(2,1)S(1)}, bf16[4,512,128]{2,1,0:T(8,128)(2,1)}, u32[]{:S(2)}) copy-start(bf16[4,512,128]{2,1,0:T(8,128)(2,1)} %all_to_all.41.og_ref) | copy-start | bytes 1572868
  163.3 51.9 %all-to-all-start.4 = ((bf16[4,4,512,128]{3,2,1,0:T(8,128)(2,1)}), bf16[4,4,512,128]{3,2,1,0:T(8,128)(2,1)S(1)}, u32[]{:S(2)}, u32[]{:S(2)}) async-start(bf16[4,4,512,128]{3,2,1,0:T(8,128)(2,1)} %broadcast_in_dim.12), calls=%async_computation.4 | async-start | bytes 4194304 | tf_op jit(solution)/shard_map/all_to_all | solution.py:460
  173.0 49.0 %copy-start.4 = (bf16[4,256,256]{2,1,0:T(8,128)(2,1)S(1)}, bf16[4,256,256]{2,1,0:T(8,128)(2,1)}, u32[]{:S(2)}) copy-start(bf16[4,256,256]{2,1,0:T(8,128)(2,1)} %all_to_all.43) | copy-start | bytes 1572868
  215.2 1.3 copy-start

commit v2 on v0

--- a/solution.py
+++ b/solution.py
@@ -1,6 +1,10 @@
+import functools
+
 import jax
 import jax.numpy as jnp
 from jax import lax
+from jax.experimental import pallas as pl
+from jax.experimental.pallas import tpu as pltpu
 from jax.sharding import PartitionSpec as P
 
 HEADS = 16
@@ -140,6 +144,452 @@
     return (final[3], final[4], final[5])
 
 
+NT = (((1,), (1,)), ((), ()))
+NN = (((1,), (0,)), ((), ()))
+LOG2E = 1.4426950408889634
+
+
+def mm(one, two, dims=NN):
+    return lax.dot_general(one, two, dims, preferred_element_type=jnp.float32)
+
+
+def whole(shape):
+    return pl.BlockSpec(shape, lambda *unused: (0,) * len(shape))
+
+
+def pairs_kernel(tok_ref, key_w_ref, value_w_ref, out_ref, *, heads):
+    tok = tok_ref[...]
+    keys = mm(tok, key_w_ref[...]).astype(jnp.bfloat16)
+    values = mm(tok, value_w_ref[...]).astype(jnp.bfloat16)
+    for h in range(heads):
+        cols = slice(h * HEAD, (h + 1) * HEAD)
+        out_ref[h, 0] = jnp.concatenate([keys[:, cols], values[:, cols]], axis=1)
+
+
+def project_pairs(tokens, weight, groups):
+    rows, width = tokens.shape
+    cols = width // groups
+    heads = cols // HEAD
+    return pl.pallas_call(
+        functools.partial(pairs_kernel, heads=heads),
+        grid=(groups,),
+        in_specs=[
+            whole((rows, width)),
+            pl.BlockSpec((width, cols), lambda n: (0, n)),
+            pl.BlockSpec((width, cols), lambda n: (0, n + groups)),
+        ],
+        out_specs=pl.BlockSpec((heads, 1, rows, 2 * HEAD), lambda n: (0, n, 0, 0)),
+        out_shape=jax.ShapeDtypeStruct((heads, groups, rows, 2 * HEAD), jnp.bfloat16),
+        name="project_pairs",
+    )(tokens, weight, weight)
+
+
+def queries_kernel(
+    index_ref, counts_ref, lat_ref, w_ref, grad_ref, out_ref, queries, *, heads, extra
+):
+    step = pl.program_id(0)
+    rows = grad_ref.shape[0]
+
+    @pl.when(step == 0)
+    def _():
+        queries[...] = mm(lat_ref[...], w_ref[...]).astype(jnp.bfloat16)
+
+    lane = lax.broadcasted_iota(jnp.int32, (extra, 2 * HEAD), 1)
+    counts = jnp.zeros((extra, 2 * HEAD), jnp.float32)
+    for n in range(counts_ref.shape[0]):
+        counts = jnp.where(lane == n, counts_ref[n].astype(jnp.float32), counts)
+    out_ref[0, rows:, :] = counts.astype(jnp.bfloat16)
+    for h in range(heads):
+        cols = slice(h * HEAD, (h + 1) * HEAD)
+
+        @pl.when(step == h)
+        def _(cols=cols):
+            out_ref[0, :rows, :] = jnp.concatenate([queries[:, cols], grad_ref[:, cols]], axis=1)
+
+
+def project_queries(latents, weight, cotangent, index, counts, groups, extra=16):
+    rows, width = latents.shape
+    cols = width // groups
+    heads = cols // HEAD
+    return pl.pallas_call(
+        functools.partial(queries_kernel, heads=heads, extra=extra),
+        grid_spec=pltpu.PrefetchScalarGridSpec(
+            num_scalar_prefetch=2,
+            grid=(heads,),
+            in_specs=[
+                pl.BlockSpec((rows, width), lambda i, at, c: (0, 0)),
+                pl.BlockSpec((width, cols), lambda i, at, c: (0, at[0])),
+                pl.BlockSpec((rows, cols), lambda i, at, c: (0, at[0])),
+            ],
+            out_specs=pl.BlockSpec(
+                (1, rows + extra, 2 * HEAD), lambda i, at, c: (i ^ at[1], 0, 0)
+            ),
+            scratch_shapes=[pltpu.VMEM((rows, cols), jnp.bfloat16)],
+        ),
+        out_shape=jax.ShapeDtypeStruct((heads, rows + extra, 2 * HEAD), jnp.bfloat16),
+        name="project_queries",
+    )(index, counts, latents, weight, cotangent)
+
+
+def count_of(counts_ref, index_ref, source):
+    return counts_ref[source // 4 ^ index_ref[1], source % 4]
+
+
+def pack_tokens(counts_ref, index_ref, kv_ref, wide, kv, kvt, valid, tile):
+    sources, slot, width = kv_ref.shape
+    padded = kv.shape[0]
+    row8 = lax.broadcasted_iota(jnp.int32, (8, width), 0)
+    at = jnp.int32(0)
+    for s in range(sources):
+        offset = at % 8
+        base = pl.multiple_of(at - offset, 8)
+        rows = kv_ref[s].astype(jnp.float32)
+        rows = jnp.concatenate([rows, jnp.zeros((8, width), jnp.float32)], axis=0)
+        rows = pltpu.roll(rows, offset, 0)
+        earlier = wide[pl.ds(base, 8), :]
+        wide[pl.ds(base, 8), :] = jnp.where(row8 < offset, earlier, rows[:8])
+        wide[pl.ds(base + 8, slot), :] = rows[8:]
+        at = at + count_of(counts_ref, index_ref, s)
+    for t in range(0, padded, tile):
+        size = min(tile, padded - t)
+        part = wide[t:t + size, :]
+        if t + size > valid:
+            part = jnp.where(
+                lax.broadcasted_iota(jnp.int32, (size, width), 0) < valid - t, part, 0.0
+            )
+        kv[t:t + size, :] = part.astype(jnp.bfloat16)
+        kvt[:, t:t + size] = part.T.astype(jnp.bfloat16)
+
+
+def unpack_tokens(counts_ref, index_ref, acc, dkv_ref):
+    sources, slot, width = dkv_ref.shape
+    scale = jnp.where(
+        lax.broadcasted_iota(jnp.int32, (slot, width), 1) < HEAD, HEAD ** (-0.5), 1.0
+    )
+    row = lax.broadcasted_iota(jnp.int32, (slot, width), 0)
+    at = jnp.int32(0)
+    for s in range(sources):
+        count = count_of(counts_ref, index_ref, s)
+        offset = at % 8
+        base = pl.multiple_of(at - offset, 8)
+        rows = pltpu.roll(acc[pl.ds(base, slot + 8), :], (slot + 8 - offset) % (slot + 8), 0)
+        dkv_ref[s] = jnp.where(row < count, rows[:slot] * scale, 0.0).astype(jnp.bfloat16)
+        at = at + count
+
+
+def attend_block(qg, kv, kvt, scores, acc, valid, tile):
+    block, width = qg.shape
+    padded = kv.shape[0]
+    factor = HEAD ** (-0.5)
+    lane = lax.broadcasted_iota(jnp.int32, (block, width), 1)
+    zero = jnp.zeros_like(qg)
+    query = jnp.where(lane < HEAD, qg, zero)
+    grad = jnp.where(lane < HEAD, zero, qg)
+    grad_t = qg.astype(jnp.float32).T[HEAD:, :]
+    tiles = [(t, min(tile, padded - t)) for t in range(0, padded, tile)]
+    highest = jnp.full((8, block), NEG, jnp.float32)
+    for t, size in tiles:
+        part = mm(kv[t:t + size, :], query, NT)
+        if t + size > valid:
+            part = jnp.where(
+                lax.broadcasted_iota(jnp.int32, (size, block), 0) < valid - t, part, NEG
+            )
+        scores[t:t + size, :] = part
+        highest = jnp.maximum(highest, jnp.max(part.reshape(size // 8, 8, block), axis=0))
+    top = jnp.max(highest, axis=0, keepdims=True)
+    total = jnp.zeros((8, block), jnp.float32)
+    out_t = jnp.zeros((HEAD, block), jnp.float32)
+    for t, size in tiles:
+        power = jnp.exp2((scores[t:t + size, :] - top) * (factor * LOG2E))
+        scores[t:t + size, :] = power
+        total = total + jnp.sum(power.reshape(size // 8, 8, block), axis=0)
+        out_t = out_t + mm(kvt[HEAD:, t:t + size], power.astype(jnp.bfloat16))
+    inverse = 1.0 / jnp.sum(total, axis=0, keepdims=True)
+    out_t = out_t * inverse
+    delta = jnp.sum(grad_t * out_t, axis=0, keepdims=True)
+    query_t = jnp.zeros((HEAD, block), jnp.float32)
+    for t, size in tiles:
+        dprob = mm(kv[t:t + size, :], grad, NT)
+        prob = scores[t:t + size, :] * inverse
+        dscore = (prob * (dprob - delta)).astype(jnp.bfloat16)
+        acc[t:t + size, :] += mm(dscore, query) + mm(prob.astype(jnp.bfloat16), grad)
+        query_t = query_t + mm(kvt[:HEAD, t:t + size], dscore)
+    both = jnp.concatenate([out_t, query_t * factor], axis=0)
+    return both.T.astype(jnp.bfloat16)
+
+
+def first_kernel(
+    counts_ref, index_ref, kv_ref, qg_ref, og_ref, kv, kvt, acc, wide, scores, *, valid, tile
+):
+    @pl.when(pl.program_id(0) == 0)
+    def _():
+        pack_tokens(counts_ref, index_ref, kv_ref, wide, kv, kvt, valid, tile)
+        acc[...] = jnp.zeros(acc.shape, jnp.float32)
+
+    og_ref[0] = attend_block(qg_ref[0], kv, kvt, scores, acc, valid, tile)
+
+
+def later_kernel(
+    counts_ref,
+    index_ref,
+    kv,
+    kvt,
+    acc_ref,
+    qg_ref,
+    og_ref,
+    out_ref,
+    acc,
+    scores,
+    *,
+    valid,
+    tile,
+    last,
+):
+    @pl.when(pl.program_id(0) == 0)
+    def _():
+        acc[...] = acc_ref[...]
+
+    og_ref[0] = attend_block(qg_ref[0], kv, kvt, scores, acc, valid, tile)
+
+    @pl.when(pl.program_id(0) == pl.num_programs(0) - 1)
+    def _():
+        if last:
+            unpack_tokens(counts_ref, index_ref, acc, out_ref)
+        else:
+            out_ref[...] = acc[...]
+
+
+def attention(counts, index, kv, qg, valid, latent_rows, chunks, tile=256):
+    sources, slot, width = kv.shape
+    blocks = qg.shape[0]
+    block = latent_rows // chunks
+    padded = -(-valid // 128) * 128
+    room = padded + slot + 16
+    packed = [
+        jax.ShapeDtypeStruct((padded, width), jnp.bfloat16),
+        jax.ShapeDtypeStruct((width, padded), jnp.bfloat16),
+    ]
+    acc_shape = jax.ShapeDtypeStruct((room, width), jnp.float32)
+    og_shape = jax.ShapeDtypeStruct((blocks, block, width), jnp.bfloat16)
+    wide = pltpu.VMEM((room, width), jnp.float32)
+    scores = pltpu.VMEM((padded, block), jnp.float32)
+    og_spec = pl.BlockSpec((1, block, width), lambda i, c, at: (i, 0, 0))
+    cost = pl.CostEstimate(
+        flops=24 * blocks * block * padded * 256,
+        transcendentals=blocks * block * padded,
+        bytes_accessed=4 * room * width * 3,
+    )
+    outs = []
+    for j in range(chunks):
+        last = j == chunks - 1
+        qg_spec = pl.BlockSpec((1, block, width), lambda i, c, at, j=j: (i, j, 0))
+        if j == 0:
+            og, key_value, key_value_t, acc = pl.pallas_call(
+                functools.partial(first_kernel, valid=valid, tile=tile),
+                grid_spec=pltpu.PrefetchScalarGridSpec(
+                    num_scalar_prefetch=2,
+                    grid=(blocks,),
+                    in_specs=[whole(kv.shape), qg_spec],
+                    out_specs=[og_spec] + [whole(s.shape) for s in packed + [acc_shape]],
+                    scratch_shapes=[wide, scores],
+                ),
+                out_shape=[og_shape] + packed + [acc_shape],
+                cost_estimate=cost,
+                name="attention_first",
+            )(counts, index, kv, qg)
+        else:
+            out_shape = jax.ShapeDtypeStruct(kv.shape, jnp.bfloat16) if last else acc_shape
+            og, acc = pl.pallas_call(
+                functools.partial(later_kernel, valid=valid, tile=tile, last=last),
+                grid_spec=pltpu.PrefetchScalarGridSpec(
+                    num_scalar_prefetch=2,
+                    grid=(blocks,),
+                    in_specs=[whole(s.shape) for s in packed + [acc_shape]] + [qg_spec],
+                    out_specs=[og_spec, whole(out_shape.shape)],
+                    scratch_shapes=[wide, scores],
+                ),
+                out_shape=[og_shape, out_shape],
+                cost_estimate=cost,
+                name="attention_later",
+            )(counts, index, key_value, key_value_t, acc, qg)
+        outs.append(og)
+    return outs, acc
+
+
+def side_by_side(part, heads, first, flip=0):
+    lanes = slice(0, HEAD) if first else slice(HEAD, 2 * HEAD)
+    return jnp.concatenate([part[h ^ flip][:, lanes] for h in range(heads)], axis=1)
+
+
+def token_grad_kernel(dkv_ref, key_w_ref, value_w_ref, out_ref, acc, *, heads):
+    step = pl.program_id(0)
+
+    @pl.when(step == 0)
+    def _():
+        acc[...] = jnp.zeros(acc.shape, jnp.float32)
+
+    part = [dkv_ref[h, 0] for h in range(heads)]
+    keys = side_by_side(part, heads, True)
+    values = side_by_side(part, heads, False)
+    acc[...] += mm(keys, key_w_ref[...], NT) + mm(values, value_w_ref[...], NT)
+
+    @pl.when(step == pl.num_programs(0) - 1)
+    def _():
+        out_ref[...] = acc[...].astype(jnp.bfloat16)
+
+
+def token_grad(dkv, weight):
+    heads, groups, rows, pair = dkv.shape
+    width = weight.shape[0]
+    cols = heads * HEAD
+    return pl.pallas_call(
+        functools.partial(token_grad_kernel, heads=heads),
+        grid=(groups,),
+        in_specs=[
+            pl.BlockSpec((heads, 1, rows, pair), lambda n: (0, n, 0, 0)),
+            pl.BlockSpec((width, cols), lambda n: (0, n)),
+            pl.BlockSpec((width, cols), lambda n: (0, n + groups)),
+        ],
+        out_specs=whole((rows, width)),
+        out_shape=jax.ShapeDtypeStruct((rows, width), jnp.bfloat16),
+        scratch_shapes=[pltpu.VMEM((rows, width), jnp.float32)],
+        name="token_grad",
+    )(dkv, weight, weight)
+
+
+def latent_grad_kernel(index_ref, *refs, heads, groups):
+    w_ref = refs[groups]
+    out_ref, grad_ref = refs[-2:]
+    cols = heads * HEAD
+    total = None
+    for k in range(groups):
+        part = refs[k]
+        at = pl.multiple_of((index_ref[0] ^ k) * cols, cols)
+        out_ref[:, pl.ds(at, cols)] = side_by_side(part, heads, True, index_ref[1])
+        term = mm(side_by_side(part, heads, False, index_ref[1]), w_ref[:, pl.ds(at, cols)], NT)
+        total = term if total is None else total + term
+    grad_ref[...] = total.astype(jnp.bfloat16)
+
+
+def latent_grad(index, parts, weight, chunk, chunks, earlier):
+    heads, rows, pair = parts[0].shape
+    groups = len(parts)
+    width = weight.shape[0]
+    shape = jax.ShapeDtypeStruct((rows * chunks, width), jnp.bfloat16)
+    part_spec = pl.BlockSpec((heads, rows, pair), lambda i, at: (0, 0, 0))
+    out_spec = pl.BlockSpec((rows, width), lambda i, at: (chunk, 0))
+    return pl.pallas_call(
+        functools.partial(latent_grad_kernel, heads=heads, groups=groups),
+        grid_spec=pltpu.PrefetchScalarGridSpec(
+            num_scalar_prefetch=1,
+            grid=(1,),
+            in_specs=[part_spec] * groups
+            + [pl.BlockSpec(weight.shape, lambda i, at: (0, 0))]
+            + [pl.BlockSpec(memory_space=pl.ANY)] * len(earlier),
+            out_specs=[out_spec, out_spec],
+        ),
+        out_shape=[shape, shape],
+        input_output_aliases={2 + groups + k: k for k in range(len(earlier))},
+        name="latent_grad",
+    )(index, *parts, weight, *earlier)
+
+
+def weight_grad_kernel(*refs, slots):
+    out_ref = refs[-1]
+    total = None
+    for k in range(slots):
+        at = 0
+        for og_ref in refs[slots:-1]:
+            rows = og_ref.shape[1]
+            low = og_ref[k].astype(jnp.float32).T[HEAD:, :].astype(jnp.bfloat16)
+            term = mm(low, refs[k][at:at + rows, :])
+            total = term if total is None else total + term
+            at = at + rows
+    out_ref[...] = total.astype(jnp.bfloat16)
+
+
+def weight_grad(latents, outs):
+    width = latents[0].shape[1]
+    return pl.pallas_call(
+        functools.partial(weight_grad_kernel, slots=len(latents)),
+        out_shape=jax.ShapeDtypeStruct((HEAD, width), jnp.bfloat16),
+        name="weight_grad",
+    )(*latents, *outs)
+
+
+def turn_kernel(index_ref, *refs):
+    out_ref, scratch = refs[-2:]
+    for k, ref in enumerate(refs[:-2]):
+        at = pl.multiple_of((index_ref[1] ^ k) * HEAD, HEAD)
+        scratch[pl.ds(at, HEAD), :] = ref[...].astype(jnp.float32)
+    out_ref[...] = scratch[...].T.astype(jnp.bfloat16)
+
+
+def turn(index, parts):
+    width = parts[0].shape[1]
+    cols = HEAD * len(parts)
+    spec = pl.BlockSpec((HEAD, width), lambda i, at: (0, 0))
+    return pl.pallas_call(
+        turn_kernel,
+        grid_spec=pltpu.PrefetchScalarGridSpec(
+            num_scalar_prefetch=1,
+            grid=(1,),
+            in_specs=[spec] * len(parts),
+            out_specs=pl.BlockSpec((width, cols), lambda i, at: (0, 0)),
+            scratch_shapes=[pltpu.VMEM((cols, width), jnp.float32)],
+        ),
+        out_shape=jax.ShapeDtypeStruct((width, cols), jnp.bfloat16),
+        name="turn",
+    )(index, *parts)
+
+
+def swapped(shard, axis, bit):
+    return lax.ppermute(shard, axis, [(i, i ^ bit) for i in range(lax.axis_size(axis))])
+
+
+def exchanged(slots, axis):
+    others = [swapped(slots[k], axis, k) for k in range(1, slots.shape[0])]
+    return jnp.stack([slots[0]] + others)
+
+
+def gathered(shard, axis):
+    near = swapped(shard, axis, 1)
+    far = swapped(shard, axis, 2)
+    return [shard, near, far, swapped(far, axis, 1)]
+
+
+def by_head(tokens, latents, cotangent, query_weight, keyvalue_weight, counts):
+    blocks = lax.axis_size("blk")
+    groups = lax.axis_size("narrow")
+    everyone = ("blk", "narrow")
+    tok_rows, width = tokens.shape
+    latent_rows = latents.shape[0]
+    chunks = 2
+    valid = tok_rows * groups * 614 // 1024 * blocks
+    index = jnp.stack([lax.axis_index("narrow"), lax.axis_index("blk")]).astype(jnp.int32)
+    pairs = project_pairs(tokens, keyvalue_weight, groups)
+    pairs = pairs.reshape(blocks * groups, tok_rows, 2 * HEAD)
+    held, pairs = lax.optimization_barrier((latents, pairs))
+    pairs = lax.all_to_all(pairs, everyone, 0, 0, tiled=True)
+    qg = project_queries(held, query_weight, cotangent, index, counts.reshape(groups), groups)
+    qg = exchanged(qg, "blk")
+    all_counts = qg[:, latent_rows, :groups].astype(jnp.int32)
+    held, qg = lax.optimization_barrier((latents, qg))
+    every = gathered(held, "blk")
+    outs, dkv = attention(all_counts, index, pairs, qg, valid, latent_rows, chunks)
+    parts = [gathered(exchanged(og, "blk"), "narrow") for og in outs]
+    dkv = lax.all_to_all(dkv, everyone, 0, 0, tiled=True)
+    grad_tokens = token_grad(
+        dkv.reshape(blocks, groups, tok_rows, 2 * HEAD), keyvalue_weight
+    )
+    grad_query_weight = turn(index, gathered(weight_grad(every, outs), "blk"))
+    done = ()
+    for j in range(chunks):
+        done = latent_grad(index, parts[j], query_weight, j, chunks, done)
+    latent_out, grad_latents = done
+    return (latent_out, grad_latents, grad_query_weight, grad_tokens)
+
+
 def on_device(tokens, latents, cotangent, query_weight, keyvalue_weight, counts):
     narrow_size = lax.axis_size("narrow")
     narrow_index = lax.axis_index("narrow")
@@ -195,8 +645,9 @@
         P(),
         P(("groups", "blk"), None),
     )
+    one_head_each = mesh.shape["blk"] == 4 and mesh.shape["narrow"] == 4
     return jax.shard_map(
-        on_device,
+        by_head if one_head_each else on_device,
         mesh=mesh,
         in_specs=placed,
         out_specs=(

time: 776 us -> 157 us (0.20)
  waiting for transfers between devices: 381 us -> 55.9 us
  blocking collectives: 134 us -> 0 us
  matrix products: 105 us -> 0 us
  Pallas kernels: 0 us -> 64.2 us
  local copies, waits for them, and re-layouts: 70.6 us -> 7.96 us
  other arithmetic: 49.2 us -> 2.07 us
  between operations: 14.1 us -> 0.76 us
    ppermute x32 -> x21, waiting for transfers between devices: 232 us -> 49.9 us  [swapped(): lax.ppermute(shard, axis, [(i, i ^ bit) for i in range(lax.axis_size(axis...]
    all_gather x1 -> x0, waiting for transfers between devices: 120 us -> none  [merged_2(): everything = jax.tree.map(lambda part: lax.all_gather(part, axis), shard)]
    dot_general x33 -> x0, matrix products: 105 us -> none  [the longest x4 19.9 us: attend_forward(): jnp.einsum('hqk,khd->qhd', powers.astype(jnp.bfloat16), value_heads, pref...]
    psum x2 -> x0, blocking collectives: 102 us -> none  [the longest x1 76.5 us: on_device(): grad_latents = lax.psum(latent_term, 'narrow').astype(jnp.bfloat16)]
    pallas_call x0 -> x9, Pallas kernels: none -> 64.2 us  [the longest x1 17.4 us: attention(): pl.pallas_call(functools.partial(later_kernel, valid=valid, tile=tile, la...]
    all_gather x2 -> x0, blocking collectives: 31.9 us -> none  [merged_2(): everything = jax.tree.map(lambda part: lax.all_gather(part, axis), shard)]
    reduce_scatter x1 -> x0, waiting for transfers between devices: 30 us -> none  [on_device(): lax.psum_scatter(query_grad, 'narrow', scatter_dimension=1, tiled=True)]
    add x16 -> x0, other arithmetic: 27.3 us -> none  [the longest x4 13 us: backward_cycle_step(): query_grad + query_term]
  transfers between devices with their start and end apart: 34 -> 23, of which waited for: 18 -> 12; matrix products, arithmetic and copies ran while one was open for 8% -> 3% of each run, Pallas kernels for 0% -> 35%
where the time goes in v2:
time: 157 us; the launch traced here: 156 us
  Pallas kernels  64.2 us (41%)
  waiting for transfers between devices  55.9 us (36%)
  starting transfers between devices  25.3 us (16%)
  local copies, waits for them, and re-layouts  7.96 us (5%)
  other arithmetic  2.07 us (1%)
    ppermute x21, waiting for transfers between devices, swapped(): lax.ppermute(shard, axis, [(i, i ^ bit) for i in range(lax.axis_size(axis...  49.9 us
    pallas_call x1, Pallas kernels, attention(): pl.pallas_call(functools.partial(later_kernel, valid=valid, tile=tile, la...  17.4 us
    pallas_call x1, Pallas kernels, attention(): pl.pallas_call(functools.partial(first_kernel, valid=valid, tile=tile), g...  17 us
    ppermute x21, starting transfers between devices, swapped(): lax.ppermute(shard, axis, [(i, i ^ bit) for i in range(lax.axis_size(axis...  14 us
    pallas_call x2, Pallas kernels, latent_grad(): pl.pallas_call(functools.partial(latent_grad_kernel, heads=heads, groups=...  8.57 us
    all_to_all x1, starting transfers between devices, by_head(): pairs = lax.all_to_all(pairs, everyone, 0, 0, tiled=True)  7.38 us
    all_to_all x1, waiting for transfers between devices, by_head(): pairs = lax.all_to_all(pairs, everyone, 0, 0, tiled=True)  6.03 us
    unnamed x30, local copies, waits for them, and re-layouts  5.76 us
  transfers between devices with their start and end apart: 23, of which 12 were waited for; matrix products, arithmetic and copies ran while one was open for 3% of the time, Pallas kernels for 35%

profile of v2, /device:TPU:0, one launch (start us, length us, event | category | flops | bytes accessed | tf_op | source)
XLA Modules:
  0.0 156.2 jit_solution(2825151434091063314)
XLA Ops:
  0.6 5.3 %project_pairs.1 = bf16[4,4,256,128]{3,2,1,0:T(8,128)(2,1)} custom-call(bf16[256,1024]{1,0:T(8,128)(2,1)} %tok_ref.1, bf16[1024,2048]{1,0:T(8,128)(2,1)} %value_w_ref.3, bf16[1024,2048]{1,0:T(8,128)(2,1)} %value_w_ref.3), custom_call_target="tpu_custom_call" | custom-call | tf_op jit(solution)/shard_map/project_pairs/pallas_call | solution.py:173
  5.9 7.4 %all-to-all-start = ((bf16[16,256,128]{2,1,0:T(8,128)(2,1)}), bf16[16,256,128]{2,1,0:T(8,128)(2,1)S(1)}, u32[]{:S(2)}, u32[]{:S(2)}) async-start(bf16[16,256,128]{2,1,0:T(8,128)(2,1)} %bitcast.34), calls=%async_computation | async-start | bytes 2097152 | tf_op jit(solution)/shard_map/all_to_all | solution.py:573
  13.9 4.3 %project_queries.1 = bf16[4,528,128]{2,1,0:T(8,128)(2,1)} custom-call(s32[2]{0:T(128)} %pad_add_fusion.index_ref, s32[4]{0:T(128)} %bitcast.46, bf16[512,1024]{1,0:T(8,128)(2,1)} %refs_0_, bf16[1024,1024]{1,0:T(8,128)(2,1)} %refs_4_.3, bf16[512,1024]{1,0:T(8,128)(2,1)} %grad_ref.1), custom_call_target="tpu_custom_call" | custom-call | tf_op jit(solution)/shard_map/project_queries/pallas_call | solution.py:214
  18.2 1.2 fusion
  19.9 1.6 %collective-permute-start.1 = (bf16[528,128]{1,0:T(8,128)(2,1)S(1)}, bf16[528,128]{1,0:T(8,128)(2,1)S(1)}, u32[]{:S(2)}, u32[]{:S(2)}) collective-permute-start(bf16[528,128]{1,0:T(8,128)(2,1)S(1)} %get-tuple-element.34), channel_id=1, source_target_pairs={{0,8},{4,12},{8,0},{12,4},{1,9},{5,13},{9,1},{13,5},{2,10},{6,14},... | collective-permute-start | bytes 405512 | tf_op jit(solution)/shard_map/ppermute | solution.py:547
  21.6 7.8 %collective-permute-done.1 = bf16[528,128]{1,0:T(8,128)(2,1)S(1)} collective-permute-done((bf16[528,128]{1,0:T(8,128)(2,1)S(1)}, bf16[528,128]{1,0:T(8,128)(2,1)S(1)}, u32[]{:S(2)}, u32[]{:S(2)}) %collective-permute-start.1) | collective-permute-done | bytes 135200 | tf_op jit(solution)/shard_map/ppermute | solution.py:547
  29.3 3.2 %collective-permute-done.2 = bf16[528,128]{1,0:T(8,128)(2,1)S(1)} collective-permute-done((bf16[528,128]{1,0:T(8,128)(2,1)S(1)}, bf16[528,128]{1,0:T(8,128)(2,1)S(1)}, u32[]{:S(2)}, u32[]{:S(2)}) %collective-permute-start.2) | collective-permute-done | bytes 135200 | tf_op jit(solution)/shard_map/ppermute | solution.py:547
  34.1 6.0 %all-to-all-done.kv_ref = bf16[16,256,128]{2,1,0:T(8,128)(2,1)S(1)} async-done(((bf16[16,256,128]{2,1,0:T(8,128)(2,1)}), bf16[16,256,128]{2,1,0:T(8,128)(2,1)S(1)}, u32[]{:S(2)}, u32[]{:S(2)}) %all-to-all-start) | async-done | bytes 1048608 | tf_op jit(solution)/shard_map/all_to_all | solution.py:573
  40.2 1.0 copy-done.5
  41.1 17.0 %attention_first.1 = (bf16[4,256,128]{2,1,0:T(8,128)(2,1)}, bf16[2560,128]{1,0:T(8,128)(2,1)}, bf16[128,2560]{1,0:T(8,128)(2,1)}, f32[2832,128]{1,0:T(8,128)}) custom-call(s32[4,4]{1,0:T(4,128)} %bitcast.44, s32[2]{0:T(128)} %pad_add_fusion.index_ref, bf16[16,256,128]{2,1,0:T(8,128)(2,1)} %copy-done.5, bf16[4,528,128]{2,1,0:T(8,128)(2,1)} %copy-done.7), custom_call_target="tpu_custom_call" | custom-call | flops 16106127360 | bytes 4349952 | tf_op jit(solution)/shard_map/attention_first/pallas_call | solution.py:387
  58.1 17.4 %attention_later.1 = (bf16[4,256,128]{2,1,0:T(8,128)(2,1)}, bf16[16,256,128]{2,1,0:T(8,128)(2,1)}) custom-call(s32[4,4]{1,0:T(4,128)} %bitcast.45, s32[2]{0:T(128)} %pad_add_fusion.index_ref, bf16[2560,128]{1,0:T(8,128)(2,1)} %get-tuple-element.21.kv, bf16[128,2560]{1,0:T(8,128)(2,1)} %get-tuple-element.22.kvt, f32[2832,128]{1,0:T(8,128)} %get-tuple-element.23.acc_ref, ...), custom_call_target="tpu_custom_call" | custom-call | flops 16106127360 | bytes 4349952 | tf_op jit(solution)/shard_map/attention_later/pallas_call | solution.py:402
  75.5 4.0 %all-to-all-start.1 = ((bf16[16,256,128]{2,1,0:T(8,128)(2,1)}), bf16[16,256,128]{2,1,0:T(8,128)(2,1)S(1)}, u32[]{:S(2)}, u32[]{:S(2)}) async-start(bf16[16,256,128]{2,1,0:T(8,128)(2,1)} %get-tuple-element.31), calls=%async_computation.1 | async-start | bytes 2097152 | tf_op jit(solution)/shard_map/all_to_all | solution.py:581
  80.3 1.7 %collective-permute-start.10 = (bf16[256,128]{1,0:T(8,128)(2,1)S(1)}, bf16[256,128]{1,0:T(8,128)(2,1)S(1)}, u32[]{:S(2)}, u32[]{:S(2)}) collective-permute-start(bf16[256,128]{1,0:T(8,128)(2,1)S(1)} %get-tuple-element.38), channel_id=1, source_target_pairs={{0,8},{4,12},{8,0},{12,4},{1,9},{5,13},{9,1},{13,5},{2,10},{6,14},... | collective-permute-start | bytes 196616 | tf_op jit(solution)/shard_map/ppermute | solution.py:547
  82.0 1.0 fusion.2
  84.0 9.1 %collective-permute-done.10 = bf16[256,128]{1,0:T(8,128)(2,1)S(1)} collective-permute-done((bf16[256,128]{1,0:T(8,128)(2,1)S(1)}, bf16[256,128]{1,0:T(8,128)(2,1)S(1)}, u32[]{:S(2)}, u32[]{:S(2)}) %collective-permute-start.10) | collective-permute-done | bytes 65568 | tf_op jit(solution)/shard_map/ppermute | solution.py:547
  93.1 1.2 collective-permute-done.11
  94.2 1.3 collective-permute-start.5
  95.6 2.1 %collective-permute-done.4 = bf16[256,128]{1,0:T(8,128)(2,1)S(1)} collective-permute-done((bf16[256,128]{1,0:T(8,128)(2,1)S(1)}, bf16[256,128]{1,0:T(8,128)(2,1)S(1)}, u32[]{:S(2)}, u32[]{:S(2)}) %collective-permute-start.4) | collective-permute-done | bytes 65568 | tf_op jit(solution)/shard_map/ppermute | solution.py:547
  99.5 1.0 copy-done.3
  100.5 3.9 %weight_grad.1.refs_0_ = bf16[64,1024]{1,0:T(8,128)(2,1)} custom-call(bf16[512,1024]{1,0:T(8,128)(2,1)} %refs_0_, bf16[512,1024]{1,0:T(8,128)(2,1)} %copy-done.3, bf16[512,1024]{1,0:T(8,128)(2,1)} %copy-done.2, bf16[512,1024]{1,0:T(8,128)(2,1)} %collective-permute-done.17.refs_3_, bf16[4,256,128]{2,1,0:T(8,128)(2,1)} %get-tuple-element.25.refs_4_, ...), custom_call_target="tpu_custom_call" | custom-call | tf_op jit(solution)/shard_map/weight_grad/pallas_call | solution.py:513
  104.3 1.6 %collective-permute-start.19 = (bf16[64,1024]{1,0:T(8,128)(2,1)}, bf16[64,1024]{1,0:T(8,128)(2,1)S(1)}, u32[]{:S(2)}, u32[]{:S(2)}) collective-permute-start(bf16[64,1024]{1,0:T(8,128)(2,1)} %weight_grad.1.refs_0_), channel_id=1, source_target_pairs={{0,8},{4,12},{8,0},{12,4},{1,9},{5,13},{9,1},{13,5},{2,10},{6,14},... | collective-permute-start | bytes 393224 | tf_op jit(solution)/shard_map/ppermute | solution.py:547
  105.9 2.8 %collective-permute-start.12 = (bf16[4,256,128]{2,1,0:T(8,128)(2,1)S(1)}, bf16[4,256,128]{2,1,0:T(8,128)(2,1)S(1)}, u32[]{:S(2)}, u32[]{:S(2)}) collective-permute-start(bf16[4,256,128]{2,1,0:T(8,128)(2,1)S(1)} %pad_maximum_fusion.2.refs_0_), channel_id=1, source_target_pairs={{0,1},{1,0},{2,3},{3,2},{4,5},{5,4},{6,7},{7,6},{8,9},{9,8},{10,11... | collective-permute-start | bytes 786440 | tf_op jit(solution)/shard_map/ppermute | solution.py:547
  108.7 14.6 %collective-permute-done.13.refs_2_ = bf16[4,256,128]{2,1,0:T(8,128)(2,1)} collective-permute-done((bf16[4,256,128]{2,1,0:T(8,128)(2,1)S(1)}, bf16[4,256,128]{2,1,0:T(8,128)(2,1)}, u32[]{:S(2)}, u32[]{:S(2)}) %collective-permute-start.13) | collective-permute-done | bytes 262176 | tf_op jit(solution)/shard_map/ppermute | solution.py:547
  123.3 5.1 %collective-permute-done.7.refs_2_ = bf16[4,256,128]{2,1,0:T(8,128)(2,1)} collective-permute-done((bf16[4,256,128]{2,1,0:T(8,128)(2,1)}, bf16[4,256,128]{2,1,0:T(8,128)(2,1)}, u32[]{:S(2)}, u32[]{:S(2)}) %collective-permute-start.7) | collective-permute-done | bytes 262176 | tf_op jit(solution)/shard_map/ppermute | solution.py:547
  128.4 2.0 %collective-permute-start.8 = (bf16[4,256,128]{2,1,0:T(8,128)(2,1)}, bf16[4,256,128]{2,1,0:T(8,128)(2,1)S(1)}, u32[]{:S(2)}, u32[]{:S(2)}) collective-permute-start(bf16[4,256,128]{2,1,0:T(8,128)(2,1)} %collective-permute-done.7.refs_2_), channel_id=1, source_target_pairs={{0,1},{1,0},{2,3},{3,2},{4,5},{5,4},{6,7},{7,6},{8,9},{9,8},{10,11... | collective-permute-start | bytes 786440 | tf_op jit(solution)/shard_map/ppermute | solution.py:547
  130.4 1.3 collective-permute-done.20.refs_3_
  132.4 2.8 %turn.1 = bf16[1024,256]{1,0:T(8,128)(2,1)} custom-call(s32[2]{0:T(128)} %pad_add_fusion.index_ref, bf16[64,1024]{1,0:T(8,128)(2,1)} %weight_grad.1.refs_0_, bf16[64,1024]{1,0:T(8,128)(2,1)} %copy-done.13, bf16[64,1024]{1,0:T(8,128)(2,1)} %copy-done.12, bf16[64,1024]{1,0:T(8,128)(2,1)} %copy-done.14), custom_call_target="tpu_custom_call" | custom-call | tf_op jit(solution)/shard_map/turn/pallas_call | solution.py:532
  136.7 4.3 %latent_grad.2 = (bf16[512,1024]{1,0:T(8,128)(2,1)}, bf16[512,1024]{1,0:T(8,128)(2,1)}) custom-call(s32[2]{0:T(128)} %pad_add_fusion.index_ref, bf16[4,256,128]{2,1,0:T(8,128)(2,1)} %copy-done.6, bf16[4,256,128]{2,1,0:T(8,128)(2,1)} %copy-done.8, bf16[4,256,128]{2,1,0:T(8,128)(2,1)} %collective-permute-done.13.refs_2_, bf16[4,256,128]{2,1,0:T(8,128)(2,1)} %copy-done.9, ...), custom_call_target="tpu_custom_call" | custom-call | tf_op jit(solution)/shard_map/latent_grad/pallas_call | solution.py:481
  141.0 4.2 %collective-permute-done.8.refs_3_ = bf16[4,256,128]{2,1,0:T(8,128)(2,1)S(1)} collective-permute-done((bf16[4,256,128]{2,1,0:T(8,128)(2,1)}, bf16[4,256,128]{2,1,0:T(8,128)(2,1)S(1)}, u32[]{:S(2)}, u32[]{:S(2)}) %collective-permute-start.8) | collective-permute-done | bytes 262176 | tf_op jit(solution)/shard_map/ppermute | solution.py:547
  145.9 4.3 %latent_grad.3 = (bf16[512,1024]{1,0:T(8,128)(2,1)}, bf16[512,1024]{1,0:T(8,128)(2,1)}) custom-call(s32[2]{0:T(128)} %pad_add_fusion.index_ref, bf16[4,256,128]{2,1,0:T(8,128)(2,1)} %pad_maximum_fusion.1.refs_0_, bf16[4,256,128]{2,1,0:T(8,128)(2,1)} %copy-done.10, ...), custom_call_target="tpu_custom_call", output_to_operand_aliasing={{0}: (6, {}), {1}: (7, {})} | custom-call | tf_op jit(solution)/shard_map/latent_grad/pallas_call | solution.py:481
  150.2 1.0 copy-done
  151.2 5.1 %token_grad.1 = bf16[256,1024]{1,0:T(8,128)(2,1)} custom-call(bf16[4,4,256,128]{3,2,1,0:T(8,128)(2,1)} %bitcast.33, bf16[1024,2048]{1,0:T(8,128)(2,1)} %value_w_ref.3, bf16[1024,2048]{1,0:T(8,128)(2,1)} %value_w_ref.3), custom_call_target="tpu_custom_call" | custom-call | tf_op jit(solution)/shard_map/token_grad/pallas_call | solution.py:445
  (61 shorter events, 9.2 us)
Async XLA Ops:
  5.9 34.2 %all-to-all-start = ((bf16[16,256,128]{2,1,0:T(8,128)(2,1)}), bf16[16,256,128]{2,1,0:T(8,128)(2,1)S(1)}, u32[]{:S(2)}, u32[]{:S(2)}) async-start(bf16[16,256,128]{2,1,0:T(8,128)(2,1)} %bitcast.34), calls=%async_computation | async-start | bytes 2097152 | tf_op jit(solution)/shard_map/all_to_all | solution.py:573
  18.2 14.4 %copy-start.1 = (bf16[512,1024]{1,0:T(8,128)(2,1)S(1)}, bf16[512,1024]{1,0:T(8,128)(2,1)}, u32[]{:S(2)}) copy-start(bf16[512,1024]{1,0:T(8,128)(2,1)} %refs_0_) | copy-start | bytes 3145732
  19.4 2.1 %collective-permute-start = (bf16[528,128]{1,0:T(8,128)(2,1)S(1)}, bf16[528,128]{1,0:T(8,128)(2,1)S(1)}, u32[]{:S(2)}, u32[]{:S(2)}) collective-permute-start(bf16[528,128]{1,0:T(8,128)(2,1)S(1)} %get-tuple-element.35), channel_id=1, source_target_pairs={{0,4},{4,0},{8,12},{12,8},{1,5},{5,1},{9,13},{13,9},{2,6},{6,2},{1... | collective-permute-start | bytes 405512 | tf_op jit(solution)/shard_map/ppermute | solution.py:547
  19.9 9.4 %collective-permute-start.1 = (bf16[528,128]{1,0:T(8,128)(2,1)S(1)}, bf16[528,128]{1,0:T(8,128)(2,1)S(1)}, u32[]{:S(2)}, u32[]{:S(2)}) collective-permute-start(bf16[528,128]{1,0:T(8,128)(2,1)S(1)} %get-tuple-element.34), channel_id=1, source_target_pairs={{0,8},{4,12},{8,0},{12,4},{1,9},{5,13},{9,1},{13,5},{2,10},{6,14},... | collective-permute-start | bytes 405512 | tf_op jit(solution)/shard_map/ppermute | solution.py:547
  21.5 11.0 %collective-permute-start.2 = (bf16[528,128]{1,0:T(8,128)(2,1)S(1)}, bf16[528,128]{1,0:T(8,128)(2,1)S(1)}, u32[]{:S(2)}, u32[]{:S(2)}) collective-permute-start(bf16[528,128]{1,0:T(8,128)(2,1)S(1)} %get-tuple-element.33), channel_id=1, source_target_pairs={{0,12},{4,8},{8,4},{12,0},{1,13},{5,9},{9,5},{13,1},{2,14},{6,10},... | collective-permute-start | bytes 405512 | tf_op jit(solution)/shard_map/ppermute | solution.py:547
  32.6 47.0 %collective-permute-start.16 = (bf16[512,1024]{1,0:T(8,128)(2,1)S(1)}, bf16[512,1024]{1,0:T(8,128)(2,1)S(1)}, u32[]{:S(2)}, u32[]{:S(2)}) collective-permute-start(bf16[512,1024]{1,0:T(8,128)(2,1)S(1)} %copy-done.1), channel_id=1, source_target_pairs={{0,8},{4,12},{8,0},{12,4},{1,9},{5,13},{9,1},{13,5},{2,10},{6,14},... | collective-permute-start | bytes 3145736 | tf_op jit(solution)/shard_map/ppermute | solution.py:547
  75.5 4.6 %copy-start.4 = (bf16[4,256,128]{2,1,0:T(8,128)(2,1)S(1)}, bf16[4,256,128]{2,1,0:T(8,128)(2,1)}, u32[]{:S(2)}) copy-start(bf16[4,256,128]{2,1,0:T(8,128)(2,1)} %get-tuple-element.25.refs_4_) | copy-start | bytes 786436
  75.5 74.7 %all-to-all-start.1 = ((bf16[16,256,128]{2,1,0:T(8,128)(2,1)}), bf16[16,256,128]{2,1,0:T(8,128)(2,1)S(1)}, u32[]{:S(2)}, u32[]{:S(2)}) async-start(bf16[16,256,128]{2,1,0:T(8,128)(2,1)} %get-tuple-element.31), calls=%async_computation.1 | async-start | bytes 2097152 | tf_op jit(solution)/shard_map/all_to_all | solution.py:581
  79.5 20.0 %collective-permute-start.15 = (bf16[512,1024]{1,0:T(8,128)(2,1)S(1)}, bf16[512,1024]{1,0:T(8,128)(2,1)S(1)}, u32[]{:S(2)}, u32[]{:S(2)}) collective-permute-start(bf16[512,1024]{1,0:T(8,128)(2,1)S(1)} %copy-done.1), channel_id=1, source_target_pairs={{0,4},{4,0},{8,12},{12,8},{1,5},{5,1},{9,13},{13,9},{2,6},{6,2},{1... | collective-permute-start | bytes 3145736 | tf_op jit(solution)/shard_map/ppermute | solution.py:547
  79.7 20.8 %copy-start.2 = (bf16[512,1024]{1,0:T(8,128)(2,1)}, bf16[512,1024]{1,0:T(8,128)(2,1)S(1)}, u32[]{:S(2)}) copy-start(bf16[512,1024]{1,0:T(8,128)(2,1)S(1)} %collective-permute-done.16.refs_2_) | copy-start | bytes 3145732
  79.7 20.8 %collective-permute-start.17 = (bf16[512,1024]{1,0:T(8,128)(2,1)S(1)}, bf16[512,1024]{1,0:T(8,128)(2,1)}, u32[]{:S(2)}, u32[]{:S(2)}) collective-permute-start(bf16[512,1024]{1,0:T(8,128)(2,1)S(1)} %collective-permute-done.16.refs_2_), channel_id=1, source_target_pairs={{0,4},{4,0},{8,12},{12,8},{1,5},{5,1},{9,13},{13,9},{2,6},{6,2},{1... | collective-permute-start | bytes 3145736 | tf_op jit(solution)/shard_map/ppermute | solution.py:547
  80.1 3.8 %collective-permute-start.9 = (bf16[256,128]{1,0:T(8,128)(2,1)S(1)}, bf16[256,128]{1,0:T(8,128)(2,1)S(1)}, u32[]{:S(2)}, u32[]{:S(2)}) collective-permute-start(bf16[256,128]{1,0:T(8,128)(2,1)S(1)} %get-tuple-element.39), channel_id=1, source_target_pairs={{0,4},{4,0},{8,12},{12,8},{1,5},{5,1},{9,13},{13,9},{2,6},{6,2},{1... | collective-permute-start | bytes 196616 | tf_op jit(solution)/shard_map/ppermute | solution.py:547
  80.3 12.8 %collective-permute-start.10 = (bf16[256,128]{1,0:T(8,128)(2,1)S(1)}, bf16[256,128]{1,0:T(8,128)(2,1)S(1)}, u32[]{:S(2)}, u32[]{:S(2)}) collective-permute-start(bf16[256,128]{1,0:T(8,128)(2,1)S(1)} %get-tuple-element.38), channel_id=1, source_target_pairs={{0,8},{4,12},{8,0},{12,4},{1,9},{5,13},{9,1},{13,5},{2,10},{6,14},... | collective-permute-start | bytes 196616 | tf_op jit(solution)/shard_map/ppermute | solution.py:547
  81.9 12.3 %collective-permute-start.11 = (bf16[256,128]{1,0:T(8,128)(2,1)S(1)}, bf16[256,128]{1,0:T(8,128)(2,1)S(1)}, u32[]{:S(2)}, u32[]{:S(2)}) collective-permute-start(bf16[256,128]{1,0:T(8,128)(2,1)S(1)} %get-tuple-element.37), channel_id=1, source_target_pairs={{0,12},{4,8},{8,4},{12,0},{1,13},{5,9},{9,5},{13,1},{2,14},{6,10},... | collective-permute-start | bytes 196616 | tf_op jit(solution)/shard_map/ppermute | solution.py:547
  83.8 11.7 %collective-permute-start.3 = (bf16[256,128]{1,0:T(8,128)(2,1)S(1)}, bf16[256,128]{1,0:T(8,128)(2,1)S(1)}, u32[]{:S(2)}, u32[]{:S(2)}) collective-permute-start(bf16[256,128]{1,0:T(8,128)(2,1)S(1)} %get-tuple-element.43), channel_id=1, source_target_pairs={{0,4},{4,0},{8,12},{12,8},{1,5},{5,1},{9,13},{13,9},{2,6},{6,2},{1... | collective-permute-start | bytes 196616 | tf_op jit(solution)/shard_map/ppermute | solution.py:547
  93.1 4.6 %collective-permute-start.4 = (bf16[256,128]{1,0:T(8,128)(2,1)S(1)}, bf16[256,128]{1,0:T(8,128)(2,1)S(1)}, u32[]{:S(2)}, u32[]{:S(2)}) collective-permute-start(bf16[256,128]{1,0:T(8,128)(2,1)S(1)} %get-tuple-element.42), channel_id=1, source_target_pairs={{0,8},{4,12},{8,0},{12,4},{1,9},{5,13},{9,1},{13,5},{2,10},{6,14},... | collective-permute-start | bytes 196616 | tf_op jit(solution)/shard_map/ppermute | solution.py:547
  94.2 3.9 %collective-permute-start.5 = (bf16[256,128]{1,0:T(8,128)(2,1)S(1)}, bf16[256,128]{1,0:T(8,128)(2,1)S(1)}, u32[]{:S(2)}, u32[]{:S(2)}) collective-permute-start(bf16[256,128]{1,0:T(8,128)(2,1)S(1)} %get-tuple-element.41), channel_id=1, source_target_pairs={{0,12},{4,8},{8,4},{12,0},{1,13},{5,9},{9,5},{13,1},{2,14},{6,10},... | collective-permute-start | bytes 196616 | tf_op jit(solution)/shard_map/ppermute | solution.py:547
  95.5 10.4 %copy-start.6 = (bf16[4,256,128]{2,1,0:T(8,128)(2,1)}, bf16[4,256,128]{2,1,0:T(8,128)(2,1)S(1)}, u32[]{:S(2)}) copy-start(bf16[4,256,128]{2,1,0:T(8,128)(2,1)S(1)} %pad_maximum_fusion.2.refs_0_) | copy-start | bytes 786436
  95.6 27.8 %collective-permute-start.13 = (bf16[4,256,128]{2,1,0:T(8,128)(2,1)S(1)}, bf16[4,256,128]{2,1,0:T(8,128)(2,1)}, u32[]{:S(2)}, u32[]{:S(2)}) collective-permute-start(bf16[4,256,128]{2,1,0:T(8,128)(2,1)S(1)} %pad_maximum_fusion.2.refs_0_), channel_id=1, source_target_pairs={{0,2},{1,3},{2,0},{3,1},{4,6},{5,7},{6,4},{7,5},{8,10},{9,11},{10,... | collective-permute-start | bytes 786440 | tf_op jit(solution)/shard_map/ppermute | solution.py:547
  98.9 29.5 %collective-permute-start.7 = (bf16[4,256,128]{2,1,0:T(8,128)(2,1)}, bf16[4,256,128]{2,1,0:T(8,128)(2,1)}, u32[]{:S(2)}, u32[]{:S(2)}) collective-permute-start(bf16[4,256,128]{2,1,0:T(8,128)(2,1)} %pad_maximum_fusion.1.refs_0_), channel_id=1, source_target_pairs={{0,2},{1,3},{2,0},{3,1},{4,6},{5,7},{6,4},{7,5},{8,10},{9,11},{10,... | collective-permute-start | bytes 786440 | tf_op jit(solution)/shard_map/ppermute | solution.py:547
  99.5 1.0 copy-start.3
  104.3 24.1 %collective-permute-start.19 = (bf16[64,1024]{1,0:T(8,128)(2,1)}, bf16[64,1024]{1,0:T(8,128)(2,1)S(1)}, u32[]{:S(2)}, u32[]{:S(2)}) collective-permute-start(bf16[64,1024]{1,0:T(8,128)(2,1)} %weight_grad.1.refs_0_), channel_id=1, source_target_pairs={{0,8},{4,12},{8,0},{12,4},{1,9},{5,13},{9,1},{13,5},{2,10},{6,14},... | collective-permute-start | bytes 393224 | tf_op jit(solution)/shard_map/ppermute | solution.py:547
  105.9 24.5 %collective-permute-start.18 = (bf16[64,1024]{1,0:T(8,128)(2,1)}, bf16[64,1024]{1,0:T(8,128)(2,1)S(1)}, u32[]{:S(2)}, u32[]{:S(2)}) collective-permute-start(bf16[64,1024]{1,0:T(8,128)(2,1)} %weight_grad.1.refs_0_), channel_id=1, source_target_pairs={{0,4},{4,0},{8,12},{12,8},{1,5},{5,1},{9,13},{13,9},{2,6},{6,2},{1... | collective-permute-start | bytes 393224 | tf_op jit(solution)/shard_map/ppermute | solution.py:547
  105.9 29.3 %collective-permute-start.12 = (bf16[4,256,128]{2,1,0:T(8,128)(2,1)S(1)}, bf16[4,256,128]{2,1,0:T(8,128)(2,1)S(1)}, u32[]{:S(2)}, u32[]{:S(2)}) collective-permute-start(bf16[4,256,128]{2,1,0:T(8,128)(2,1)S(1)} %pad_maximum_fusion.2.refs_0_), channel_id=1, source_target_pairs={{0,1},{1,0},{2,3},{3,2},{4,5},{5,4},{6,7},{7,6},{8,9},{9,8},{10,11... | collective-permute-start | bytes 786440 | tf_op jit(solution)/shard_map/ppermute | solution.py:547
  123.3 12.0 %collective-permute-start.14 = (bf16[4,256,128]{2,1,0:T(8,128)(2,1)}, bf16[4,256,128]{2,1,0:T(8,128)(2,1)S(1)}, u32[]{:S(2)}, u32[]{:S(2)}) collective-permute-start(bf16[4,256,128]{2,1,0:T(8,128)(2,1)} %collective-permute-done.13.refs_2_), channel_id=1, source_target_pairs={{0,1},{1,0},{2,3},{3,2},{4,5},{5,4},{6,7},{7,6},{8,9},{9,8},{10,11... | collective-permute-start | bytes 786440 | tf_op jit(solution)/shard_map/ppermute | solution.py:547
  128.4 12.6 %collective-permute-start.6 = (bf16[4,256,128]{2,1,0:T(8,128)(2,1)}, bf16[4,256,128]{2,1,0:T(8,128)(2,1)S(1)}, u32[]{:S(2)}, u32[]{:S(2)}) collective-permute-start(bf16[4,256,128]{2,1,0:T(8,128)(2,1)} %pad_maximum_fusion.1.refs_0_), channel_id=1, source_target_pairs={{0,1},{1,0},{2,3},{3,2},{4,5},{5,4},{6,7},{7,6},{8,9},{9,8},{10,11... | collective-permute-start | bytes 786440 | tf_op jit(solution)/shard_map/ppermute | solution.py:547
  128.4 3.4 %copy-start.12 = (bf16[64,1024]{1,0:T(8,128)(2,1)}, bf16[64,1024]{1,0:T(8,128)(2,1)S(1)}, u32[]{:S(2)}) copy-start(bf16[64,1024]{1,0:T(8,128)(2,1)S(1)} %collective-permute-done.19.refs_2_) | copy-start | bytes 393220
  128.4 16.8 %collective-permute-start.8 = (bf16[4,256,128]{2,1,0:T(8,128)(2,1)}, bf16[4,256,128]{2,1,0:T(8,128)(2,1)S(1)}, u32[]{:S(2)}, u32[]{:S(2)}) collective-permute-start(bf16[4,256,128]{2,1,0:T(8,128)(2,1)} %collective-permute-done.7.refs_2_), channel_id=1, source_target_pairs={{0,1},{1,0},{2,3},{3,2},{4,5},{5,4},{6,7},{7,6},{8,9},{9,8},{10,11... | collective-permute-start | bytes 786440 | tf_op jit(solution)/shard_map/ppermute | solution.py:547
  130.4 1.4 copy-start.13
  130.4 1.3 collective-permute-start.20
  141.0 4.2 %copy-start.10 = (bf16[4,256,128]{2,1,0:T(8,128)(2,1)}, bf16[4,256,128]{2,1,0:T(8,128)(2,1)S(1)}, u32[]{:S(2)}) copy-start(bf16[4,256,128]{2,1,0:T(8,128)(2,1)S(1)} %collective-permute-done.6.refs_1_) | copy-start | bytes 786436
  150.2 1.0 copy-start
  (6 other events, 4.7 us)

commit v3 on v2

--- a/solution.py
+++ b/solution.py
@@ -238,187 +238,249 @@
 def pack_tokens(counts_ref, index_ref, kv_ref, wide, kv, kvt, valid, tile):
     sources, slot, width = kv_ref.shape
     padded = kv.shape[0]
-    row8 = lax.broadcasted_iota(jnp.int32, (8, width), 0)
-    at = jnp.int32(0)
+    at = 0
     for s in range(sources):
-        offset = at % 8
-        base = pl.multiple_of(at - offset, 8)
-        rows = kv_ref[s].astype(jnp.float32)
-        rows = jnp.concatenate([rows, jnp.zeros((8, width), jnp.float32)], axis=0)
-        rows = pltpu.roll(rows, offset, 0)
-        earlier = wide[pl.ds(base, 8), :]
-        wide[pl.ds(base, 8), :] = jnp.where(row8 < offset, earlier, rows[:8])
-        wide[pl.ds(base + 8, slot), :] = rows[8:]
+        wide[pl.ds(at, slot), :] = kv_ref[s].astype(jnp.float32)
         at = at + count_of(counts_ref, index_ref, s)
     for t in range(0, padded, tile):
         size = min(tile, padded - t)
         part = wide[t:t + size, :]
         if t + size > valid:
             part = jnp.where(
-                lax.broadcasted_iota(jnp.int32, (size, width), 0) < valid - t, part, 0.0
+                lax.broadcasted_iota(jnp.int32, (size, width), 0) < valid - t, part, wide[:1, :]
             )
         kv[t:t + size, :] = part.astype(jnp.bfloat16)
         kvt[:, t:t + size] = part.T.astype(jnp.bfloat16)
 
 
-def unpack_tokens(counts_ref, index_ref, acc, dkv_ref):
+def unpack_tokens(counts_ref, index_ref, acc, wide, dkv_ref, tile):
     sources, slot, width = dkv_ref.shape
+    padded = acc.shape[1]
     scale = jnp.where(
-        lax.broadcasted_iota(jnp.int32, (slot, width), 1) < HEAD, HEAD ** (-0.5), 1.0
-    )
+        lax.broadcasted_iota(jnp.int32, (tile, width), 1) < HEAD, HEAD ** (-0.5), 1.0
+    )
+    for t in range(0, padded, tile):
+        size = min(tile, padded - t)
+        wide[t:t + size, :] = acc[:, t:t + size].T * scale[:size]
     row = lax.broadcasted_iota(jnp.int32, (slot, width), 0)
-    at = jnp.int32(0)
+    at = 0
     for s in range(sources):
         count = count_of(counts_ref, index_ref, s)
-        offset = at % 8
-        base = pl.multiple_of(at - offset, 8)
-        rows = pltpu.roll(acc[pl.ds(base, slot + 8), :], (slot + 8 - offset) % (slot + 8), 0)
-        dkv_ref[s] = jnp.where(row < count, rows[:slot] * scale, 0.0).astype(jnp.bfloat16)
+        rows = wide[pl.ds(at, slot), :]
+        dkv_ref[s] = jnp.where(row < count, rows, 0.0).astype(jnp.bfloat16)
         at = at + count
 
 
-def attend_block(qg, kv, kvt, scores, acc, valid, tile):
-    block, width = qg.shape
+class Block:
+    def __init__(self, qg, slot, kv, kvt, acc, scores, dprobs, sums, valid):
+        self.slot, self.kv, self.kvt, self.acc, self.valid = slot, kv, kvt, acc, valid
+        self.scores, self.dprobs, self.sums = scores.at[slot], dprobs.at[slot], sums.at[slot]
+        self.count, width = qg.shape
+        lane = lax.broadcasted_iota(jnp.int32, (self.count, width), 1)
+        zero = jnp.zeros_like(qg)
+        self.query = jnp.where(lane < HEAD, qg, zero)
+        self.grad = jnp.where(lane < HEAD, zero, qg)
+        turned = qg.astype(jnp.float32).T
+        self.grad_wide = turned[HEAD:, :]
+        self.query_t = turned[:HEAD, :].astype(jnp.bfloat16)
+        self.grad_t = turned[HEAD:, :].astype(jnp.bfloat16)
+
+    def fold(self, part, op):
+        return op(part.reshape(part.shape[0] // 8, 8, self.count), axis=0)
+
+    def score(self, rows, highest):
+        part = mm(self.kv[rows, :], self.query, NT)
+        self.scores[rows, :] = part
+        self.dprobs[rows, :] = mm(self.kv[rows, :], self.grad, NT)
+        return jnp.maximum(highest, self.fold(part, jnp.max))
+
+    def scored(self, highest):
+        padded = self.kv.shape[0]
+        self.top = jnp.max(highest, axis=0, keepdims=True)
+        self.scores[self.valid:, :] = jnp.full((padded - self.valid, self.count), NEG, jnp.float32)
+        self.sums[...] = jnp.zeros(self.sums.shape, jnp.float32)
+
+    def attend(self, rows, total):
+        power = jnp.exp2((self.scores[rows, :] - self.top) * (HEAD ** (-0.5) * LOG2E))
+        self.scores[rows, :] = power
+        self.sums[:HEAD, :] += mm(self.kvt[HEAD:, rows], power.astype(jnp.bfloat16))
+        return total + self.fold(power, jnp.sum)
+
+    def attended(self, total):
+        self.inverse = 1.0 / jnp.sum(total, axis=0, keepdims=True)
+        self.out = self.sums[:HEAD, :] * self.inverse
+        self.delta = jnp.sum(self.grad_wide * self.out, axis=0, keepdims=True)
+
+    def back(self, rows, unused):
+        prob = self.scores[rows, :] * self.inverse
+        dscore = (prob * (self.dprobs[rows, :] - self.delta)).astype(jnp.bfloat16)
+        self.acc[:HEAD, rows] += mm(self.query_t, dscore, NT)
+        self.acc[HEAD:, rows] += mm(self.grad_t, prob.astype(jnp.bfloat16), NT)
+        self.sums[HEAD:, :] += mm(self.kvt[:HEAD, rows], dscore)
+        return unused
+
+    def ended(self, unused):
+        both = jnp.concatenate([self.out, self.sums[HEAD:, :] * HEAD ** (-0.5)], axis=0)
+        self.both = both.T.astype(jnp.bfloat16)
+
+
+def attend_blocks(qgs, scores, dprobs, sums, kv, kvt, acc, valid, tile):
+    count = len(qgs)
     padded = kv.shape[0]
-    factor = HEAD ** (-0.5)
-    lane = lax.broadcasted_iota(jnp.int32, (block, width), 1)
-    zero = jnp.zeros_like(qg)
-    query = jnp.where(lane < HEAD, qg, zero)
-    grad = jnp.where(lane < HEAD, zero, qg)
-    grad_t = qg.astype(jnp.float32).T[HEAD:, :]
-    tiles = [(t, min(tile, padded - t)) for t in range(0, padded, tile)]
-    highest = jnp.full((8, block), NEG, jnp.float32)
-    for t, size in tiles:
-        part = mm(kv[t:t + size, :], query, NT)
-        if t + size > valid:
-            part = jnp.where(
-                lax.broadcasted_iota(jnp.int32, (size, block), 0) < valid - t, part, NEG
+    blocks = []
+    for step in range(count + 2):
+        if step < count:
+            blocks.append(
+                Block(qgs[step], step % 3, kv, kvt, acc, scores, dprobs, sums, valid)
             )
-        scores[t:t + size, :] = part
-        highest = jnp.maximum(highest, jnp.max(part.reshape(size // 8, 8, block), axis=0))
-    top = jnp.max(highest, axis=0, keepdims=True)
-    total = jnp.zeros((8, block), jnp.float32)
-    out_t = jnp.zeros((HEAD, block), jnp.float32)
-    for t, size in tiles:
-        power = jnp.exp2((scores[t:t + size, :] - top) * (factor * LOG2E))
-        scores[t:t + size, :] = power
-        total = total + jnp.sum(power.reshape(size // 8, 8, block), axis=0)
-        out_t = out_t + mm(kvt[HEAD:, t:t + size], power.astype(jnp.bfloat16))
-    inverse = 1.0 / jnp.sum(total, axis=0, keepdims=True)
-    out_t = out_t * inverse
-    delta = jnp.sum(grad_t * out_t, axis=0, keepdims=True)
-    query_t = jnp.zeros((HEAD, block), jnp.float32)
-    for t, size in tiles:
-        dprob = mm(kv[t:t + size, :], grad, NT)
-        prob = scores[t:t + size, :] * inverse
-        dscore = (prob * (dprob - delta)).astype(jnp.bfloat16)
-        acc[t:t + size, :] += mm(dscore, query) + mm(prob.astype(jnp.bfloat16), grad)
-        query_t = query_t + mm(kvt[:HEAD, t:t + size], dscore)
-    both = jnp.concatenate([out_t, query_t * factor], axis=0)
-    return both.T.astype(jnp.bfloat16)
+        work = []
+        if 0 <= step - 2 < count:
+            work.append((blocks[step - 2].back, blocks[step - 2].ended, 0.0))
+        if 0 <= step - 1 < count:
+            work.append((blocks[step - 1].attend, blocks[step - 1].attended, 0.0))
+        if step < count:
+            work.append((blocks[step].score, blocks[step].scored, NEG))
+
+        def body(k, carried, work=work):
+            rows = pl.ds(pl.multiple_of(k * tile, tile), tile)
+            return tuple(one[0](rows, held) for one, held in zip(work, carried))
+
+        found = lax.fori_loop(
+            0,
+            padded // tile,
+            body,
+            tuple(jnp.full((8, block_rows(qgs)), one[2], jnp.float32) for one in work),
+        )
+        for one, held in zip(work, found):
+            one[1](held)
+    return [block.both for block in blocks]
+
+
+def block_rows(qgs):
+    return qgs[0].shape[0]
 
 
 def first_kernel(
-    counts_ref, index_ref, kv_ref, qg_ref, og_ref, kv, kvt, acc, wide, scores, *, valid, tile
+    counts_ref, index_ref, kv_ref, qg_ref, *refs, valid, tile
 ):
+    pair = qg_ref.shape[0]
+    outs, (kv, kvt, acc, wide, scores, dprobs, sums) = refs[:-7], refs[-7:]
+
     @pl.when(pl.program_id(0) == 0)
     def _():
         pack_tokens(counts_ref, index_ref, kv_ref, wide, kv, kvt, valid, tile)
         acc[...] = jnp.zeros(acc.shape, jnp.float32)
 
-    og_ref[0] = attend_block(qg_ref[0], kv, kvt, scores, acc, valid, tile)
-
-
-def later_kernel(
-    counts_ref,
-    index_ref,
-    kv,
-    kvt,
-    acc_ref,
-    qg_ref,
-    og_ref,
-    out_ref,
-    acc,
-    scores,
-    *,
-    valid,
-    tile,
-    last,
-):
+    found = attend_blocks(
+        [qg_ref[k] for k in range(pair)], scores, dprobs, sums, kv, kvt, acc, valid, tile
+    )
+    for k in range(pair):
+        outs[0][k] = found[k]
+        outs[1 + k][...] = found[k]
+
+
+def later_kernel(counts_ref, index_ref, kv, kvt, acc_ref, qg_ref, *refs, valid, tile):
+    *outs, out_ref, acc, wide, scores, dprobs, sums = refs
+
     @pl.when(pl.program_id(0) == 0)
     def _():
         acc[...] = acc_ref[...]
 
-    og_ref[0] = attend_block(qg_ref[0], kv, kvt, scores, acc, valid, tile)
+    pair = qg_ref.shape[0]
+    found = attend_blocks(
+        [qg_ref[k] for k in range(pair)], scores, dprobs, sums, kv, kvt, acc, valid, tile
+    )
+    for k in range(pair):
+        outs[0][k] = found[k]
+        outs[1 + k][...] = found[k]
 
     @pl.when(pl.program_id(0) == pl.num_programs(0) - 1)
     def _():
-        if last:
-            unpack_tokens(counts_ref, index_ref, acc, out_ref)
-        else:
-            out_ref[...] = acc[...]
-
-
-def attention(counts, index, kv, qg, valid, latent_rows, chunks, tile=256):
+        unpack_tokens(counts_ref, index_ref, acc, wide, out_ref, tile)
+
+
+def attention_first(counts, index, kv, qg, valid, block, tile=1280):
     sources, slot, width = kv.shape
     blocks = qg.shape[0]
-    block = latent_rows // chunks
     padded = -(-valid // 128) * 128
     room = padded + slot + 16
-    packed = [
+    shapes = [
         jax.ShapeDtypeStruct((padded, width), jnp.bfloat16),
         jax.ShapeDtypeStruct((width, padded), jnp.bfloat16),
+        jax.ShapeDtypeStruct((width, padded), jnp.float32),
     ]
-    acc_shape = jax.ShapeDtypeStruct((room, width), jnp.float32)
-    og_shape = jax.ShapeDtypeStruct((blocks, block, width), jnp.bfloat16)
-    wide = pltpu.VMEM((room, width), jnp.float32)
-    scores = pltpu.VMEM((padded, block), jnp.float32)
-    og_spec = pl.BlockSpec((1, block, width), lambda i, c, at: (i, 0, 0))
-    cost = pl.CostEstimate(
-        flops=24 * blocks * block * padded * 256,
-        transcendentals=blocks * block * padded,
-        bytes_accessed=4 * room * width * 3,
-    )
-    outs = []
-    for j in range(chunks):
-        last = j == chunks - 1
-        qg_spec = pl.BlockSpec((1, block, width), lambda i, c, at, j=j: (i, j, 0))
-        if j == 0:
-            og, key_value, key_value_t, acc = pl.pallas_call(
-                functools.partial(first_kernel, valid=valid, tile=tile),
-                grid_spec=pltpu.PrefetchScalarGridSpec(
-                    num_scalar_prefetch=2,
-                    grid=(blocks,),
-                    in_specs=[whole(kv.shape), qg_spec],
-                    out_specs=[og_spec] + [whole(s.shape) for s in packed + [acc_shape]],
-                    scratch_shapes=[wide, scores],
-                ),
-                out_shape=[og_shape] + packed + [acc_shape],
-                cost_estimate=cost,
-                name="attention_first",
-            )(counts, index, kv, qg)
-        else:
-            out_shape = jax.ShapeDtypeStruct(kv.shape, jnp.bfloat16) if last else acc_shape
-            og, acc = pl.pallas_call(
-                functools.partial(later_kernel, valid=valid, tile=tile, last=last),
-                grid_spec=pltpu.PrefetchScalarGridSpec(
-                    num_scalar_prefetch=2,
-                    grid=(blocks,),
-                    in_specs=[whole(s.shape) for s in packed + [acc_shape]] + [qg_spec],
-                    out_specs=[og_spec, whole(out_shape.shape)],
-                    scratch_shapes=[wide, scores],
-                ),
-                out_shape=[og_shape, out_shape],
-                cost_estimate=cost,
-                name="attention_later",
-            )(counts, index, key_value, key_value_t, acc, qg)
-        outs.append(og)
-    return outs, acc
-
-
-def side_by_side(part, heads, first, flip=0):
+    out_shape = jax.ShapeDtypeStruct((blocks, block, width), jnp.bfloat16)
+    pair = blocks
+    out_spec = pl.BlockSpec((pair, block, width), lambda i, c, at: (i, 0, 0))
+    alone = [jax.ShapeDtypeStruct((block, width), jnp.bfloat16)] * blocks
+    return pl.pallas_call(
+        functools.partial(first_kernel, valid=valid, tile=tile),
+        grid_spec=pltpu.PrefetchScalarGridSpec(
+            num_scalar_prefetch=2,
+            grid=(blocks // pair,),
+            in_specs=[
+                whole(kv.shape),
+                pl.BlockSpec((pair, block, width), lambda i, c, at: (i, 0, 0)),
+            ],
+            out_specs=[out_spec] + [whole(s.shape) for s in alone + shapes],
+            scratch_shapes=[
+                pltpu.VMEM((room, width), jnp.float32),
+                pltpu.VMEM((3, padded, block), jnp.float32),
+                pltpu.VMEM((3, padded, block), jnp.float32),
+                pltpu.VMEM((3, width, block), jnp.float32),
+            ],
+        ),
+        out_shape=[out_shape] + alone + shapes,
+        cost_estimate=attention_cost(blocks * block, padded),
+        name="attention_first",
+    )(counts, index, kv, qg)
+
+
+def attention_later(counts, index, packed, kv_shape, qg, valid, at, block, tile=1280):
+    blocks, _, width = qg.shape
+    padded, pair = packed[0].shape[0], blocks
+    out_shape = [
+        jax.ShapeDtypeStruct((blocks, block, width), jnp.bfloat16),
+        *[jax.ShapeDtypeStruct((block, width), jnp.bfloat16)] * blocks,
+        jax.ShapeDtypeStruct(kv_shape, jnp.bfloat16),
+    ]
+    return pl.pallas_call(
+        functools.partial(later_kernel, valid=valid, tile=tile),
+        grid_spec=pltpu.PrefetchScalarGridSpec(
+            num_scalar_prefetch=2,
+            grid=(blocks // pair,),
+            in_specs=[whole(part.shape) for part in packed]
+            + [pl.BlockSpec((pair, block, width), lambda i, c, b: (i, at, 0))],
+            out_specs=[
+                pl.BlockSpec((pair, block, width), lambda i, c, b: (i, 0, 0)),
+                *[whole((block, width))] * blocks,
+                whole(kv_shape),
+            ],
+            scratch_shapes=[
+                pltpu.VMEM(packed[2].shape, jnp.float32),
+                pltpu.VMEM((padded + kv_shape[1] + 16, width), jnp.float32),
+                pltpu.VMEM((3, padded, block), jnp.float32),
+                pltpu.VMEM((3, padded, block), jnp.float32),
+                pltpu.VMEM((3, width, block), jnp.float32),
+            ],
+        ),
+        out_shape=out_shape,
+        cost_estimate=attention_cost(blocks * block, padded),
+        name="attention_later",
+    )(counts, index, *packed, qg)
+
+
+def attention_cost(rows, padded):
+    return pl.CostEstimate(
+        flops=24 * rows * padded * 256,
+        transcendentals=rows * padded,
+        bytes_accessed=8 * padded * 2 * HEAD,
+    )
+
+
+def side_by_side(part, heads, first):
     lanes = slice(0, HEAD) if first else slice(HEAD, 2 * HEAD)
-    return jnp.concatenate([part[h ^ flip][:, lanes] for h in range(heads)], axis=1)
+    return jnp.concatenate([part[h][:, lanes] for h in range(heads)], axis=1)
 
 
 def token_grad_kernel(dkv_ref, key_w_ref, value_w_ref, out_ref, acc, *, heads):
@@ -457,64 +519,76 @@
     )(dkv, weight, weight)
 
 
-def latent_grad_kernel(index_ref, *refs, heads, groups):
-    w_ref = refs[groups]
+def latent_grad_kernel(index_ref, *refs, heads, groups, split):
+    w_ref = refs[groups * heads if split else groups]
     out_ref, grad_ref = refs[-2:]
     cols = heads * HEAD
     total = None
     for k in range(groups):
-        part = refs[k]
+        if split:
+            part = [refs[k * heads + h][...] for h in range(heads)]
+            part = [chosen(part, h, index_ref[1]) for h in range(heads)]
+        else:
+            part = [refs[k][h ^ index_ref[1]] for h in range(heads)]
         at = pl.multiple_of((index_ref[0] ^ k) * cols, cols)
-        out_ref[:, pl.ds(at, cols)] = side_by_side(part, heads, True, index_ref[1])
-        term = mm(side_by_side(part, heads, False, index_ref[1]), w_ref[:, pl.ds(at, cols)], NT)
+        out_ref[:, pl.ds(at, cols)] = side_by_side(part, heads, True)
+        term = mm(side_by_side(part, heads, False), w_ref[:, pl.ds(at, cols)], NT)
         total = term if total is None else total + term
     grad_ref[...] = total.astype(jnp.bfloat16)
 
 
+def chosen(part, h, flip):
+    low = jnp.where(flip % 2 == 1, part[h ^ 1], part[h])
+    high = jnp.where(flip % 2 == 1, part[h ^ 3], part[h ^ 2])
+    return jnp.where(flip // 2 == 1, high, low)
+
+
 def latent_grad(index, parts, weight, chunk, chunks, earlier):
-    heads, rows, pair = parts[0].shape
+    split = isinstance(parts[0], list)
     groups = len(parts)
+    heads = len(parts[0]) if split else parts[0].shape[0]
+    parts = sum(parts, []) if split else parts
+    rows = parts[0].shape[-2]
     width = weight.shape[0]
     shape = jax.ShapeDtypeStruct((rows * chunks, width), jnp.bfloat16)
-    part_spec = pl.BlockSpec((heads, rows, pair), lambda i, at: (0, 0, 0))
     out_spec = pl.BlockSpec((rows, width), lambda i, at: (chunk, 0))
     return pl.pallas_call(
-        functools.partial(latent_grad_kernel, heads=heads, groups=groups),
+        functools.partial(latent_grad_kernel, heads=heads, groups=groups, split=split),
         grid_spec=pltpu.PrefetchScalarGridSpec(
             num_scalar_prefetch=1,
             grid=(1,),
-            in_specs=[part_spec] * groups
+            in_specs=[
+                pl.BlockSpec(part.shape, lambda i, at, n=part.ndim: (0,) * n) for part in parts
+            ]
             + [pl.BlockSpec(weight.shape, lambda i, at: (0, 0))]
             + [pl.BlockSpec(memory_space=pl.ANY)] * len(earlier),
             out_specs=[out_spec, out_spec],
         ),
         out_shape=[shape, shape],
-        input_output_aliases={2 + groups + k: k for k in range(len(earlier))},
+        input_output_aliases={2 + len(parts) + k: k for k in range(len(earlier))},
         name="latent_grad",
     )(index, *parts, weight, *earlier)
 
 
 def weight_grad_kernel(*refs, slots):
-    out_ref = refs[-1]
+    out_ref, one_ref, two_ref = refs[-1], refs[slots], refs[slots + 1]
+    rows = two_ref.shape[1]
     total = None
     for k in range(slots):
-        at = 0
-        for og_ref in refs[slots:-1]:
-            rows = og_ref.shape[1]
-            low = og_ref[k].astype(jnp.float32).T[HEAD:, :].astype(jnp.bfloat16)
-            term = mm(low, refs[k][at:at + rows, :])
-            total = term if total is None else total + term
-            at = at + rows
+        low = one_ref[k].astype(jnp.float32).T[HEAD:, :].astype(jnp.bfloat16)
+        term = mm(low, refs[k][:rows, :])
+        total = term if total is None else total + term
+        low = two_ref[k].astype(jnp.float32).T[HEAD:, :].astype(jnp.bfloat16)
+        total = total + mm(low, refs[k][rows:, :])
     out_ref[...] = total.astype(jnp.bfloat16)
 
 
-def weight_grad(latents, outs):
-    width = latents[0].shape[1]
+def weight_grad(latents, one, two):
     return pl.pallas_call(
         functools.partial(weight_grad_kernel, slots=len(latents)),
-        out_shape=jax.ShapeDtypeStruct((HEAD, width), jnp.bfloat16),
+        out_shape=jax.ShapeDtypeStruct((HEAD, latents[0].shape[1]), jnp.bfloat16),
         name="weight_grad",
-    )(*latents, *outs)
+    )(*latents, one, two)
 
 
 def turn_kernel(index_ref, *refs):
@@ -548,8 +622,9 @@
 
 
 def exchanged(slots, axis):
-    others = [swapped(slots[k], axis, k) for k in range(1, slots.shape[0])]
-    return jnp.stack([slots[0]] + others)
+    return [slots[0]] + [
+        swapped(slots[k], axis, k) for k in range(1, lax.axis_size(axis))
+    ]
 
 
 def gathered(shard, axis):
@@ -572,21 +647,34 @@
     held, pairs = lax.optimization_barrier((latents, pairs))
     pairs = lax.all_to_all(pairs, everyone, 0, 0, tiled=True)
     qg = project_queries(held, query_weight, cotangent, index, counts.reshape(groups), groups)
-    qg = exchanged(qg, "blk")
+    qg = jnp.stack(exchanged(qg, "blk"))
     all_counts = qg[:, latent_rows, :groups].astype(jnp.int32)
+    half = latent_rows // chunks
     held, qg = lax.optimization_barrier((latents, qg))
-    every = gathered(held, "blk")
-    outs, dkv = attention(all_counts, index, pairs, qg, valid, latent_rows, chunks)
-    parts = [gathered(exchanged(og, "blk"), "narrow") for og in outs]
+    far = swapped(held, "blk", 2)
+    found = attention_first(all_counts, index, pairs, qg, valid, half)
+    one, ones, packed = found[0], found[1:1 + blocks], found[1 + blocks:]
+    near_one, far_one = swapped(one, "narrow", 1), swapped(one, "narrow", 2)
+    two, *twos, dkv = attention_later(
+        all_counts, index, packed, pairs.shape, qg, valid, 1, half
+    )
+    dkv, ones, twos, near_one, far_one, far = lax.optimization_barrier(
+        (dkv, ones, twos, near_one, far_one, far)
+    )
+    every = [latents, swapped(latents, "blk", 1), far, swapped(far, "blk", 1)]
+    last_one = swapped(far_one, "narrow", 1)
     dkv = lax.all_to_all(dkv, everyone, 0, 0, tiled=True)
+    own_two = jnp.stack(exchanged(twos, "blk"))
+    own_two, every, two = lax.optimization_barrier((own_two, every, two))
+    part_two = gathered(own_two, "narrow")
+    part_one = [exchanged(held, "blk") for held in (ones, near_one, far_one, last_one)]
+    grad_query_weight = turn(index, gathered(weight_grad(every, one, two), "blk"))
     grad_tokens = token_grad(
         dkv.reshape(blocks, groups, tok_rows, 2 * HEAD), keyvalue_weight
     )
-    grad_query_weight = turn(index, gathered(weight_grad(every, outs), "blk"))
-    done = ()
-    for j in range(chunks):
-        done = latent_grad(index, parts[j], query_weight, j, chunks, done)
-    latent_out, grad_latents = done
+    done = latent_grad(index, part_one, query_weight, 0, chunks, ())
+    done, part_two = lax.optimization_barrier((done, part_two))
+    latent_out, grad_latents = latent_grad(index, part_two, query_weight, 1, chunks, done)
     return (latent_out, grad_latents, grad_query_weight, grad_tokens)
 
 

time: 157 us -> 146 us (0.930)
  waiting for transfers between devices: 55.9 us -> 36.3 us
  starting transfers between devices: 25.3 us -> 34.4 us
  local copies, waits for them, and re-layouts: 7.96 us -> 12.8 us
  Pallas kernels: 64.2 us -> 59.8 us
    ppermute x21 -> x30, waiting for transfers between devices: 49.9 us -> 30.2 us  [swapped(): lax.ppermute(shard, axis, [(i, i ^ bit) for i in range(lax.axis_size(axis...]
    ppermute x21 -> x30, starting transfers between devices: 14 us -> 22.8 us  [swapped(): lax.ppermute(shard, axis, [(i, i ^ bit) for i in range(lax.axis_size(axis...]
    pallas_call x2, Pallas kernels: 34.4 us -> 29.7 us  [the longest x1 15.1 us: attention_later(): pl.pallas_call(functools.partial(later_kernel, valid=valid, tile=tile), g...]
    squeeze x0 -> x3, local copies, waits for them, and re-layouts: none -> 3.87 us  [exchanged(): slots[k]]
    unnamed x30 -> x54, local copies, waits for them, and re-layouts: 5.76 us -> 7.72 us
  transfers between devices with their start and end apart: 23 -> 32, of which waited for: 12 -> 10; matrix products, arithmetic and copies ran while one was open for 3% -> 4% of each run, Pallas kernels for 35% -> 34%
where the time goes in v3:
time: 146 us; the launch traced here: 145 us
  Pallas kernels  59.8 us (41%)
  waiting for transfers between devices  36.3 us (25%)
  starting transfers between devices  34.4 us (24%)
  local copies, waits for them, and re-layouts  12.8 us (9%)
    ppermute x30, waiting for transfers between devices, swapped(): lax.ppermute(shard, axis, [(i, i ^ bit) for i in range(lax.axis_size(axis...  30.2 us
    ppermute x30, starting transfers between devices, swapped(): lax.ppermute(shard, axis, [(i, i ^ bit) for i in range(lax.axis_size(axis...  22.8 us
    pallas_call x1, Pallas kernels, attention_later(): pl.pallas_call(functools.partial(later_kernel, valid=valid, tile=tile), g...  15.1 us
    pallas_call x1, Pallas kernels, attention_first(): pl.pallas_call(functools.partial(first_kernel, valid=valid, tile=tile), g...  14.6 us
    pallas_call x2, Pallas kernels, latent_grad(): pl.pallas_call(functools.partial(latent_grad_kernel, heads=heads, groups=...  8.75 us
    unnamed x54, local copies, waits for them, and re-layouts  7.72 us
    all_to_all x1, starting transfers between devices, by_head(): pairs = lax.all_to_all(pairs, everyone, 0, 0, tiled=True)  7.38 us
    all_to_all x1, waiting for transfers between devices, by_head(): pairs = lax.all_to_all(pairs, everyone, 0, 0, tiled=True)  6.03 us
  transfers between devices with their start and end apart: 32, of which 10 were waited for; matrix products, arithmetic and copies ran while one was open for 4% of the time, Pallas kernels for 34%

profile of v3, /device:TPU:0, one launch (start us, length us, event | category | flops | bytes accessed | tf_op | source)
XLA Modules:
  0.0 145.5 jit_solution(3334927195684811133)
XLA Ops:
  0.6 5.3 %project_pairs.1 = bf16[4,4,256,128]{3,2,1,0:T(8,128)(2,1)} custom-call(bf16[256,1024]{1,0:T(8,128)(2,1)} %tok_ref.1, bf16[1024,2048]{1,0:T(8,128)(2,1)} %value_w_ref.3, bf16[1024,2048]{1,0:T(8,128)(2,1)} %value_w_ref.3), custom_call_target="tpu_custom_call" | custom-call | tf_op jit(solution)/shard_map/project_pairs/pallas_call | solution.py:173
  5.9 7.4 %all-to-all-start = ((bf16[16,256,128]{2,1,0:T(8,128)(2,1)}), bf16[16,256,128]{2,1,0:T(8,128)(2,1)S(1)}, u32[]{:S(2)}, u32[]{:S(2)}) async-start(bf16[16,256,128]{2,1,0:T(8,128)(2,1)} %bitcast.44), calls=%async_computation | async-start | bytes 2097152 | tf_op jit(solution)/shard_map/all_to_all | solution.py:648
  14.0 4.3 %project_queries.1 = bf16[4,528,128]{2,1,0:T(8,128)(2,1)} custom-call(s32[2]{0:T(128)} %pad_add_fusion.index_ref, s32[4]{0:T(128)} %bitcast.54, bf16[512,1024]{1,0:T(8,128)(2,1)} %refs_0_, bf16[1024,1024]{1,0:T(8,128)(2,1)} %refs_4_.1, bf16[512,1024]{1,0:T(8,128)(2,1)} %grad_ref.1), custom_call_target="tpu_custom_call" | custom-call | tf_op jit(solution)/shard_map/project_queries/pallas_call | solution.py:214
  18.2 1.2 fusion
  19.9 1.6 %collective-permute-start.1 = (bf16[528,128]{1,0:T(8,128)(2,1)S(1)}, bf16[528,128]{1,0:T(8,128)(2,1)S(1)}, u32[]{:S(2)}, u32[]{:S(2)}) collective-permute-start(bf16[528,128]{1,0:T(8,128)(2,1)S(1)} %get-tuple-element.98), channel_id=1, source_target_pairs={{0,8},{4,12},{8,0},{12,4},{1,9},{5,13},{9,1},{13,5},{2,10},{6,14},... | collective-permute-start | bytes 405512 | tf_op jit(solution)/shard_map/ppermute | solution.py:621
  21.6 7.8 %collective-permute-done.1 = bf16[528,128]{1,0:T(8,128)(2,1)S(1)} collective-permute-done((bf16[528,128]{1,0:T(8,128)(2,1)S(1)}, bf16[528,128]{1,0:T(8,128)(2,1)S(1)}, u32[]{:S(2)}, u32[]{:S(2)}) %collective-permute-start.1) | collective-permute-done | bytes 135200 | tf_op jit(solution)/shard_map/ppermute | solution.py:621
  29.4 3.2 %collective-permute-done.2 = bf16[528,128]{1,0:T(8,128)(2,1)S(1)} collective-permute-done((bf16[528,128]{1,0:T(8,128)(2,1)S(1)}, bf16[528,128]{1,0:T(8,128)(2,1)S(1)}, u32[]{:S(2)}, u32[]{:S(2)}) %collective-permute-start.2) | collective-permute-done | bytes 135200 | tf_op jit(solution)/shard_map/ppermute | solution.py:621
  34.1 6.0 %all-to-all-done.kv_ref = bf16[16,256,128]{2,1,0:T(8,128)(2,1)S(1)} async-done(((bf16[16,256,128]{2,1,0:T(8,128)(2,1)}), bf16[16,256,128]{2,1,0:T(8,128)(2,1)S(1)}, u32[]{:S(2)}, u32[]{:S(2)}) %all-to-all-start) | async-done | bytes 1048608 | tf_op jit(solution)/shard_map/all_to_all | solution.py:648
  41.1 14.6 %attention_first.1 = (bf16[4,256,128]{2,1,0:T(8,128)(2,1)}, bf16[256,128]{1,0:T(8,128)(2,1)}, bf16[256,128]{1,0:T(8,128)(2,1)}, bf16[256,128]{1,0:T(8,128)(2,1)}...) custom-call(s32[4,4]{1,0:T(4,128)} %bitcast.52, ...), custom_call_target="tpu_custom_call" | custom-call | flops 16106127360 | bytes 2621440 | tf_op jit(solution)/shard_map/attention_first/pallas_call | solution.py:416
  55.7 1.5 %collective-permute-start.4 = (bf16[4,256,128]{2,1,0:T(8,128)(2,1)}, bf16[4,256,128]{2,1,0:T(8,128)(2,1)}, u32[]{:S(2)}, u32[]{:S(2)}) collective-permute-start(bf16[4,256,128]{2,1,0:T(8,128)(2,1)} %get-tuple-element.65.refs_4_), channel_id=1, source_target_pairs={{0,2},{1,3},{2,0},{3,1},{4,6},{5,7},{6,4},{7,5},{8,10},{9,11},{10,... | collective-permute-start | bytes 786440 | tf_op jit(solution)/shard_map/ppermute | solution.py:621
  57.3 15.1 %attention_later.1 = (bf16[4,256,128]{2,1,0:T(8,128)(2,1)}, bf16[256,128]{1,0:T(8,128)(2,1)}, bf16[256,128]{1,0:T(8,128)(2,1)}, bf16[256,128]{1,0:T(8,128)(2,1)}...) custom-call(s32[4,4]{1,0:T(4,128)} %bitcast.53, s32[2]{0:T(128)} %pad_add_fusion.index_ref, ...), custom_call_target="tpu_custom_call" | custom-call | flops 16106127360 | bytes 2621440 | tf_op jit(solution)/shard_map/attention_later/pallas_call | solution.py:447
  72.4 4.2 %all-to-all-start.1 = ((bf16[16,256,128]{2,1,0:T(8,128)(2,1)}), bf16[16,256,128]{2,1,0:T(8,128)(2,1)S(1)}, u32[]{:S(2)}, u32[]{:S(2)}) async-start(bf16[16,256,128]{2,1,0:T(8,128)(2,1)} %get-tuple-element.95), calls=%async_computation.1 | async-start | bytes 2097152 | tf_op jit(solution)/shard_map/all_to_all | solution.py:666
  77.6 1.6 %collective-permute-start.20 = (bf16[256,128]{1,0:T(8,128)(2,1)}, bf16[256,128]{1,0:T(8,128)(2,1)S(1)}, u32[]{:S(2)}, u32[]{:S(2)}) collective-permute-start(bf16[256,128]{1,0:T(8,128)(2,1)} %get-tuple-element.77), channel_id=1, source_target_pairs={{0,8},{4,12},{8,0},{12,4},{1,9},{5,13},{9,1},{13,5},{2,10},{6,14},... | collective-permute-start | bytes 196616 | tf_op jit(solution)/shard_map/ppermute | solution.py:621
  79.9 1.2 collective-permute-done.19
  81.1 1.8 %collective-permute-start.15 = (bf16[4,256,128]{2,1,0:T(8,128)(2,1)}, bf16[4,256,128]{2,1,0:T(8,128)(2,1)}, u32[]{:S(2)}, u32[]{:S(2)}) collective-permute-start(bf16[4,256,128]{2,1,0:T(8,128)(2,1)} %collective-permute-done.4), channel_id=1, source_target_pairs={{0,1},{1,0},{2,3},{3,2},{4,5},{5,4},{6,7},{7,6},{8,9},{9,8},{10,11... | collective-permute-start | bytes 786440 | tf_op jit(solution)/shard_map/ppermute | solution.py:621
  82.9 7.7 %collective-permute-done.20 = bf16[256,128]{1,0:T(8,128)(2,1)S(1)} collective-permute-done((bf16[256,128]{1,0:T(8,128)(2,1)}, bf16[256,128]{1,0:T(8,128)(2,1)S(1)}, u32[]{:S(2)}, u32[]{:S(2)}) %collective-permute-start.20) | collective-permute-done | bytes 65568 | tf_op jit(solution)/shard_map/ppermute | solution.py:621
  91.6 1.1 collective-permute-start.11
  94.8 1.6 %slice_bitcast_fusion.7 = (bf16[256,128]{1,0:T(8,128)(2,1)S(1)}, bf16[256,128]{1,0:T(8,128)(2,1)S(1)}, bf16[256,128]{1,0:T(8,128)(2,1)S(1)}, bf16[256,128]{1,0:T(8,128)(2,1)}) fusion(bf16[4,256,128]{2,1,0:T(8,128)(2,1)} %collective-permute-done.4), kind=kLoop, calls=%fused_computation.9 | loop fusion | bytes 524288 | tf_op jit(solution)/shard_map/squeeze | solution.py:626
  96.8 1.7 %collective-permute-start.13 = (bf16[256,128]{1,0:T(8,128)(2,1)S(1)}, bf16[256,128]{1,0:T(8,128)(2,1)S(1)}, u32[]{:S(2)}, u32[]{:S(2)}) collective-permute-start(bf16[256,128]{1,0:T(8,128)(2,1)S(1)} %get-tuple-element.105), channel_id=1, source_target_pairs={{0,8},{4,12},{8,0},{12,4},{1,9},{5,13},{9,1},{13,5},{2,10},{6,14},... | collective-permute-start | bytes 196616 | tf_op jit(solution)/shard_map/ppermute | solution.py:621
  98.9 2.3 %collective-permute-done.13.refs_10_ = bf16[256,128]{1,0:T(8,128)(2,1)S(1)} collective-permute-done((bf16[256,128]{1,0:T(8,128)(2,1)S(1)}, bf16[256,128]{1,0:T(8,128)(2,1)S(1)}, u32[]{:S(2)}, u32[]{:S(2)}) %collective-permute-start.13) | collective-permute-done | bytes 65568 | tf_op jit(solution)/shard_map/ppermute | solution.py:621
  101.9 3.9 %weight_grad.1.refs_0_ = bf16[64,1024]{1,0:T(8,128)(2,1)} custom-call(bf16[512,1024]{1,0:T(8,128)(2,1)} %refs_0_, bf16[512,1024]{1,0:T(8,128)(2,1)} %copy-done.3, bf16[512,1024]{1,0:T(8,128)(2,1)} %copy-done.2, bf16[512,1024]{1,0:T(8,128)(2,1)} %copy-done.4, bf16[4,256,128]{2,1,0:T(8,128)(2,1)} %get-tuple-element.65.refs_4_, ...), custom_call_target="tpu_custom_call" | custom-call | tf_op jit(solution)/shard_map/weight_grad/pallas_call | solution.py:587
  105.7 3.0 %collective-permute-start.7 = (bf16[256,128]{1,0:T(8,128)(2,1)}, bf16[256,128]{1,0:T(8,128)(2,1)S(1)}, u32[]{:S(2)}, u32[]{:S(2)}) collective-permute-start(bf16[256,128]{1,0:T(8,128)(2,1)} %get-tuple-element.69), channel_id=1, source_target_pairs={{0,8},{4,12},{8,0},{12,4},{1,9},{5,13},{9,1},{13,5},{2,10},{6,14},... | collective-permute-start | bytes 196616 | tf_op jit(solution)/shard_map/ppermute | solution.py:621
  109.3 2.9 %collective-permute-start.24 = (bf16[4,256,128]{2,1,0:T(8,128)(2,1)S(1)}, bf16[4,256,128]{2,1,0:T(8,128)(2,1)S(1)}, u32[]{:S(2)}, u32[]{:S(2)}) collective-permute-start(bf16[4,256,128]{2,1,0:T(8,128)(2,1)S(1)} %pad_maximum_fusion.1.refs_0_), channel_id=1, source_target_pairs={{0,1},{1,0},{2,3},{3,2},{4,5},{5,4},{6,7},{7,6},{8,9},{9,8},{10,11... | collective-permute-start | bytes 786440 | tf_op jit(solution)/shard_map/ppermute | solution.py:621
  112.2 1.4 collective-permute-start.28
  114.5 1.7 %slice_bitcast_fusion.3 = (bf16[256,128]{1,0:T(8,128)(2,1)S(1)}, bf16[256,128]{1,0:T(8,128)(2,1)S(1)}, bf16[256,128]{1,0:T(8,128)(2,1)S(1)}, bf16[256,128]{1,0:T(8,128)(2,1)}) fusion(bf16[4,256,128]{2,1,0:T(8,128)(2,1)} %collective-permute-done.15), kind=kLoop, calls=%fused_computation.5 | loop fusion | bytes 524288 | tf_op jit(solution)/shard_map/squeeze | solution.py:626
  116.2 1.5 %collective-permute-start.17 = (bf16[256,128]{1,0:T(8,128)(2,1)S(1)}, bf16[256,128]{1,0:T(8,128)(2,1)S(1)}, u32[]{:S(2)}, u32[]{:S(2)}) collective-permute-start(bf16[256,128]{1,0:T(8,128)(2,1)S(1)} %get-tuple-element.101), channel_id=1, source_target_pairs={{0,8},{4,12},{8,0},{12,4},{1,9},{5,13},{9,1},{13,5},{2,10},{6,14},... | collective-permute-start | bytes 196616 | tf_op jit(solution)/shard_map/ppermute | solution.py:621
  118.3 2.4 %collective-permute-done.17.refs_14_ = bf16[256,128]{1,0:T(8,128)(2,1)S(1)} collective-permute-done((bf16[256,128]{1,0:T(8,128)(2,1)S(1)}, bf16[256,128]{1,0:T(8,128)(2,1)S(1)}, u32[]{:S(2)}, u32[]{:S(2)}) %collective-permute-start.17) | collective-permute-done | bytes 65568 | tf_op jit(solution)/shard_map/ppermute | solution.py:621
  121.3 3.7 %collective-permute-done.18.refs_15_ = bf16[256,128]{1,0:T(8,128)(2,1)S(1)} collective-permute-done((bf16[256,128]{1,0:T(8,128)(2,1)S(1)}, bf16[256,128]{1,0:T(8,128)(2,1)S(1)}, u32[]{:S(2)}, u32[]{:S(2)}) %collective-permute-start.18) | collective-permute-done | bytes 65568 | tf_op jit(solution)/shard_map/ppermute | solution.py:621
  125.7 4.4 %latent_grad.2 = (bf16[512,1024]{1,0:T(8,128)(2,1)}, bf16[512,1024]{1,0:T(8,128)(2,1)}) custom-call(s32[2]{0:T(128)} %pad_add_fusion.index_ref, bf16[256,128]{1,0:T(8,128)(2,1)} %get-tuple-element.67.refs_0_, bf16[256,128]{1,0:T(8,128)(2,1)} %collective-permute-done.6.refs_1_, bf16[256,128]{1,0:T(8,128)(2,1)} %copy-done.21, bf16[256,128]{1,0:T(8,128)(2,1)} %copy-done.22, ...), custom_call_target="tpu_custom_call" | custom-call | tf_op jit(solution)/shard_map/latent_grad/pallas_call | solution.py:555
  131.4 2.8 %turn.1 = bf16[1024,256]{1,0:T(8,128)(2,1)} custom-call(s32[2]{0:T(128)} %pad_add_fusion.index_ref, bf16[64,1024]{1,0:T(8,128)(2,1)} %weight_grad.1.refs_0_, bf16[64,1024]{1,0:T(8,128)(2,1)} %copy-done.12, bf16[64,1024]{1,0:T(8,128)(2,1)} %copy-done.11, bf16[64,1024]{1,0:T(8,128)(2,1)} %copy-done.13), custom_call_target="tpu_custom_call" | custom-call | tf_op jit(solution)/shard_map/turn/pallas_call | solution.py:606
  135.1 4.3 %latent_grad.3 = (bf16[512,1024]{1,0:T(8,128)(2,1)}, bf16[512,1024]{1,0:T(8,128)(2,1)}) custom-call(s32[2]{0:T(128)} %pad_add_fusion.index_ref, bf16[4,256,128]{2,1,0:T(8,128)(2,1)} %copy-done.6, bf16[4,256,128]{2,1,0:T(8,128)(2,1)} %copy-done.9, bf16[4,256,128]{2,1,0:T(8,128)(2,1)} %copy-done.8, ...), custom_call_target="tpu_custom_call", output_to_operand_aliasing={{0}: (6, {}), {1}: (7, {})} | custom-call | tf_op jit(solution)/shard_map/latent_grad/pallas_call | solution.py:555
  140.4 5.1 %token_grad.1 = bf16[256,1024]{1,0:T(8,128)(2,1)} custom-call(bf16[4,4,256,128]{3,2,1,0:T(8,128)(2,1)} %bitcast.43, bf16[1024,2048]{1,0:T(8,128)(2,1)} %value_w_ref.3, bf16[1024,2048]{1,0:T(8,128)(2,1)} %value_w_ref.3), custom_call_target="tpu_custom_call" | custom-call | tf_op jit(solution)/shard_map/token_grad/pallas_call | solution.py:507
  (103 shorter events, 16.3 us)
Async XLA Ops:
  5.9 34.2 %all-to-all-start = ((bf16[16,256,128]{2,1,0:T(8,128)(2,1)}), bf16[16,256,128]{2,1,0:T(8,128)(2,1)S(1)}, u32[]{:S(2)}, u32[]{:S(2)}) async-start(bf16[16,256,128]{2,1,0:T(8,128)(2,1)} %bitcast.44), calls=%async_computation | async-start | bytes 2097152 | tf_op jit(solution)/shard_map/all_to_all | solution.py:648
  19.5 2.1 %collective-permute-start = (bf16[528,128]{1,0:T(8,128)(2,1)S(1)}, bf16[528,128]{1,0:T(8,128)(2,1)S(1)}, u32[]{:S(2)}, u32[]{:S(2)}) collective-permute-start(bf16[528,128]{1,0:T(8,128)(2,1)S(1)} %get-tuple-element.99), channel_id=1, source_target_pairs={{0,4},{4,0},{8,12},{12,8},{1,5},{5,1},{9,13},{13,9},{2,6},{6,2},{1... | collective-permute-start | bytes 405512 | tf_op jit(solution)/shard_map/ppermute | solution.py:621
  19.9 9.4 %collective-permute-start.1 = (bf16[528,128]{1,0:T(8,128)(2,1)S(1)}, bf16[528,128]{1,0:T(8,128)(2,1)S(1)}, u32[]{:S(2)}, u32[]{:S(2)}) collective-permute-start(bf16[528,128]{1,0:T(8,128)(2,1)S(1)} %get-tuple-element.98), channel_id=1, source_target_pairs={{0,8},{4,12},{8,0},{12,4},{1,9},{5,13},{9,1},{13,5},{2,10},{6,14},... | collective-permute-start | bytes 405512 | tf_op jit(solution)/shard_map/ppermute | solution.py:621
  21.6 11.0 %collective-permute-start.2 = (bf16[528,128]{1,0:T(8,128)(2,1)S(1)}, bf16[528,128]{1,0:T(8,128)(2,1)S(1)}, u32[]{:S(2)}, u32[]{:S(2)}) collective-permute-start(bf16[528,128]{1,0:T(8,128)(2,1)S(1)} %get-tuple-element.97), channel_id=1, source_target_pairs={{0,12},{4,8},{8,4},{12,0},{1,13},{5,9},{9,5},{13,1},{2,14},{6,10},... | collective-permute-start | bytes 405512 | tf_op jit(solution)/shard_map/ppermute | solution.py:621
  32.6 39.7 %collective-permute-start.5 = (bf16[512,1024]{1,0:T(8,128)(2,1)S(1)}, bf16[512,1024]{1,0:T(8,128)(2,1)S(1)}, u32[]{:S(2)}, u32[]{:S(2)}) collective-permute-start(bf16[512,1024]{1,0:T(8,128)(2,1)S(1)} %copy-done.1), channel_id=1, source_target_pairs={{0,8},{4,12},{8,0},{12,4},{1,9},{5,13},{9,1},{13,5},{2,10},{6,14},... | collective-permute-start | bytes 3145736 | tf_op jit(solution)/shard_map/ppermute | solution.py:621
  55.7 16.7 %collective-permute-start.3 = (bf16[4,256,128]{2,1,0:T(8,128)(2,1)}, bf16[4,256,128]{2,1,0:T(8,128)(2,1)S(1)}, u32[]{:S(2)}, u32[]{:S(2)}) collective-permute-start(bf16[4,256,128]{2,1,0:T(8,128)(2,1)} %get-tuple-element.65.refs_4_), channel_id=1, source_target_pairs={{0,1},{1,0},{2,3},{3,2},{4,5},{5,4},{6,7},{7,6},{8,9},{9,8},{10,11... | collective-permute-start | bytes 786440 | tf_op jit(solution)/shard_map/ppermute | solution.py:621
  55.7 16.7 %collective-permute-start.4 = (bf16[4,256,128]{2,1,0:T(8,128)(2,1)}, bf16[4,256,128]{2,1,0:T(8,128)(2,1)}, u32[]{:S(2)}, u32[]{:S(2)}) collective-permute-start(bf16[4,256,128]{2,1,0:T(8,128)(2,1)} %get-tuple-element.65.refs_4_), channel_id=1, source_target_pairs={{0,2},{1,3},{2,0},{3,1},{4,6},{5,7},{6,4},{7,5},{8,10},{9,11},{10,... | collective-permute-start | bytes 786440 | tf_op jit(solution)/shard_map/ppermute | solution.py:621
  72.4 67.0 %all-to-all-start.1 = ((bf16[16,256,128]{2,1,0:T(8,128)(2,1)}), bf16[16,256,128]{2,1,0:T(8,128)(2,1)S(1)}, u32[]{:S(2)}, u32[]{:S(2)}) async-start(bf16[16,256,128]{2,1,0:T(8,128)(2,1)} %get-tuple-element.95), calls=%async_computation.1 | async-start | bytes 2097152 | tf_op jit(solution)/shard_map/all_to_all | solution.py:666
  76.7 16.1 %collective-permute-start.22 = (bf16[512,1024]{1,0:T(8,128)(2,1)S(1)}, bf16[512,1024]{1,0:T(8,128)(2,1)S(1)}, u32[]{:S(2)}, u32[]{:S(2)}) collective-permute-start(bf16[512,1024]{1,0:T(8,128)(2,1)S(1)} %copy-done.1), channel_id=1, source_target_pairs={{0,4},{4,0},{8,12},{12,8},{1,5},{5,1},{9,13},{13,9},{2,6},{6,2},{1... | collective-permute-start | bytes 3145736 | tf_op jit(solution)/shard_map/ppermute | solution.py:621
  77.1 15.6 %collective-permute-start.23 = (bf16[512,1024]{1,0:T(8,128)(2,1)S(1)}, bf16[512,1024]{1,0:T(8,128)(2,1)S(1)}, u32[]{:S(2)}, u32[]{:S(2)}) collective-permute-start(bf16[512,1024]{1,0:T(8,128)(2,1)S(1)} %collective-permute-done.5.refs_2_), channel_id=1, source_target_pairs={{0,4},{4,0},{8,12},{12,8},{1,5},{5,1},{9,13},{13,9},{2,6},{6,2},{1... | collective-permute-start | bytes 3145736 | tf_op jit(solution)/shard_map/ppermute | solution.py:621
  77.2 3.9 %collective-permute-start.19 = (bf16[256,128]{1,0:T(8,128)(2,1)}, bf16[256,128]{1,0:T(8,128)(2,1)S(1)}, u32[]{:S(2)}, u32[]{:S(2)}) collective-permute-start(bf16[256,128]{1,0:T(8,128)(2,1)} %get-tuple-element.76), channel_id=1, source_target_pairs={{0,4},{4,0},{8,12},{12,8},{1,5},{5,1},{9,13},{13,9},{2,6},{6,2},{1... | collective-permute-start | bytes 196616 | tf_op jit(solution)/shard_map/ppermute | solution.py:621
  77.6 12.9 %collective-permute-start.20 = (bf16[256,128]{1,0:T(8,128)(2,1)}, bf16[256,128]{1,0:T(8,128)(2,1)S(1)}, u32[]{:S(2)}, u32[]{:S(2)}) collective-permute-start(bf16[256,128]{1,0:T(8,128)(2,1)} %get-tuple-element.77), channel_id=1, source_target_pairs={{0,8},{4,12},{8,0},{12,4},{1,9},{5,13},{9,1},{13,5},{2,10},{6,14},... | collective-permute-start | bytes 196616 | tf_op jit(solution)/shard_map/ppermute | solution.py:621
  79.3 12.3 %collective-permute-start.21 = (bf16[256,128]{1,0:T(8,128)(2,1)}, bf16[256,128]{1,0:T(8,128)(2,1)S(1)}, u32[]{:S(2)}, u32[]{:S(2)}) collective-permute-start(bf16[256,128]{1,0:T(8,128)(2,1)} %get-tuple-element.78), channel_id=1, source_target_pairs={{0,12},{4,8},{8,4},{12,0},{1,13},{5,9},{9,5},{13,1},{2,14},{6,10},... | collective-permute-start | bytes 196616 | tf_op jit(solution)/shard_map/ppermute | solution.py:621
  81.1 31.1 %collective-permute-start.15 = (bf16[4,256,128]{2,1,0:T(8,128)(2,1)}, bf16[4,256,128]{2,1,0:T(8,128)(2,1)}, u32[]{:S(2)}, u32[]{:S(2)}) collective-permute-start(bf16[4,256,128]{2,1,0:T(8,128)(2,1)} %collective-permute-done.4), channel_id=1, source_target_pairs={{0,1},{1,0},{2,3},{3,2},{4,5},{5,4},{6,7},{7,6},{8,9},{9,8},{10,11... | collective-permute-start | bytes 786440 | tf_op jit(solution)/shard_map/ppermute | solution.py:621
  90.5 6.2 %collective-permute-start.10 = (bf16[256,128]{1,0:T(8,128)(2,1)S(1)}, bf16[256,128]{1,0:T(8,128)(2,1)S(1)}, u32[]{:S(2)}, u32[]{:S(2)}) collective-permute-start(bf16[256,128]{1,0:T(8,128)(2,1)S(1)} %get-tuple-element.109), channel_id=1, source_target_pairs={{0,8},{4,12},{8,0},{12,4},{1,9},{5,13},{9,1},{13,5},{2,10},{6,14},... | collective-permute-start | bytes 196616 | tf_op jit(solution)/shard_map/ppermute | solution.py:621
  91.6 6.9 %collective-permute-start.11 = (bf16[256,128]{1,0:T(8,128)(2,1)S(1)}, bf16[256,128]{1,0:T(8,128)(2,1)S(1)}, u32[]{:S(2)}, u32[]{:S(2)}) collective-permute-start(bf16[256,128]{1,0:T(8,128)(2,1)S(1)} %get-tuple-element.108), channel_id=1, source_target_pairs={{0,12},{4,8},{8,4},{12,0},{1,13},{5,9},{9,5},{13,1},{2,14},{6,10},... | collective-permute-start | bytes 196616 | tf_op jit(solution)/shard_map/ppermute | solution.py:621
  94.8 19.7 %collective-permute-start.25 = (bf16[4,256,128]{2,1,0:T(8,128)(2,1)S(1)}, bf16[4,256,128]{2,1,0:T(8,128)(2,1)S(1)}, u32[]{:S(2)}, u32[]{:S(2)}) collective-permute-start(bf16[4,256,128]{2,1,0:T(8,128)(2,1)S(1)} %pad_maximum_fusion.1.refs_0_), channel_id=1, source_target_pairs={{0,2},{1,3},{2,0},{3,1},{4,6},{5,7},{6,4},{7,5},{8,10},{9,11},{10,... | collective-permute-start | bytes 786440 | tf_op jit(solution)/shard_map/ppermute | solution.py:621
  96.3 2.3 %collective-permute-start.12 = (bf16[256,128]{1,0:T(8,128)(2,1)S(1)}, bf16[256,128]{1,0:T(8,128)(2,1)S(1)}, u32[]{:S(2)}, u32[]{:S(2)}) collective-permute-start(bf16[256,128]{1,0:T(8,128)(2,1)S(1)} %get-tuple-element.106), channel_id=1, source_target_pairs={{0,4},{4,0},{8,12},{12,8},{1,5},{5,1},{9,13},{13,9},{2,6},{6,2},{1... | collective-permute-start | bytes 196616 | tf_op jit(solution)/shard_map/ppermute | solution.py:621
  96.8 4.5 %collective-permute-start.13 = (bf16[256,128]{1,0:T(8,128)(2,1)S(1)}, bf16[256,128]{1,0:T(8,128)(2,1)S(1)}, u32[]{:S(2)}, u32[]{:S(2)}) collective-permute-start(bf16[256,128]{1,0:T(8,128)(2,1)S(1)} %get-tuple-element.105), channel_id=1, source_target_pairs={{0,8},{4,12},{8,0},{12,4},{1,9},{5,13},{9,1},{13,5},{2,10},{6,14},... | collective-permute-start | bytes 196616 | tf_op jit(solution)/shard_map/ppermute | solution.py:621
  98.5 7.3 %collective-permute-start.14 = (bf16[256,128]{1,0:T(8,128)(2,1)S(1)}, bf16[256,128]{1,0:T(8,128)(2,1)S(1)}, u32[]{:S(2)}, u32[]{:S(2)}) collective-permute-start(bf16[256,128]{1,0:T(8,128)(2,1)S(1)} %get-tuple-element.104), channel_id=1, source_target_pairs={{0,12},{4,8},{8,4},{12,0},{1,13},{5,9},{9,5},{13,1},{2,14},{6,10},... | collective-permute-start | bytes 196616 | tf_op jit(solution)/shard_map/ppermute | solution.py:621
  98.6 10.1 %collective-permute-start.9 = (bf16[256,128]{1,0:T(8,128)(2,1)S(1)}, bf16[256,128]{1,0:T(8,128)(2,1)S(1)}, u32[]{:S(2)}, u32[]{:S(2)}) collective-permute-start(bf16[256,128]{1,0:T(8,128)(2,1)S(1)} %get-tuple-element.110), channel_id=1, source_target_pairs={{0,4},{4,0},{8,12},{12,8},{1,5},{5,1},{9,13},{13,9},{2,6},{6,2},{1... | collective-permute-start | bytes 196616 | tf_op jit(solution)/shard_map/ppermute | solution.py:621
  101.9 7.5 %collective-permute-start.6 = (bf16[256,128]{1,0:T(8,128)(2,1)}, bf16[256,128]{1,0:T(8,128)(2,1)}, u32[]{:S(2)}, u32[]{:S(2)}) collective-permute-start(bf16[256,128]{1,0:T(8,128)(2,1)} %get-tuple-element.68), channel_id=1, source_target_pairs={{0,4},{4,0},{8,12},{12,8},{1,5},{5,1},{9,13},{13,9},{2,6},{6,2},{1... | collective-permute-start | bytes 196616 | tf_op jit(solution)/shard_map/ppermute | solution.py:621
  105.7 10.4 %collective-permute-start.7 = (bf16[256,128]{1,0:T(8,128)(2,1)}, bf16[256,128]{1,0:T(8,128)(2,1)S(1)}, u32[]{:S(2)}, u32[]{:S(2)}) collective-permute-start(bf16[256,128]{1,0:T(8,128)(2,1)} %get-tuple-element.69), channel_id=1, source_target_pairs={{0,8},{4,12},{8,0},{12,4},{1,9},{5,13},{9,1},{13,5},{2,10},{6,14},... | collective-permute-start | bytes 196616 | tf_op jit(solution)/shard_map/ppermute | solution.py:621
  108.7 7.5 %collective-permute-start.8 = (bf16[256,128]{1,0:T(8,128)(2,1)S(1)}, bf16[256,128]{1,0:T(8,128)(2,1)S(1)}, u32[]{:S(2)}, u32[]{:S(2)}) collective-permute-start(bf16[256,128]{1,0:T(8,128)(2,1)S(1)} %copy-done.26), channel_id=1, source_target_pairs={{0,12},{4,8},{8,4},{12,0},{1,13},{5,9},{9,5},{13,1},{2,14},{6,10},... | collective-permute-start | bytes 196616 | tf_op jit(solution)/shard_map/ppermute | solution.py:621
  109.3 24.9 %collective-permute-start.24 = (bf16[4,256,128]{2,1,0:T(8,128)(2,1)S(1)}, bf16[4,256,128]{2,1,0:T(8,128)(2,1)S(1)}, u32[]{:S(2)}, u32[]{:S(2)}) collective-permute-start(bf16[4,256,128]{2,1,0:T(8,128)(2,1)S(1)} %pad_maximum_fusion.1.refs_0_), channel_id=1, source_target_pairs={{0,1},{1,0},{2,3},{3,2},{4,5},{5,4},{6,7},{7,6},{8,9},{9,8},{10,11... | collective-permute-start | bytes 786440 | tf_op jit(solution)/shard_map/ppermute | solution.py:621
  112.2 5.7 %collective-permute-start.28 = (bf16[64,1024]{1,0:T(8,128)(2,1)}, bf16[64,1024]{1,0:T(8,128)(2,1)S(1)}, u32[]{:S(2)}, u32[]{:S(2)}) collective-permute-start(bf16[64,1024]{1,0:T(8,128)(2,1)} %weight_grad.1.refs_0_), channel_id=1, source_target_pairs={{0,8},{4,12},{8,0},{12,4},{1,9},{5,13},{9,1},{13,5},{2,10},{6,14},... | collective-permute-start | bytes 393224 | tf_op jit(solution)/shard_map/ppermute | solution.py:621
  114.5 19.8 %collective-permute-start.26 = (bf16[4,256,128]{2,1,0:T(8,128)(2,1)S(1)}, bf16[4,256,128]{2,1,0:T(8,128)(2,1)S(1)}, u32[]{:S(2)}, u32[]{:S(2)}) collective-permute-start(bf16[4,256,128]{2,1,0:T(8,128)(2,1)S(1)} %collective-permute-done.25.refs_2_), channel_id=1, source_target_pairs={{0,1},{1,0},{2,3},{3,2},{4,5},{5,4},{6,7},{7,6},{8,9},{9,8},{10,11... | collective-permute-start | bytes 786440 | tf_op jit(solution)/shard_map/ppermute | solution.py:621
  116.2 1.6 %collective-permute-start.16 = (bf16[256,128]{1,0:T(8,128)(2,1)S(1)}, bf16[256,128]{1,0:T(8,128)(2,1)S(1)}, u32[]{:S(2)}, u32[]{:S(2)}) collective-permute-start(bf16[256,128]{1,0:T(8,128)(2,1)S(1)} %get-tuple-element.102), channel_id=1, source_target_pairs={{0,4},{4,0},{8,12},{12,8},{1,5},{5,1},{9,13},{13,9},{2,6},{6,2},{1... | collective-permute-start | bytes 196616 | tf_op jit(solution)/shard_map/ppermute | solution.py:621
  116.2 4.5 %collective-permute-start.17 = (bf16[256,128]{1,0:T(8,128)(2,1)S(1)}, bf16[256,128]{1,0:T(8,128)(2,1)S(1)}, u32[]{:S(2)}, u32[]{:S(2)}) collective-permute-start(bf16[256,128]{1,0:T(8,128)(2,1)S(1)} %get-tuple-element.101), channel_id=1, source_target_pairs={{0,8},{4,12},{8,0},{12,4},{1,9},{5,13},{9,1},{13,5},{2,10},{6,14},... | collective-permute-start | bytes 196616 | tf_op jit(solution)/shard_map/ppermute | solution.py:621
  117.7 12.4 %collective-permute-start.27 = (bf16[64,1024]{1,0:T(8,128)(2,1)}, bf16[64,1024]{1,0:T(8,128)(2,1)S(1)}, u32[]{:S(2)}, u32[]{:S(2)}) collective-permute-start(bf16[64,1024]{1,0:T(8,128)(2,1)} %weight_grad.1.refs_0_), channel_id=1, source_target_pairs={{0,4},{4,0},{8,12},{12,8},{1,5},{5,1},{9,13},{13,9},{2,6},{6,2},{1... | collective-permute-start | bytes 393224 | tf_op jit(solution)/shard_map/ppermute | solution.py:621
  117.9 12.3 %collective-permute-start.29 = (bf16[64,1024]{1,0:T(8,128)(2,1)S(1)}, bf16[64,1024]{1,0:T(8,128)(2,1)S(1)}, u32[]{:S(2)}, u32[]{:S(2)}) collective-permute-start(bf16[64,1024]{1,0:T(8,128)(2,1)S(1)} %collective-permute-done.28.refs_2_), channel_id=1, source_target_pairs={{0,4},{4,0},{8,12},{12,8},{1,5},{5,1},{9,13},{13,9},{2,6},{6,2},{1... | collective-permute-start | bytes 393224 | tf_op jit(solution)/shard_map/ppermute | solution.py:621
  120.7 4.4 %collective-permute-start.18 = (bf16[256,128]{1,0:T(8,128)(2,1)S(1)}, bf16[256,128]{1,0:T(8,128)(2,1)S(1)}, u32[]{:S(2)}, u32[]{:S(2)}) collective-permute-start(bf16[256,128]{1,0:T(8,128)(2,1)S(1)} %get-tuple-element.100), channel_id=1, source_target_pairs={{0,12},{4,8},{8,4},{12,0},{1,13},{5,9},{9,5},{13,1},{2,14},{6,10},... | collective-permute-start | bytes 196616 | tf_op jit(solution)/shard_map/ppermute | solution.py:621
  (27 other events, 204.5 us)

commit v4 on v3

--- a/solution.py
+++ b/solution.py
@@ -155,6 +155,14 @@
 
 def whole(shape):
     return pl.BlockSpec(shape, lambda *unused: (0,) * len(shape))
+
+
+def in_vmem(array):
+    return pltpu.with_memory_space_constraint(array, pltpu.VMEM)
+
+
+def held_whole():
+    return pl.BlockSpec(memory_space=pltpu.VMEM)
 
 
 def pairs_kernel(tok_ref, key_w_ref, value_w_ref, out_ref, *, heads):
@@ -419,10 +427,10 @@
             num_scalar_prefetch=2,
             grid=(blocks // pair,),
             in_specs=[
-                whole(kv.shape),
+                held_whole(),
                 pl.BlockSpec((pair, block, width), lambda i, c, at: (i, 0, 0)),
             ],
-            out_specs=[out_spec] + [whole(s.shape) for s in alone + shapes],
+            out_specs=[out_spec] + [whole(s.shape) for s in alone] + [held_whole() for s in shapes],
             scratch_shapes=[
                 pltpu.VMEM((room, width), jnp.float32),
                 pltpu.VMEM((3, padded, block), jnp.float32),
@@ -433,7 +441,7 @@
         out_shape=[out_shape] + alone + shapes,
         cost_estimate=attention_cost(blocks * block, padded),
         name="attention_first",
-    )(counts, index, kv, qg)
+    )(counts, index, in_vmem(kv), qg)
 
 
 def attention_later(counts, index, packed, kv_shape, qg, valid, at, block, tile=1280):
@@ -449,7 +457,7 @@
         grid_spec=pltpu.PrefetchScalarGridSpec(
             num_scalar_prefetch=2,
             grid=(blocks // pair,),
-            in_specs=[whole(part.shape) for part in packed]
+            in_specs=[held_whole() for part in packed]
             + [pl.BlockSpec((pair, block, width), lambda i, c, b: (i, at, 0))],
             out_specs=[
                 pl.BlockSpec((pair, block, width), lambda i, c, b: (i, 0, 0)),
@@ -490,7 +498,7 @@
     def _():
         acc[...] = jnp.zeros(acc.shape, jnp.float32)
 
-    part = [dkv_ref[h, 0] for h in range(heads)]
+    part = [dkv_ref[h, step] for h in range(heads)]
     keys = side_by_side(part, heads, True)
     values = side_by_side(part, heads, False)
     acc[...] += mm(keys, key_w_ref[...], NT) + mm(values, value_w_ref[...], NT)
@@ -508,7 +516,7 @@
         functools.partial(token_grad_kernel, heads=heads),
         grid=(groups,),
         in_specs=[
-            pl.BlockSpec((heads, 1, rows, pair), lambda n: (0, n, 0, 0)),
+            held_whole(),
             pl.BlockSpec((width, cols), lambda n: (0, n)),
             pl.BlockSpec((width, cols), lambda n: (0, n + groups)),
         ],
@@ -516,20 +524,19 @@
         out_shape=jax.ShapeDtypeStruct((rows, width), jnp.bfloat16),
         scratch_shapes=[pltpu.VMEM((rows, width), jnp.float32)],
         name="token_grad",
-    )(dkv, weight, weight)
-
-
-def latent_grad_kernel(index_ref, *refs, heads, groups, split):
-    w_ref = refs[groups * heads if split else groups]
+    )(in_vmem(dkv), weight, weight)
+
+
+def latent_grad_kernel(index_ref, *refs, heads, groups, by_slot):
+    parts, w_ref = refs[:heads if by_slot else groups], refs[heads if by_slot else groups]
     out_ref, grad_ref = refs[-2:]
     cols = heads * HEAD
     total = None
     for k in range(groups):
-        if split:
-            part = [refs[k * heads + h][...] for h in range(heads)]
-            part = [chosen(part, h, index_ref[1]) for h in range(heads)]
+        if by_slot:
+            part = [chosen([ref[k] for ref in parts], h, index_ref[1]) for h in range(heads)]
         else:
-            part = [refs[k][h ^ index_ref[1]] for h in range(heads)]
+            part = [parts[k][h ^ index_ref[1]] for h in range(heads)]
         at = pl.multiple_of((index_ref[0] ^ k) * cols, cols)
         out_ref[:, pl.ds(at, cols)] = side_by_side(part, heads, True)
         term = mm(side_by_side(part, heads, False), w_ref[:, pl.ds(at, cols)], NT)
@@ -543,31 +550,27 @@
     return jnp.where(flip // 2 == 1, high, low)
 
 
-def latent_grad(index, parts, weight, chunk, chunks, earlier):
-    split = isinstance(parts[0], list)
-    groups = len(parts)
-    heads = len(parts[0]) if split else parts[0].shape[0]
-    parts = sum(parts, []) if split else parts
+def latent_grad(index, parts, weight, chunk, chunks, earlier, by_slot):
+    groups, heads = 4, 4
     rows = parts[0].shape[-2]
     width = weight.shape[0]
     shape = jax.ShapeDtypeStruct((rows * chunks, width), jnp.bfloat16)
     out_spec = pl.BlockSpec((rows, width), lambda i, at: (chunk, 0))
     return pl.pallas_call(
-        functools.partial(latent_grad_kernel, heads=heads, groups=groups, split=split),
+        functools.partial(
+            latent_grad_kernel, heads=heads, groups=groups, by_slot=by_slot
+        ),
         grid_spec=pltpu.PrefetchScalarGridSpec(
             num_scalar_prefetch=1,
             grid=(1,),
-            in_specs=[
-                pl.BlockSpec(part.shape, lambda i, at, n=part.ndim: (0,) * n) for part in parts
-            ]
-            + [pl.BlockSpec(weight.shape, lambda i, at: (0, 0))]
+            in_specs=[held_whole()] * (len(parts) + 1)
             + [pl.BlockSpec(memory_space=pl.ANY)] * len(earlier),
             out_specs=[out_spec, out_spec],
         ),
         out_shape=[shape, shape],
         input_output_aliases={2 + len(parts) + k: k for k in range(len(earlier))},
         name="latent_grad",
-    )(index, *parts, weight, *earlier)
+    )(index, *[in_vmem(part) for part in parts], weight, *earlier)
 
 
 def weight_grad_kernel(*refs, slots):
@@ -602,19 +605,18 @@
 def turn(index, parts):
     width = parts[0].shape[1]
     cols = HEAD * len(parts)
-    spec = pl.BlockSpec((HEAD, width), lambda i, at: (0, 0))
     return pl.pallas_call(
         turn_kernel,
         grid_spec=pltpu.PrefetchScalarGridSpec(
             num_scalar_prefetch=1,
             grid=(1,),
-            in_specs=[spec] * len(parts),
+            in_specs=[held_whole()] * len(parts),
             out_specs=pl.BlockSpec((width, cols), lambda i, at: (0, 0)),
             scratch_shapes=[pltpu.VMEM((cols, width), jnp.float32)],
         ),
         out_shape=jax.ShapeDtypeStruct((width, cols), jnp.bfloat16),
         name="turn",
-    )(index, *parts)
+    )(index, *[in_vmem(part) for part in parts])
 
 
 def swapped(shard, axis, bit):
@@ -667,14 +669,20 @@
     own_two = jnp.stack(exchanged(twos, "blk"))
     own_two, every, two = lax.optimization_barrier((own_two, every, two))
     part_two = gathered(own_two, "narrow")
-    part_one = [exchanged(held, "blk") for held in (ones, near_one, far_one, last_one)]
+    by_slot = [
+        jnp.stack([ones[k], near_one[k], far_one[k], last_one[k]]) for k in range(blocks)
+    ]
+    part_one = exchanged(by_slot, "blk")
     grad_query_weight = turn(index, gathered(weight_grad(every, one, two), "blk"))
+    done = latent_grad(index, part_one, query_weight, 0, chunks, (), True)
+    done, dkv = lax.optimization_barrier((done, dkv))
     grad_tokens = token_grad(
         dkv.reshape(blocks, groups, tok_rows, 2 * HEAD), keyvalue_weight
     )
-    done = latent_grad(index, part_one, query_weight, 0, chunks, ())
-    done, part_two = lax.optimization_barrier((done, part_two))
-    latent_out, grad_latents = latent_grad(index, part_two, query_weight, 1, chunks, done)
+    done, part_two, grad_tokens = lax.optimization_barrier((done, part_two, grad_tokens))
+    latent_out, grad_latents = latent_grad(
+        index, part_two, query_weight, 1, chunks, done, False
+    )
     return (latent_out, grad_latents, grad_query_weight, grad_tokens)
 
 

time: 146 us -> 137 us (0.938)
  local copies, waits for them, and re-layouts: 12.8 us -> 4.16 us
  starting transfers between devices: 34.4 us -> 28.3 us
  waiting for transfers between devices: 36.3 us -> 40.8 us
  other arithmetic: 1.35 us -> 3.79 us
  Pallas kernels: 59.8 us -> 58.1 us
    ppermute x30 -> x21, starting transfers between devices: 22.8 us -> 16.5 us  [swapped(): lax.ppermute(shard, axis, [(i, i ^ bit) for i in range(lax.axis_size(axis...]
    unnamed x54 -> x28, local copies, waits for them, and re-layouts: 7.72 us -> 1.61 us
    ppermute x30 -> x21, waiting for transfers between devices: 30.2 us -> 34.7 us  [swapped(): lax.ppermute(shard, axis, [(i, i ^ bit) for i in range(lax.axis_size(axis...]
    squeeze x3 -> x0, local copies, waits for them, and re-layouts: 3.87 us -> none  [exchanged(): slots[k]]
    another operation x0 -> x4, other arithmetic: none -> 2.49 us  [by_head(): jnp.stack([ones[k], near_one[k], far_one[k], last_one[k]])]
  transfers between devices with their start and end apart: 32 -> 23, of which waited for: 10 -> 8; matrix products, arithmetic and copies ran while one was open for 4% -> 5% of each run, Pallas kernels for 34% -> 36%
where the time goes in v4:
time: 137 us; the launch traced here: 136 us
  Pallas kernels  58.1 us (42%)
  waiting for transfers between devices  40.8 us (30%)
  starting transfers between devices  28.3 us (21%)
  local copies, waits for them, and re-layouts  4.16 us (3%)
  other arithmetic  3.79 us (3%)
    ppermute x21, waiting for transfers between devices, swapped(): lax.ppermute(shard, axis, [(i, i ^ bit) for i in range(lax.axis_size(axis...  34.7 us
    ppermute x21, starting transfers between devices, swapped(): lax.ppermute(shard, axis, [(i, i ^ bit) for i in range(lax.axis_size(axis...  16.5 us
    pallas_call x1, Pallas kernels, attention_later(): pl.pallas_call(functools.partial(later_kernel, valid=valid, tile=tile), g...  15.1 us
    pallas_call x1, Pallas kernels, attention_first(): pl.pallas_call(functools.partial(first_kernel, valid=valid, tile=tile), g...  14.1 us
    pallas_call x2, Pallas kernels, latent_grad(): pl.pallas_call(functools.partial(latent_grad_kernel, heads=heads, groups=...  8.02 us
    all_to_all x1, starting transfers between devices, by_head(): pairs = lax.all_to_all(pairs, everyone, 0, 0, tiled=True)  7.38 us
    all_to_all x1, waiting for transfers between devices, by_head(): pairs = lax.all_to_all(pairs, everyone, 0, 0, tiled=True)  6.05 us
    pallas_call x1, Pallas kernels, project_pairs(): pl.pallas_call(functools.partial(pairs_kernel, heads=heads), grid=(groups...  5.29 us
  transfers between devices with their start and end apart: 23, of which 8 were waited for; matrix products, arithmetic and copies ran while one was open for 5% of the time, Pallas kernels for 36%

profile of v4, /device:TPU:0, one launch (start us, length us, event | category | flops | bytes accessed | tf_op | source)
XLA Modules:
  0.0 135.9 jit_solution(11765396653570534535)
XLA Ops:
  0.6 5.3 %project_pairs.1 = bf16[4,4,256,128]{3,2,1,0:T(8,128)(2,1)} custom-call(bf16[256,1024]{1,0:T(8,128)(2,1)} %tok_ref.1, bf16[1024,2048]{1,0:T(8,128)(2,1)} %value_w_ref.3, bf16[1024,2048]{1,0:T(8,128)(2,1)} %value_w_ref.3), custom_call_target="tpu_custom_call" | custom-call | tf_op jit(solution)/shard_map/project_pairs/pallas_call | solution.py:181
  5.9 7.4 %all-to-all-start = ((bf16[16,256,128]{2,1,0:T(8,128)(2,1)}), bf16[16,256,128]{2,1,0:T(8,128)(2,1)S(1)}, u32[]{:S(2)}, u32[]{:S(2)}) async-start(bf16[16,256,128]{2,1,0:T(8,128)(2,1)} %bitcast.24), calls=%async_computation | async-start | bytes 2097152 | tf_op jit(solution)/shard_map/all_to_all | solution.py:650
  13.9 4.3 %project_queries.1 = bf16[4,528,128]{2,1,0:T(8,128)(2,1)} custom-call(s32[2]{0:T(128)} %pad_add_fusion.index_ref, s32[4]{0:T(128)} %bitcast.38, bf16[512,1024]{1,0:T(8,128)(2,1)} %refs_0_, bf16[1024,1024]{1,0:T(8,128)(2,1)} %refs_4_.3, bf16[512,1024]{1,0:T(8,128)(2,1)} %grad_ref.1), custom_call_target="tpu_custom_call" | custom-call | tf_op jit(solution)/shard_map/project_queries/pallas_call | solution.py:222
  18.2 1.2 fusion
  19.9 1.6 %collective-permute-start.1 = (bf16[528,128]{1,0:T(8,128)(2,1)S(1)}, bf16[528,128]{1,0:T(8,128)(2,1)S(1)}, u32[]{:S(2)}, u32[]{:S(2)}) collective-permute-start(bf16[528,128]{1,0:T(8,128)(2,1)S(1)} %get-tuple-element.106), channel_id=1, source_target_pairs={{0,8},{4,12},{8,0},{12,4},{1,9},{5,13},{9,1},{13,5},{2,10},{6,14},... | collective-permute-start | bytes 405512 | tf_op jit(solution)/shard_map/ppermute | solution.py:623
  21.5 7.8 %collective-permute-done.1 = bf16[528,128]{1,0:T(8,128)(2,1)S(1)} collective-permute-done((bf16[528,128]{1,0:T(8,128)(2,1)S(1)}, bf16[528,128]{1,0:T(8,128)(2,1)S(1)}, u32[]{:S(2)}, u32[]{:S(2)}) %collective-permute-start.1) | collective-permute-done | bytes 135200 | tf_op jit(solution)/shard_map/ppermute | solution.py:623
  29.3 3.2 %collective-permute-done.2 = bf16[528,128]{1,0:T(8,128)(2,1)S(1)} collective-permute-done((bf16[528,128]{1,0:T(8,128)(2,1)S(1)}, bf16[528,128]{1,0:T(8,128)(2,1)S(1)}, u32[]{:S(2)}, u32[]{:S(2)}) %collective-permute-start.2) | collective-permute-done | bytes 135200 | tf_op jit(solution)/shard_map/ppermute | solution.py:623
  32.6 0.9 collective-permute-start.5
  34.1 6.1 %all-to-all-done.kv_ref = bf16[16,256,128]{2,1,0:T(8,128)(2,1)S(1)} async-done(((bf16[16,256,128]{2,1,0:T(8,128)(2,1)}), bf16[16,256,128]{2,1,0:T(8,128)(2,1)S(1)}, u32[]{:S(2)}, u32[]{:S(2)}) %all-to-all-start) | async-done | bytes 1048608 | tf_op jit(solution)/shard_map/all_to_all | solution.py:650
  40.2 14.1 %attention_first.1 = (bf16[4,256,128]{2,1,0:T(8,128)(2,1)}, bf16[256,128]{1,0:T(8,128)(2,1)}, bf16[256,128]{1,0:T(8,128)(2,1)}, bf16[256,128]{1,0:T(8,128)(2,1)}...) custom-call(s32[4,4]{1,0:T(4,128)} %bitcast.36, ...), custom_call_target="tpu_custom_call" | custom-call | flops 16106127360 | bytes 2621440 | tf_op jit(solution)/shard_map/attention_first/pallas_call | solution.py:424
  54.2 1.5 %collective-permute-start.4 = (bf16[4,256,128]{2,1,0:T(8,128)(2,1)}, bf16[4,256,128]{2,1,0:T(8,128)(2,1)S(1)}, u32[]{:S(2)}, u32[]{:S(2)}) collective-permute-start(bf16[4,256,128]{2,1,0:T(8,128)(2,1)} %get-tuple-element.69.refs_4_), channel_id=1, source_target_pairs={{0,2},{1,3},{2,0},{3,1},{4,6},{5,7},{6,4},{7,5},{8,10},{9,11},{10,... | collective-permute-start | bytes 786440 | tf_op jit(solution)/shard_map/ppermute | solution.py:623
  55.8 15.1 %attention_later.1 = (bf16[4,256,128]{2,1,0:T(8,128)(2,1)}, bf16[256,128]{1,0:T(8,128)(2,1)}, bf16[256,128]{1,0:T(8,128)(2,1)}, bf16[256,128]{1,0:T(8,128)(2,1)}...) custom-call(s32[4,4]{1,0:T(4,128)} %bitcast.37, s32[2]{0:T(128)} %pad_add_fusion.index_ref, ...), custom_call_target="tpu_custom_call" | custom-call | flops 16106127360 | bytes 2621440 | tf_op jit(solution)/shard_map/attention_later/pallas_call | solution.py:455
  70.9 4.4 %all-to-all-start.1 = ((bf16[16,256,128]{2,1,0:T(8,128)(2,1)}), bf16[16,256,128]{2,1,0:T(8,128)(2,1)S(1)}, u32[]{:S(2)}, u32[]{:S(2)}) async-start(bf16[16,256,128]{2,1,0:T(8,128)(2,1)} %get-tuple-element.79), calls=%async_computation.1 | async-start | bytes 2097152 | tf_op jit(solution)/shard_map/all_to_all | solution.py:668
  76.3 1.6 %collective-permute-start.11 = (bf16[256,128]{1,0:T(8,128)(2,1)S(1)}, bf16[256,128]{1,0:T(8,128)(2,1)S(1)}, u32[]{:S(2)}, u32[]{:S(2)}) collective-permute-start(bf16[256,128]{1,0:T(8,128)(2,1)S(1)} %copy-done.12), channel_id=1, source_target_pairs={{0,8},{4,12},{8,0},{12,4},{1,9},{5,13},{9,1},{13,5},{2,10},{6,14},... | collective-permute-start | bytes 196616 | tf_op jit(solution)/shard_map/ppermute | solution.py:623
  78.0 1.7 %collective-permute-done.10 = bf16[256,128]{1,0:T(8,128)(2,1)S(1)} collective-permute-done((bf16[256,128]{1,0:T(8,128)(2,1)S(1)}, bf16[256,128]{1,0:T(8,128)(2,1)S(1)}, u32[]{:S(2)}, u32[]{:S(2)}) %collective-permute-start.10) | collective-permute-done | bytes 65568 | tf_op jit(solution)/shard_map/ppermute | solution.py:623
  79.8 1.8 %collective-permute-start.6 = (bf16[4,256,128]{2,1,0:T(8,128)(2,1)S(1)}, bf16[4,256,128]{2,1,0:T(8,128)(2,1)S(1)}, u32[]{:S(2)}, u32[]{:S(2)}) collective-permute-start(bf16[4,256,128]{2,1,0:T(8,128)(2,1)S(1)} %collective-permute-done.4), channel_id=1, source_target_pairs={{0,1},{1,0},{2,3},{3,2},{4,5},{5,4},{6,7},{7,6},{8,9},{9,8},{10,11... | collective-permute-start | bytes 786440 | tf_op jit(solution)/shard_map/ppermute | solution.py:623
  82.3 7.0 %collective-permute-done.11 = bf16[256,128]{1,0:T(8,128)(2,1)S(1)} collective-permute-done((bf16[256,128]{1,0:T(8,128)(2,1)S(1)}, bf16[256,128]{1,0:T(8,128)(2,1)S(1)}, u32[]{:S(2)}, u32[]{:S(2)}) %collective-permute-start.11) | collective-permute-done | bytes 65568 | tf_op jit(solution)/shard_map/ppermute | solution.py:623
  89.2 1.0 collective-permute-done.12
  90.3 9.2 %collective-permute-done.6 = bf16[4,256,128]{2,1,0:T(8,128)(2,1)S(1)} collective-permute-done((bf16[4,256,128]{2,1,0:T(8,128)(2,1)S(1)}, bf16[4,256,128]{2,1,0:T(8,128)(2,1)S(1)}, u32[]{:S(2)}, u32[]{:S(2)}) %collective-permute-start.6) | collective-permute-done | bytes 262176 | tf_op jit(solution)/shard_map/ppermute | solution.py:623
  100.9 3.9 %collective-permute-start.16 = (bf16[4,256,128]{2,1,0:T(8,128)(2,1)S(1)}, bf16[4,256,128]{2,1,0:T(8,128)(2,1)S(1)}, u32[]{:S(2)}, u32[]{:S(2)}) collective-permute-start(bf16[4,256,128]{2,1,0:T(8,128)(2,1)S(1)} %pad_maximum_fusion.5.refs_0_), channel_id=1, source_target_pairs={{0,2},{1,3},{2,0},{3,1},{4,6},{5,7},{6,4},{7,5},{8,10},{9,11},{10,... | collective-permute-start | bytes 786440 | tf_op jit(solution)/shard_map/ppermute | solution.py:623
  104.7 0.7 pad_maximum_fusion.3
  105.5 0.9 collective-permute-start.8
  106.4 0.7 pad_maximum_fusion.2
  107.2 3.8 %weight_grad.1.refs_0_ = bf16[64,1024]{1,0:T(8,128)(2,1)} custom-call(bf16[512,1024]{1,0:T(8,128)(2,1)} %refs_0_, bf16[512,1024]{1,0:T(8,128)(2,1)} %copy-done.4, bf16[512,1024]{1,0:T(8,128)(2,1)} %collective-permute-done.5.refs_2_, bf16[512,1024]{1,0:T(8,128)(2,1)} %copy-done.5, bf16[4,256,128]{2,1,0:T(8,128)(2,1)} %get-tuple-element.69.refs_4_, ...), custom_call_target="tpu_custom_call" | custom-call | tf_op jit(solution)/shard_map/weight_grad/pallas_call | solution.py:590
  111.0 1.5 %collective-permute-start.19 = (bf16[64,1024]{1,0:T(8,128)(2,1)}, bf16[64,1024]{1,0:T(8,128)(2,1)S(1)}, u32[]{:S(2)}, u32[]{:S(2)}) collective-permute-start(bf16[64,1024]{1,0:T(8,128)(2,1)} %weight_grad.1.refs_0_), channel_id=1, source_target_pairs={{0,8},{4,12},{8,0},{12,4},{1,9},{5,13},{9,1},{13,5},{2,10},{6,14},... | collective-permute-start | bytes 393224 | tf_op jit(solution)/shard_map/ppermute | solution.py:623
  112.5 4.8 %collective-permute-done.16.refs_2_ = bf16[4,256,128]{2,1,0:T(8,128)(2,1)S(1)} collective-permute-done((bf16[4,256,128]{2,1,0:T(8,128)(2,1)S(1)}, bf16[4,256,128]{2,1,0:T(8,128)(2,1)S(1)}, u32[]{:S(2)}, u32[]{:S(2)}) %collective-permute-start.16) | collective-permute-done | bytes 262176 | tf_op jit(solution)/shard_map/ppermute | solution.py:623
  117.8 1.0 pad_maximum_fusion.1.refs_0_
  118.8 4.0 %latent_grad.2 = (bf16[512,1024]{1,0:T(8,128)(2,1)}, bf16[512,1024]{1,0:T(8,128)(2,1)}) custom-call(s32[2]{0:T(128)} %pad_add_fusion.index_ref, bf16[4,256,128]{2,1,0:T(8,128)(2,1)S(1)} %pad_maximum_fusion.1.refs_0_, bf16[4,256,128]{2,1,0:T(8,128)(2,1)S(1)} %collective-permute-done.7.refs_1_, bf16[4,256,128]{2,1,0:T(8,128)(2,1)S(1)} %collective-permute-done.8.refs_2_, ...), custom_call_target="tpu_custom_call" | custom-call | tf_op jit(solution)/shard_map/latent_grad/pallas_call | solution.py:559
  123.5 0.9 copy-done.2
  124.4 2.6 %turn.1 = bf16[1024,256]{1,0:T(8,128)(2,1)} custom-call(s32[2]{0:T(128)} %pad_add_fusion.index_ref, bf16[64,1024]{1,0:T(8,128)(2,1)S(1)} %copy-done, bf16[64,1024]{1,0:T(8,128)(2,1)S(1)} %copy-done.2, bf16[64,1024]{1,0:T(8,128)(2,1)S(1)} %collective-permute-done.19.refs_2_, bf16[64,1024]{1,0:T(8,128)(2,1)} %collective-permute-done.20.refs_3_), custom_call_target="tpu_custom_call" | custom-call | tf_op jit(solution)/shard_map/turn/pallas_call | solution.py:608
  127.1 4.9 %token_grad.1 = bf16[256,1024]{1,0:T(8,128)(2,1)} custom-call(bf16[4,4,256,128]{3,2,1,0:T(8,128)(2,1)S(1)} %bitcast.23, bf16[1024,2048]{1,0:T(8,128)(2,1)} %value_w_ref.3, bf16[1024,2048]{1,0:T(8,128)(2,1)} %value_w_ref.3), custom_call_target="tpu_custom_call" | custom-call | tf_op jit(solution)/shard_map/token_grad/pallas_call | solution.py:515
  132.0 4.0 %latent_grad.3 = (bf16[512,1024]{1,0:T(8,128)(2,1)}, bf16[512,1024]{1,0:T(8,128)(2,1)}) custom-call(s32[2]{0:T(128)} %pad_add_fusion.index_ref, bf16[4,256,128]{2,1,0:T(8,128)(2,1)S(1)} %pad_maximum_fusion.5.refs_0_, bf16[4,256,128]{2,1,0:T(8,128)(2,1)S(1)} %collective-permute-done.15.refs_1_, ...), custom_call_target="tpu_custom_call", output_to_operand_aliasing={{0}: (6, {}), {1}: (7, {})} | custom-call | tf_op jit(solution)/shard_map/latent_grad/pallas_call | solution.py:559
  (62 shorter events, 6.2 us)
Async XLA Ops:
  5.9 34.2 %all-to-all-start = ((bf16[16,256,128]{2,1,0:T(8,128)(2,1)}), bf16[16,256,128]{2,1,0:T(8,128)(2,1)S(1)}, u32[]{:S(2)}, u32[]{:S(2)}) async-start(bf16[16,256,128]{2,1,0:T(8,128)(2,1)} %bitcast.24), calls=%async_computation | async-start | bytes 2097152 | tf_op jit(solution)/shard_map/all_to_all | solution.py:650
  18.2 14.4 %copy-start.3 = (bf16[512,1024]{1,0:T(8,128)(2,1)S(1)}, bf16[512,1024]{1,0:T(8,128)(2,1)}, u32[]{:S(2)}) copy-start(bf16[512,1024]{1,0:T(8,128)(2,1)} %refs_0_) | copy-start | bytes 3145732
  19.4 2.1 %collective-permute-start = (bf16[528,128]{1,0:T(8,128)(2,1)S(1)}, bf16[528,128]{1,0:T(8,128)(2,1)S(1)}, u32[]{:S(2)}, u32[]{:S(2)}) collective-permute-start(bf16[528,128]{1,0:T(8,128)(2,1)S(1)} %get-tuple-element.107), channel_id=1, source_target_pairs={{0,4},{4,0},{8,12},{12,8},{1,5},{5,1},{9,13},{13,9},{2,6},{6,2},{1... | collective-permute-start | bytes 405512 | tf_op jit(solution)/shard_map/ppermute | solution.py:623
  19.9 9.4 %collective-permute-start.1 = (bf16[528,128]{1,0:T(8,128)(2,1)S(1)}, bf16[528,128]{1,0:T(8,128)(2,1)S(1)}, u32[]{:S(2)}, u32[]{:S(2)}) collective-permute-start(bf16[528,128]{1,0:T(8,128)(2,1)S(1)} %get-tuple-element.106), channel_id=1, source_target_pairs={{0,8},{4,12},{8,0},{12,4},{1,9},{5,13},{9,1},{13,5},{2,10},{6,14},... | collective-permute-start | bytes 405512 | tf_op jit(solution)/shard_map/ppermute | solution.py:623
  21.5 11.0 %collective-permute-start.2 = (bf16[528,128]{1,0:T(8,128)(2,1)S(1)}, bf16[528,128]{1,0:T(8,128)(2,1)S(1)}, u32[]{:S(2)}, u32[]{:S(2)}) collective-permute-start(bf16[528,128]{1,0:T(8,128)(2,1)S(1)} %get-tuple-element.105), channel_id=1, source_target_pairs={{0,12},{4,8},{8,4},{12,0},{1,13},{5,9},{9,5},{13,1},{2,14},{6,10},... | collective-permute-start | bytes 405512 | tf_op jit(solution)/shard_map/ppermute | solution.py:623
  32.6 7.6 %copy-start.6 = (bf16[4,528,128]{2,1,0:T(8,128)(2,1)}, bf16[4,528,128]{2,1,0:T(8,128)(2,1)S(1)}, u32[]{:S(2)}) copy-start(bf16[4,528,128]{2,1,0:T(8,128)(2,1)S(1)} %pad_maximum_fusion.qg_ref) | copy-start | bytes 1622020
  32.6 38.3 %collective-permute-start.5 = (bf16[512,1024]{1,0:T(8,128)(2,1)S(1)}, bf16[512,1024]{1,0:T(8,128)(2,1)}, u32[]{:S(2)}, u32[]{:S(2)}) collective-permute-start(bf16[512,1024]{1,0:T(8,128)(2,1)S(1)} %copy-done.3), channel_id=1, source_target_pairs={{0,8},{4,12},{8,0},{12,4},{1,9},{5,13},{9,1},{13,5},{2,10},{6,14},... | collective-permute-start | bytes 3145736 | tf_op jit(solution)/shard_map/ppermute | solution.py:623
  54.2 16.6 %collective-permute-start.3 = (bf16[4,256,128]{2,1,0:T(8,128)(2,1)}, bf16[4,256,128]{2,1,0:T(8,128)(2,1)S(1)}, u32[]{:S(2)}, u32[]{:S(2)}) collective-permute-start(bf16[4,256,128]{2,1,0:T(8,128)(2,1)} %get-tuple-element.69.refs_4_), channel_id=1, source_target_pairs={{0,1},{1,0},{2,3},{3,2},{4,5},{5,4},{6,7},{7,6},{8,9},{9,8},{10,11... | collective-permute-start | bytes 786440 | tf_op jit(solution)/shard_map/ppermute | solution.py:623
  54.2 16.6 %collective-permute-start.4 = (bf16[4,256,128]{2,1,0:T(8,128)(2,1)}, bf16[4,256,128]{2,1,0:T(8,128)(2,1)S(1)}, u32[]{:S(2)}, u32[]{:S(2)}) collective-permute-start(bf16[4,256,128]{2,1,0:T(8,128)(2,1)} %get-tuple-element.69.refs_4_), channel_id=1, source_target_pairs={{0,2},{1,3},{2,0},{3,1},{4,6},{5,7},{6,4},{7,5},{8,10},{9,11},{10,... | collective-permute-start | bytes 786440 | tf_op jit(solution)/shard_map/ppermute | solution.py:623
  70.9 7.1 %copy-start.11 = (bf16[256,128]{1,0:T(8,128)(2,1)S(1)}, bf16[256,128]{1,0:T(8,128)(2,1)}, u32[]{:S(2)}) copy-start(bf16[256,128]{1,0:T(8,128)(2,1)} %get-tuple-element.85) | copy-start | bytes 196612
  70.9 19.4 %copy-start.10 = (bf16[256,128]{1,0:T(8,128)(2,1)S(1)}, bf16[256,128]{1,0:T(8,128)(2,1)}, u32[]{:S(2)}) copy-start(bf16[256,128]{1,0:T(8,128)(2,1)} %get-tuple-element.82) | copy-start | bytes 196612
  70.9 29.2 %copy-start.9 = (bf16[256,128]{1,0:T(8,128)(2,1)S(1)}, bf16[256,128]{1,0:T(8,128)(2,1)}, u32[]{:S(2)}) copy-start(bf16[256,128]{1,0:T(8,128)(2,1)} %get-tuple-element.76) | copy-start | bytes 196612
  70.9 33.8 %copy-start.8 = (bf16[256,128]{1,0:T(8,128)(2,1)S(1)}, bf16[256,128]{1,0:T(8,128)(2,1)}, u32[]{:S(2)}) copy-start(bf16[256,128]{1,0:T(8,128)(2,1)} %get-tuple-element.75) | copy-start | bytes 196612
  70.9 56.2 %all-to-all-start.1 = ((bf16[16,256,128]{2,1,0:T(8,128)(2,1)}), bf16[16,256,128]{2,1,0:T(8,128)(2,1)S(1)}, u32[]{:S(2)}, u32[]{:S(2)}) async-start(bf16[16,256,128]{2,1,0:T(8,128)(2,1)} %get-tuple-element.79), calls=%async_computation.1 | async-start | bytes 2097152 | tf_op jit(solution)/shard_map/all_to_all | solution.py:668
  75.3 31.1 %copy-start.7 = (bf16[256,128]{1,0:T(8,128)(2,1)S(1)}, bf16[256,128]{1,0:T(8,128)(2,1)}, u32[]{:S(2)}) copy-start(bf16[256,128]{1,0:T(8,128)(2,1)} %get-tuple-element.74) | copy-start | bytes 196612
  75.3 25.5 %collective-permute-start.13 = (bf16[512,1024]{1,0:T(8,128)(2,1)S(1)}, bf16[512,1024]{1,0:T(8,128)(2,1)S(1)}, u32[]{:S(2)}, u32[]{:S(2)}) collective-permute-start(bf16[512,1024]{1,0:T(8,128)(2,1)S(1)} %copy-done.3), channel_id=1, source_target_pairs={{0,4},{4,0},{8,12},{12,8},{1,5},{5,1},{9,13},{13,9},{2,6},{6,2},{1... | collective-permute-start | bytes 3145736 | tf_op jit(solution)/shard_map/ppermute | solution.py:623
  75.8 25.0 %collective-permute-start.14 = (bf16[512,1024]{1,0:T(8,128)(2,1)}, bf16[512,1024]{1,0:T(8,128)(2,1)S(1)}, u32[]{:S(2)}, u32[]{:S(2)}) collective-permute-start(bf16[512,1024]{1,0:T(8,128)(2,1)} %collective-permute-done.5.refs_2_), channel_id=1, source_target_pairs={{0,4},{4,0},{8,12},{12,8},{1,5},{5,1},{9,13},{13,9},{2,6},{6,2},{1... | collective-permute-start | bytes 3145736 | tf_op jit(solution)/shard_map/ppermute | solution.py:623
  75.9 3.9 %collective-permute-start.10 = (bf16[256,128]{1,0:T(8,128)(2,1)S(1)}, bf16[256,128]{1,0:T(8,128)(2,1)S(1)}, u32[]{:S(2)}, u32[]{:S(2)}) collective-permute-start(bf16[256,128]{1,0:T(8,128)(2,1)S(1)} %copy-done.13), channel_id=1, source_target_pairs={{0,4},{4,0},{8,12},{12,8},{1,5},{5,1},{9,13},{13,9},{2,6},{6,2},{1... | collective-permute-start | bytes 196616 | tf_op jit(solution)/shard_map/ppermute | solution.py:623
  76.3 12.9 %collective-permute-start.11 = (bf16[256,128]{1,0:T(8,128)(2,1)S(1)}, bf16[256,128]{1,0:T(8,128)(2,1)S(1)}, u32[]{:S(2)}, u32[]{:S(2)}) collective-permute-start(bf16[256,128]{1,0:T(8,128)(2,1)S(1)} %copy-done.12), channel_id=1, source_target_pairs={{0,8},{4,12},{8,0},{12,4},{1,9},{5,13},{9,1},{13,5},{2,10},{6,14},... | collective-permute-start | bytes 196616 | tf_op jit(solution)/shard_map/ppermute | solution.py:623
  78.0 12.3 %collective-permute-start.12 = (bf16[256,128]{1,0:T(8,128)(2,1)S(1)}, bf16[256,128]{1,0:T(8,128)(2,1)S(1)}, u32[]{:S(2)}, u32[]{:S(2)}) collective-permute-start(bf16[256,128]{1,0:T(8,128)(2,1)S(1)} %copy-done.11), channel_id=1, source_target_pairs={{0,12},{4,8},{8,4},{12,0},{1,13},{5,9},{9,5},{13,1},{2,14},{6,10},... | collective-permute-start | bytes 196616 | tf_op jit(solution)/shard_map/ppermute | solution.py:623
  79.8 19.7 %collective-permute-start.6 = (bf16[4,256,128]{2,1,0:T(8,128)(2,1)S(1)}, bf16[4,256,128]{2,1,0:T(8,128)(2,1)S(1)}, u32[]{:S(2)}, u32[]{:S(2)}) collective-permute-start(bf16[4,256,128]{2,1,0:T(8,128)(2,1)S(1)} %collective-permute-done.4), channel_id=1, source_target_pairs={{0,1},{1,0},{2,3},{3,2},{4,5},{5,4},{6,7},{7,6},{8,9},{9,8},{10,11... | collective-permute-start | bytes 786440 | tf_op jit(solution)/shard_map/ppermute | solution.py:623
  100.2 12.4 %collective-permute-start.9 = (bf16[4,256,128]{2,1,0:T(8,128)(2,1)S(1)}, bf16[4,256,128]{2,1,0:T(8,128)(2,1)S(1)}, u32[]{:S(2)}, u32[]{:S(2)}) collective-permute-start(bf16[4,256,128]{2,1,0:T(8,128)(2,1)S(1)} %pad_maximum_fusion.4), channel_id=1, source_target_pairs={{0,12},{4,8},{8,4},{12,0},{1,13},{5,9},{9,5},{13,1},{2,14},{6,10},... | collective-permute-start | bytes 786440 | tf_op jit(solution)/shard_map/ppermute | solution.py:623
  100.8 6.3 %copy-start.5 = (bf16[512,1024]{1,0:T(8,128)(2,1)}, bf16[512,1024]{1,0:T(8,128)(2,1)S(1)}, u32[]{:S(2)}) copy-start(bf16[512,1024]{1,0:T(8,128)(2,1)S(1)} %collective-permute-done.14.refs_3_) | copy-start | bytes 3145732
  100.9 16.5 %collective-permute-start.16 = (bf16[4,256,128]{2,1,0:T(8,128)(2,1)S(1)}, bf16[4,256,128]{2,1,0:T(8,128)(2,1)S(1)}, u32[]{:S(2)}, u32[]{:S(2)}) collective-permute-start(bf16[4,256,128]{2,1,0:T(8,128)(2,1)S(1)} %pad_maximum_fusion.5.refs_0_), channel_id=1, source_target_pairs={{0,2},{1,3},{2,0},{3,1},{4,6},{5,7},{6,4},{7,5},{8,10},{9,11},{10,... | collective-permute-start | bytes 786440 | tf_op jit(solution)/shard_map/ppermute | solution.py:623
  105.5 11.8 %collective-permute-start.8 = (bf16[4,256,128]{2,1,0:T(8,128)(2,1)}, bf16[4,256,128]{2,1,0:T(8,128)(2,1)S(1)}, u32[]{:S(2)}, u32[]{:S(2)}) collective-permute-start(bf16[4,256,128]{2,1,0:T(8,128)(2,1)} %pad_maximum_fusion.3), channel_id=1, source_target_pairs={{0,8},{4,12},{8,0},{12,4},{1,9},{5,13},{9,1},{13,5},{2,10},{6,14},... | collective-permute-start | bytes 786440 | tf_op jit(solution)/shard_map/ppermute | solution.py:623
  107.1 11.7 %collective-permute-start.7 = (bf16[4,256,128]{2,1,0:T(8,128)(2,1)}, bf16[4,256,128]{2,1,0:T(8,128)(2,1)S(1)}, u32[]{:S(2)}, u32[]{:S(2)}) collective-permute-start(bf16[4,256,128]{2,1,0:T(8,128)(2,1)} %pad_maximum_fusion.2), channel_id=1, source_target_pairs={{0,4},{4,0},{8,12},{12,8},{1,5},{5,1},{9,13},{13,9},{2,6},{6,2},{1... | collective-permute-start | bytes 786440 | tf_op jit(solution)/shard_map/ppermute | solution.py:623
  111.0 12.5 %copy-start = (bf16[64,1024]{1,0:T(8,128)(2,1)S(1)}, bf16[64,1024]{1,0:T(8,128)(2,1)}, u32[]{:S(2)}) copy-start(bf16[64,1024]{1,0:T(8,128)(2,1)} %weight_grad.1.refs_0_) | copy-start | bytes 393220
  111.0 6.4 %collective-permute-start.19 = (bf16[64,1024]{1,0:T(8,128)(2,1)}, bf16[64,1024]{1,0:T(8,128)(2,1)S(1)}, u32[]{:S(2)}, u32[]{:S(2)}) collective-permute-start(bf16[64,1024]{1,0:T(8,128)(2,1)} %weight_grad.1.refs_0_), channel_id=1, source_target_pairs={{0,8},{4,12},{8,0},{12,4},{1,9},{5,13},{9,1},{13,5},{2,10},{6,14},... | collective-permute-start | bytes 393224 | tf_op jit(solution)/shard_map/ppermute | solution.py:623
  112.5 19.4 %collective-permute-start.15 = (bf16[4,256,128]{2,1,0:T(8,128)(2,1)S(1)}, bf16[4,256,128]{2,1,0:T(8,128)(2,1)S(1)}, u32[]{:S(2)}, u32[]{:S(2)}) collective-permute-start(bf16[4,256,128]{2,1,0:T(8,128)(2,1)S(1)} %pad_maximum_fusion.5.refs_0_), channel_id=1, source_target_pairs={{0,1},{1,0},{2,3},{3,2},{4,5},{5,4},{6,7},{7,6},{8,9},{9,8},{10,11... | collective-permute-start | bytes 786440 | tf_op jit(solution)/shard_map/ppermute | solution.py:623
  117.3 14.6 %collective-permute-start.17 = (bf16[4,256,128]{2,1,0:T(8,128)(2,1)S(1)}, bf16[4,256,128]{2,1,0:T(8,128)(2,1)S(1)}, u32[]{:S(2)}, u32[]{:S(2)}) collective-permute-start(bf16[4,256,128]{2,1,0:T(8,128)(2,1)S(1)} %collective-permute-done.16.refs_2_), channel_id=1, source_target_pairs={{0,1},{1,0},{2,3},{3,2},{4,5},{5,4},{6,7},{7,6},{8,9},{9,8},{10,11... | collective-permute-start | bytes 786440 | tf_op jit(solution)/shard_map/ppermute | solution.py:623
  117.3 5.5 %collective-permute-start.18 = (bf16[64,1024]{1,0:T(8,128)(2,1)}, bf16[64,1024]{1,0:T(8,128)(2,1)S(1)}, u32[]{:S(2)}, u32[]{:S(2)}) collective-permute-start(bf16[64,1024]{1,0:T(8,128)(2,1)} %weight_grad.1.refs_0_), channel_id=1, source_target_pairs={{0,4},{4,0},{8,12},{12,8},{1,5},{5,1},{9,13},{13,9},{2,6},{6,2},{1... | collective-permute-start | bytes 393224 | tf_op jit(solution)/shard_map/ppermute | solution.py:623
  117.4 6.1 %collective-permute-start.20 = (bf16[64,1024]{1,0:T(8,128)(2,1)S(1)}, bf16[64,1024]{1,0:T(8,128)(2,1)}, u32[]{:S(2)}, u32[]{:S(2)}) collective-permute-start(bf16[64,1024]{1,0:T(8,128)(2,1)S(1)} %collective-permute-done.19.refs_2_), channel_id=1, source_target_pairs={{0,4},{4,0},{8,12},{12,8},{1,5},{5,1},{9,13},{13,9},{2,6},{6,2},{1... | collective-permute-start | bytes 393224 | tf_op jit(solution)/shard_map/ppermute | solution.py:623
  (5 other events, 17.6 us)
